TPU v7x, 32 devices: a whole 2x2x4 slice. The times are simulated.
32 devices in a mesh: dp: 4 (over z), ctx: 8 (over y, x, core).
Axes of the slice: x: 2, y: 2, z: 4, core: 2. Of those that a mesh axis runs over, the one named last changes fastest.
Arguments:
- frames: bfloat16 [32, 2, 512, 512], P(('dp', 'ctx')), parts along dimension 0, may hold values from -6 to 6
- episode_lengths: int32 [64], P('dp'), parts along dimension 0, may hold values from 1 to 1024, 8192 in all
- w_qkv: bfloat16 [512, 1536], replicated, may hold values from -1 to 1
- w_out: bfloat16 [512, 512], replicated, may hold values from -0.25 to 0.25
Outputs:
- attended: bfloat16 [32, 2, 512, 512], P(('dp', 'ctx')), parts along dimension 0
There are 4 independent parts, one for each index of `dp`. A program takes and returns all parts, laid end to end along the dimension named above; an argument that names none is the same for every part. Nothing has to cross between parts.
Inputs may be any that keep to these rules, and one draw needn't show every extreme that they name: `episode_lengths`: the lengths sum to 8192; the longest is exactly 1024 tokens.
All inputs are finite; a program needn't handle non-finite values.
Results may differ from a plain program's by a relative error of at most 0.0082.
Values may be sent and summed in bfloat16 or wider, within the bound.
No kernel may reach another device: no remote copies, remote signals or barrier semaphores. Data moves between devices by JAX's collectives and lax.ppermute only.
A program may use at most 64 MiB of HBM per device.

v0:
```python
import jax
import jax.numpy as jnp
from jax import lax
from jax.sharding import PartitionSpec as P

HEADS = 4
HEAD_DIM = 128
WIN = 2


def from_behind(block, axis, distance):
    devices = range(lax.axis_size(axis))
    route = [(i - distance, i) for i in devices if i - distance in devices]
    return lax.ppermute(block, axis, route)


def normalize(rows):
    wide = rows.astype(jnp.float32)
    factor = lax.rsqrt(jnp.mean(wide * wide, axis=-1, keepdims=True) + 1e-06)
    return (wide * factor).astype(jnp.bfloat16)


def episode_start(positions, episode_lengths):
    ends = jnp.cumsum(episode_lengths)
    passed = (ends[None, :] <= positions[:, None]).astype(jnp.int32)
    return jnp.sum(passed * episode_lengths[None, :], axis=1)


def head_scores(query_part, key_part):
    scores = lax.dot_general(
        query_part, key_part, (((1,), (1,)), ((), ())), preferred_element_type=jnp.float32
    )
    return scores * HEAD_DIM ** (-0.5)


def attend(queries, keys, values, allowed):
    outputs = []
    for head in range(HEADS):
        low = head * HEAD_DIM
        high = low + HEAD_DIM
        query_part = queries[:, low:high]
        scores = head_scores(query_part, keys[:, low:high])
        scores = jnp.where(allowed, scores, -jnp.inf)
        peak = jnp.max(scores, axis=1, keepdims=True)
        weights = jnp.exp(scores - peak)
        totals = jnp.sum(weights, axis=1, keepdims=True)
        mixed = (
            jnp.dot(
                weights.astype(jnp.bfloat16),
                values[:, low:high],
                preferred_element_type=jnp.float32,
            )
            / totals
        )
        outputs.append(mixed)
    return jnp.concatenate(outputs, axis=1).astype(jnp.bfloat16)


def local(frames, episode_lengths, w_qkv, w_out):
    width = w_out.shape[0]
    group = frames.shape[2]
    count = lax.axis_size("ctx")
    place = lax.axis_index("ctx")
    normed = normalize(frames[0])
    projected = (
        jnp.dot(normed.reshape(2 * group, width), w_qkv, preferred_element_type=jnp.float32)
        .astype(jnp.bfloat16)
        .reshape(2, group, 3 * width)
    )
    low_now = normed[0]
    high_now = normed[1]
    low_window = []
    high_window = []
    for step in range(WIN):
        low_next = from_behind(low_now, "ctx", 1)
        high_arrived = from_behind(high_now, "ctx", -1)
        high_next = jnp.where(place == count - 1, low_now, high_arrived)
        low_window.append(low_next)
        high_window.append(high_next)
        low_now = low_next
        high_now = high_next
    received = jnp.stack(low_window[::-1] + high_window[::-1], axis=0)
    received = (
        jnp.dot(
            received.reshape(2 * WIN * group, width),
            w_qkv[:, width:],
            preferred_element_type=jnp.float32,
        )
        .astype(jnp.bfloat16)
        .reshape(2 * WIN, group, 2 * width)
    )
    results = []
    for half in range(2):
        block_index = place if half == 0 else 2 * count - 1 - place
        earlier = received[half * WIN : (half + 1) * WIN].reshape(WIN * group, 2 * width)
        pairs = jnp.concatenate([earlier, projected[half, :, width:]], axis=0)
        first = block_index * group
        query_pos = first + jnp.arange(group, dtype=jnp.int32)
        key_pos = first - WIN * group + jnp.arange((WIN + 1) * group, dtype=jnp.int32)
        starts = episode_start(query_pos, episode_lengths)
        allowed = (key_pos[None, :] <= query_pos[:, None]) & (key_pos[None, :] >= starts[:, None])
        mixed = attend(projected[half, :, :width], pairs[:, :width], pairs[:, width:], allowed)
        results.append(
            jnp.dot(mixed, w_out, preferred_element_type=jnp.float32).astype(jnp.bfloat16)
        )
    return jnp.stack(results, axis=0)[None]


def solution(mesh):
    in_specs = (P(("dp", "ctx"), None, None, None), P("dp"), P(), P())
    out_specs = P(("dp", "ctx"), None, None, None)
    return jax.shard_map(local, mesh=mesh, in_specs=in_specs, out_specs=out_specs, check_vma=False)
```

profile of v0, /device:TPU:19, one launch (start us, length us, event | category | flops | bytes accessed | tf_op | source)
XLA Modules:
  0.0 60.9 jit_solution(6181365233833123858)
XLA Ops:
  0.0 1.6 %fusion.24 = f32[2,512]{1,0:T(2,128)S(1)} fusion(bf16[1,2,512,512]{3,2,1,0:T(8,128)(2,1)} %param.4), kind=kLoop, calls=%fused_computation.75 | loop fusion | flops 1571840 | bytes 1052672 | tf_op jit(solution)/shard_map/reduce_sum | solution.py:19
  1.7 1.5 %fusion.25 = bf16[2,512,512]{2,1,0:T(8,128)(2,1)S(1)} fusion(bf16[1,2,512,512]{3,2,1,0:T(8,128)(2,1)} %param.4, f32[2,512]{1,0:T(2,128)S(1)} %get-tuple-element.16), kind=kLoop, calls=%fused_computation.76 | loop fusion | flops 1572864 | bytes 2101248 | tf_op jit(solution)/shard_map/convert_element_type | solution.py:20
  3.2 1.1 %slice_bitcast_fusion.4 = (bf16[512,512]{1,0:T(8,128)(2,1)}, bf16[512,512]{1,0:T(8,128)(2,1)}) fusion(bf16[2,512,512]{2,1,0:T(8,128)(2,1)S(1)} %fusion.25), kind=kLoop, calls=%fused_computation.121 | loop fusion | bytes 2097152 | tf_op jit(solution)/shard_map/squeeze | solution.py:70
  4.3 2.6 %collective-permute-start.2 = (bf16[512,512]{1,0:T(8,128)(2,1)}, bf16[512,512]{1,0:T(8,128)(2,1)}, u32[]{:S(2)}, u32[]{:S(2)}) collective-permute-start(bf16[512,512]{1,0:T(8,128)(2,1)} %get-tuple-element.14), channel_id=1, source_target_pairs={{1,0},{2,1},{3,2},{4,3},{5,4},{6,5},{7,6},{9,8},{10,9},{11,10},{12... | collective-permute-start | bytes 1572872 | tf_op jit(solution)/shard_map/ppermute | solution.py:14
  6.8 3.9 %collective-permute-start = (bf16[512,512]{1,0:T(8,128)(2,1)}, bf16[512,512]{1,0:T(8,128)(2,1)S(1)}, u32[]{:S(2)}, u32[]{:S(2)}) collective-permute-start(bf16[512,512]{1,0:T(8,128)(2,1)} %get-tuple-element.13), channel_id=1, source_target_pairs={{0,1},{1,2},{2,3},{3,4},{4,5},{5,6},{6,7},{8,9},{9,10},{10,11},{11... | collective-permute-start | bytes 1572872 | tf_op jit(solution)/shard_map/ppermute | solution.py:14
  10.8 1.3 %fusion.26 = bf16[1024,512]{1,0:T(8,128)(2,1)} fusion(bf16[1,2,512,512]{3,2,1,0:T(8,128)(2,1)S(1)} %copy-done.1, f32[1024]{0:T(1024)S(1)} %bitcast.53), kind=kLoop, calls=%fused_computation.78 | loop fusion | flops 1572864 | bytes 2101248 | tf_op jit(solution)/shard_map/convert_element_type | solution.py:20
  12.4 3.5 %convolution_convert_fusion.1 = bf16[1024,1536]{1,0:T(8,128)(2,1)S(1)} fusion(bf16[1024,512]{1,0:T(8,128)(2,1)} %fusion.26, bf16[512,1536]{1,0:T(8,128)(2,1)} %param.6), kind=kOutput, calls=%fused_computation.29 | convolution fusion | flops 1612185600 | bytes 5767168 | tf_op jit(solution)/shard_map/dot_general | solution.py:66
  15.9 3.7 %collective-permute-done.2 = bf16[512,512]{1,0:T(8,128)(2,1)} collective-permute-done((bf16[512,512]{1,0:T(8,128)(2,1)}, bf16[512,512]{1,0:T(8,128)(2,1)}, u32[]{:S(2)}, u32[]{:S(2)}) %collective-permute-start.2) | collective-permute-done | bytes 524320 | tf_op jit(solution)/shard_map/ppermute | solution.py:14
  19.6 1.1 %broadcast_select_fusion = bf16[512,512]{1,0:T(8,128)(2,1)S(1)} fusion(bf16[512,512]{1,0:T(8,128)(2,1)} %collective-permute-done.2, pred[]{:T(512)S(6)} %eq.4, bf16[2,512,512]{2,1,0:T(8,128)(2,1)S(1)} %fusion.25), kind=kLoop, calls=%fused_computation.138 | loop fusion | flops 262144 | bytes 1572865 | tf_op jit(solution)/shard_map/jit(_where)/select_n | solution.py:77
  20.7 1.9 %collective-permute-start.3 = (bf16[512,512]{1,0:T(8,128)(2,1)S(1)}, bf16[512,512]{1,0:T(8,128)(2,1)S(1)}, u32[]{:S(2)}, u32[]{:S(2)}) collective-permute-start(bf16[512,512]{1,0:T(8,128)(2,1)S(1)} %broadcast_select_fusion), channel_id=1, source_target_pairs={{1,0},{2,1},{3,2},{4,3},{5,4},{6,5},{7,6},{9,8},{10,9},{11,10},{12... | collective-permute-start | bytes 1572872 | tf_op jit(solution)/shard_map/ppermute | solution.py:14
  23.0 4.7 %collective-permute-start.1 = (bf16[512,512]{1,0:T(8,128)(2,1)S(1)}, bf16[512,512]{1,0:T(8,128)(2,1)S(1)}, u32[]{:S(2)}, u32[]{:S(2)}) collective-permute-start(bf16[512,512]{1,0:T(8,128)(2,1)S(1)} %collective-permute-done), channel_id=1, source_target_pairs={{0,1},{1,2},{2,3},{3,4},{4,5},{5,6},{6,7},{8,9},{9,10},{10,11},{11... | collective-permute-start | bytes 1572872 | tf_op jit(solution)/shard_map/ppermute | solution.py:14
  27.8 9.8 %collective-permute-done.3 = bf16[512,512]{1,0:T(8,128)(2,1)S(1)} collective-permute-done((bf16[512,512]{1,0:T(8,128)(2,1)S(1)}, bf16[512,512]{1,0:T(8,128)(2,1)S(1)}, u32[]{:S(2)}, u32[]{:S(2)}) %collective-permute-start.3) | collective-permute-done | bytes 524320 | tf_op jit(solution)/shard_map/ppermute | solution.py:14
  37.9 2.4 %convolution_convert_fusion = bf16[2048,1024]{1,0:T(8,128)(2,1)S(1)} fusion(bf16[2048,512]{1,0:T(8,128)(2,1)S(1)} %bitcast.49, bf16[512,1536]{1,0:T(8,128)(2,1)S(1)} %copy-done.3), kind=kOutput, calls=%fused_computation.28 | convolution fusion | flops 2149580800 | bytes 7340032 | tf_op jit(solution)/shard_map/dot_general | solution.py:84
  40.8 0.9 %fusion.181 = (f32[512]{0:T(512)S(1)}, f32[512,1536]{1,0:T(8,128)S(1)}) fusion(bf16[1024,1024]{1,0:T(8,128)(2,1)S(1)} %get-tuple-element.7, bf16[512,1024]{1,0:T(8,128)(2,1)S(1)} %get-tuple-element.11, bf16[512,512]{1,0:T(8,128)(2,1)S(1)} %get-tuple-element.9, s32[512]{0:T(512)S(1)} %get-tuple-element.5, s32[512]{0:T(512)S(1)} %iota_add_fusion.3, ...), kind=kOutput, calls=%fused_computation.199 | convolution fusion | flops 206831104 | bytes 6436864 | tf_op jit(solution)/shard_map/dot_general | solution.py:30
  41.7 0.9 %fusion.180 = (f32[512]{0:T(512)S(1)}, f32[512,1536]{1,0:T(8,128)S(1)}) fusion(bf16[1024,1024]{1,0:T(8,128)(2,1)S(1)} %get-tuple-element.7, bf16[512,1024]{1,0:T(8,128)(2,1)S(1)} %get-tuple-element.11, bf16[512,512]{1,0:T(8,128)(2,1)S(1)} %get-tuple-element.9, s32[512]{0:T(512)S(1)} %get-tuple-element.5, s32[512]{0:T(512)S(1)} %iota_add_fusion.3, ...), kind=kOutput, calls=%fused_computation.198 | convolution fusion | flops 206831104 | bytes 6436864 | tf_op jit(solution)/shard_map/dot_general | solution.py:30
  42.6 0.9 %fusion.179 = (f32[512]{0:T(512)S(1)}, f32[512,1536]{1,0:T(8,128)S(1)}) fusion(bf16[1024,1024]{1,0:T(8,128)(2,1)S(1)} %get-tuple-element.7, bf16[512,1024]{1,0:T(8,128)(2,1)S(1)} %get-tuple-element.11, bf16[512,512]{1,0:T(8,128)(2,1)S(1)} %get-tuple-element.9, s32[512]{0:T(512)S(1)} %get-tuple-element.5, s32[512]{0:T(512)S(1)} %iota_add_fusion.3, ...), kind=kOutput, calls=%fused_computation.197 | convolution fusion | flops 206831104 | bytes 6436864 | tf_op jit(solution)/shard_map/dot_general | solution.py:30
  43.5 0.9 %fusion.178 = (f32[512]{0:T(512)S(1)}, f32[512,1536]{1,0:T(8,128)S(1)}) fusion(bf16[1024,1024]{1,0:T(8,128)(2,1)S(1)} %get-tuple-element.7, bf16[512,1024]{1,0:T(8,128)(2,1)S(1)} %get-tuple-element.11, bf16[512,512]{1,0:T(8,128)(2,1)S(1)} %get-tuple-element.9, s32[512]{0:T(512)S(1)} %get-tuple-element.5, s32[512]{0:T(512)S(1)} %iota_add_fusion.3, ...), kind=kOutput, calls=%fused_computation.196 | convolution fusion | flops 206831104 | bytes 6436864 | tf_op jit(solution)/shard_map/dot_general | solution.py:30
  44.5 0.9 %fusion.177 = (f32[512]{0:T(512)S(1)}, f32[512,1536]{1,0:T(8,128)S(1)}) fusion(bf16[1024,1024]{1,0:T(8,128)(2,1)S(1)} %get-tuple-element.8, bf16[512,1024]{1,0:T(8,128)(2,1)S(1)} %get-tuple-element.12, bf16[512,512]{1,0:T(8,128)(2,1)S(1)} %get-tuple-element.10, s32[512]{0:T(512)S(1)} %get-tuple-element.6, s32[512]{0:T(512)S(1)} %iota_add_fusion.2, ...), kind=kOutput, calls=%fused_computation.195 | convolution fusion | flops 206831104 | bytes 6436864 | tf_op jit(solution)/shard_map/dot_general | solution.py:30
  45.4 0.9 %fusion.176 = (f32[512]{0:T(512)S(1)}, f32[512,1536]{1,0:T(8,128)S(1)}) fusion(bf16[1024,1024]{1,0:T(8,128)(2,1)S(1)} %get-tuple-element.8, bf16[512,1024]{1,0:T(8,128)(2,1)S(1)} %get-tuple-element.12, bf16[512,512]{1,0:T(8,128)(2,1)S(1)} %get-tuple-element.10, s32[512]{0:T(512)S(1)} %get-tuple-element.6, s32[512]{0:T(512)S(1)} %iota_add_fusion.2, ...), kind=kOutput, calls=%fused_computation.194 | convolution fusion | flops 206831104 | bytes 6436864 | tf_op jit(solution)/shard_map/dot_general | solution.py:30
  46.3 0.9 %fusion.175 = (f32[512]{0:T(512)S(1)}, f32[512,1536]{1,0:T(8,128)S(1)}) fusion(bf16[1024,1024]{1,0:T(8,128)(2,1)S(1)} %get-tuple-element.8, bf16[512,1024]{1,0:T(8,128)(2,1)S(1)} %get-tuple-element.12, bf16[512,512]{1,0:T(8,128)(2,1)S(1)} %get-tuple-element.10, s32[512]{0:T(512)S(1)} %get-tuple-element.6, s32[512]{0:T(512)S(1)} %iota_add_fusion.2, ...), kind=kOutput, calls=%fused_computation.193 | convolution fusion | flops 206831104 | bytes 6436864 | tf_op jit(solution)/shard_map/dot_general | solution.py:30
  47.2 0.9 %fusion.174 = (f32[512]{0:T(512)S(1)}, f32[512,1536]{1,0:T(8,128)S(1)}) fusion(bf16[1024,1024]{1,0:T(8,128)(2,1)S(1)} %get-tuple-element.8, bf16[512,1024]{1,0:T(8,128)(2,1)S(1)} %get-tuple-element.12, bf16[512,512]{1,0:T(8,128)(2,1)S(1)} %get-tuple-element.10, s32[512]{0:T(512)S(1)} %get-tuple-element.6, s32[512]{0:T(512)S(1)} %iota_add_fusion.2, ...), kind=kOutput, calls=%fused_computation.192 | convolution fusion | flops 206831104 | bytes 6436864 | tf_op jit(solution)/shard_map/dot_general | solution.py:30
  48.1 0.6 fusion.8
  48.7 0.7 %fusion.98 = bf16[512,128]{0,1:T(8,128)(2,1)S(1)} fusion(f32[512,1536]{1,0:T(8,128)S(1)} %get-tuple-element.32, f32[512]{0:T(512)S(1)} %get-tuple-element.31, bf16[1024,1024]{1,0:T(8,128)(2,1)S(1)} %get-tuple-element.7, bf16[512,1024]{1,0:T(8,128)(2,1)S(1)} %get-tuple-element.11, f32[512]{0:T(512)S(1)} %fusion.8), kind=kOutput, calls=%fused_computation.114 | convolution fusion | flops 203816960 | bytes 6426624 | tf_op jit(solution)/shard_map/dot_general | solution.py:48
  50.0 0.7 %fusion.95 = bf16[512,128]{0,1:T(8,128)(2,1)S(1)} fusion(f32[512,1536]{1,0:T(8,128)S(1)} %get-tuple-element.30, f32[512]{0:T(512)S(1)} %get-tuple-element.29, bf16[1024,1024]{1,0:T(8,128)(2,1)S(1)} %get-tuple-element.7, bf16[512,1024]{1,0:T(8,128)(2,1)S(1)} %get-tuple-element.11, f32[512]{0:T(512)S(1)} %fusion.10), kind=kOutput, calls=%fused_computation.113 | convolution fusion | flops 203816960 | bytes 6426624 | tf_op jit(solution)/shard_map/dot_general | solution.py:48
  50.8 0.8 %fusion.12 = f32[512]{0:T(512)S(1)} fusion(f32[512,1536]{1,0:T(8,128)S(1)} %get-tuple-element.28, f32[512]{0:T(512)S(1)} %get-tuple-element.27), kind=kLoop, calls=%fused_computation.60 | loop fusion | flops 1572352 | bytes 3149824 | tf_op jit(solution)/shard_map/reduce_sum | solution.py:46
  51.5 0.7 %fusion.92 = bf16[512,128]{0,1:T(8,128)(2,1)S(1)} fusion(f32[512,1536]{1,0:T(8,128)S(1)} %get-tuple-element.28, f32[512]{0:T(512)S(1)} %get-tuple-element.27, bf16[1024,1024]{1,0:T(8,128)(2,1)S(1)} %get-tuple-element.7, bf16[512,1024]{1,0:T(8,128)(2,1)S(1)} %get-tuple-element.11, f32[512]{0:T(512)S(1)} %fusion.12), kind=kOutput, calls=%fused_computation.112 | convolution fusion | flops 203816960 | bytes 6426624 | tf_op jit(solution)/shard_map/dot_general | solution.py:48
  52.9 0.8 %fusion.89 = bf16[512,128]{0,1:T(8,128)(2,1)S(1)} fusion(f32[512,1536]{1,0:T(8,128)S(1)} %get-tuple-element.26, f32[512]{0:T(512)S(1)} %get-tuple-element.25, bf16[512,1024]{1,0:T(8,128)(2,1)S(1)} %get-tuple-element.11, bf16[1024,1024]{1,0:T(8,128)(2,1)S(1)} %get-tuple-element.7, f32[512]{0:T(512)S(1)} %fusion.14), kind=kOutput, calls=%fused_computation.111 | convolution fusion | flops 203816960 | bytes 6426624 | tf_op jit(solution)/shard_map/dot_general | solution.py:48
  54.2 0.8 %fusion.86 = bf16[512,128]{0,1:T(8,128)(2,1)S(1)} fusion(f32[512,1536]{1,0:T(8,128)S(1)} %get-tuple-element.24, f32[512]{0:T(512)S(1)} %get-tuple-element.23, bf16[1024,1024]{1,0:T(8,128)(2,1)S(1)} %get-tuple-element.8, bf16[512,1024]{1,0:T(8,128)(2,1)S(1)} %get-tuple-element.12, f32[512]{0:T(512)S(1)} %fusion.16), kind=kOutput, calls=%fused_computation.110 | convolution fusion | flops 203816960 | bytes 6426624 | tf_op jit(solution)/shard_map/dot_general | solution.py:48
  55.5 0.7 %fusion.83 = bf16[512,128]{0,1:T(8,128)(2,1)S(1)} fusion(f32[512,1536]{1,0:T(8,128)S(1)} %get-tuple-element.22, f32[512]{0:T(512)S(1)} %get-tuple-element.21, bf16[1024,1024]{1,0:T(8,128)(2,1)S(1)} %get-tuple-element.8, bf16[512,1024]{1,0:T(8,128)(2,1)S(1)} %get-tuple-element.12, f32[512]{0:T(512)S(1)} %fusion.18), kind=kOutput, calls=%fused_computation.109 | convolution fusion | flops 203816960 | bytes 6426624 | tf_op jit(solution)/shard_map/dot_general | solution.py:48
  56.8 0.7 %fusion.80 = bf16[512,128]{0,1:T(8,128)(2,1)S(1)} fusion(f32[512,1536]{1,0:T(8,128)S(1)} %get-tuple-element.20, f32[512]{0:T(512)S(1)} %get-tuple-element.19, bf16[1024,1024]{1,0:T(8,128)(2,1)S(1)} %get-tuple-element.8, bf16[512,1024]{1,0:T(8,128)(2,1)S(1)} %get-tuple-element.12, f32[512]{0:T(512)S(1)} %fusion.20), kind=kOutput, calls=%fused_computation.108 | convolution fusion | flops 203816960 | bytes 6426624 | tf_op jit(solution)/shard_map/dot_general | solution.py:48
  58.1 0.8 %fusion.77 = bf16[512,128]{0,1:T(8,128)(2,1)S(1)} fusion(f32[512,1536]{1,0:T(8,128)S(1)} %get-tuple-element.18, f32[512]{0:T(512)S(1)} %get-tuple-element.17, bf16[512,1024]{1,0:T(8,128)(2,1)S(1)} %get-tuple-element.12, bf16[1024,1024]{1,0:T(8,128)(2,1)S(1)} %get-tuple-element.8, f32[512]{0:T(512)S(1)} %fusion.22), kind=kOutput, calls=%fused_computation.107 | convolution fusion | flops 203816960 | bytes 6426624 | tf_op jit(solution)/shard_map/dot_general | solution.py:48
  59.9 1.1 %maximum_bitcast_fusion = bf16[1,2,512,512]{3,2,1,0:T(8,128)(2,1)} fusion(bf16[1,512,512]{2,1,0:T(8,128)(2,1)S(1)} %fusion.52, bf16[1,512,512]{2,1,0:T(8,128)(2,1)S(1)} %fusion.51), kind=kLoop, calls=%fused_computation.117 | loop fusion | flops 524288 | bytes 2097152 | tf_op jit(solution)/shard_map/broadcast_in_dim | solution.py:106
  (33 shorter events, 5.9 us)
Async XLA Ops:
  0.0 58.9 %copy-start = (bf16[512,512]{1,0:T(8,128)(2,1)S(1)}, bf16[512,512]{1,0:T(8,128)(2,1)}, u32[]{:S(2)}) copy-start(bf16[512,512]{1,0:T(8,128)(2,1)} %param.7) | copy-start | bytes 1572868
  0.0 10.8 %copy-start.1 = (bf16[1,2,512,512]{3,2,1,0:T(8,128)(2,1)S(1)}, bf16[1,2,512,512]{3,2,1,0:T(8,128)(2,1)}, u32[]{:S(2)}) copy-start(bf16[1,2,512,512]{3,2,1,0:T(8,128)(2,1)} %param.4) | copy-start | bytes 3145732
  1.6 10.4 %copy-start.2 = (s32[16]{0:T(128)S(1)}, s32[16]{0:T(128)}, u32[]{:S(2)}) copy-start(s32[16]{0:T(128)} %param.5) | copy-start | bytes 196
  4.3 15.3 %collective-permute-start.2 = (bf16[512,512]{1,0:T(8,128)(2,1)}, bf16[512,512]{1,0:T(8,128)(2,1)}, u32[]{:S(2)}, u32[]{:S(2)}) collective-permute-start(bf16[512,512]{1,0:T(8,128)(2,1)} %get-tuple-element.14), channel_id=1, source_target_pairs={{1,0},{2,1},{3,2},{4,3},{5,4},{6,5},{7,6},{9,8},{10,9},{11,10},{12... | collective-permute-start | bytes 1572872 | tf_op jit(solution)/shard_map/ppermute | solution.py:14
  6.8 16.1 %collective-permute-start = (bf16[512,512]{1,0:T(8,128)(2,1)}, bf16[512,512]{1,0:T(8,128)(2,1)S(1)}, u32[]{:S(2)}, u32[]{:S(2)}) collective-permute-start(bf16[512,512]{1,0:T(8,128)(2,1)} %get-tuple-element.13), channel_id=1, source_target_pairs={{0,1},{1,2},{2,3},{3,4},{4,5},{5,6},{6,7},{8,9},{9,10},{10,11},{11... | collective-permute-start | bytes 1572872 | tf_op jit(solution)/shard_map/ppermute | solution.py:14
  20.7 16.9 %collective-permute-start.3 = (bf16[512,512]{1,0:T(8,128)(2,1)S(1)}, bf16[512,512]{1,0:T(8,128)(2,1)S(1)}, u32[]{:S(2)}, u32[]{:S(2)}) collective-permute-start(bf16[512,512]{1,0:T(8,128)(2,1)S(1)} %broadcast_select_fusion), channel_id=1, source_target_pairs={{1,0},{2,1},{3,2},{4,3},{5,4},{6,5},{7,6},{9,8},{10,9},{11,10},{12... | collective-permute-start | bytes 1572872 | tf_op jit(solution)/shard_map/ppermute | solution.py:14
  23.0 14.7 %collective-permute-start.1 = (bf16[512,512]{1,0:T(8,128)(2,1)S(1)}, bf16[512,512]{1,0:T(8,128)(2,1)S(1)}, u32[]{:S(2)}, u32[]{:S(2)}) collective-permute-start(bf16[512,512]{1,0:T(8,128)(2,1)S(1)} %collective-permute-done), channel_id=1, source_target_pairs={{0,1},{1,2},{2,3},{3,4},{4,5},{5,6},{6,7},{8,9},{9,10},{10,11},{11... | collective-permute-start | bytes 1572872 | tf_op jit(solution)/shard_map/ppermute | solution.py:14
  27.8 10.1 %copy-start.3 = (bf16[512,1536]{1,0:T(8,128)(2,1)S(1)}, bf16[512,1536]{1,0:T(8,128)(2,1)}, u32[]{:S(2)}) copy-start(bf16[512,1536]{1,0:T(8,128)(2,1)} %param.6) | copy-start | bytes 4718596
where the time goes:
time: 61.2 us; the launch traced here: 60.9 us
  matrix products  20.2 us (33%)
  waiting for transfers between devices  13.5 us (22%)
  starting transfers between devices  13.1 us (21%)
  other arithmetic  11.9 us (19%)
  local copies, waits for them, and re-layouts  1.99 us (3%)
    ppermute x4, waiting for transfers between devices, from_behind(): return lax.ppermute(block, axis, route)  13.5 us
    ppermute x4, starting transfers between devices, from_behind(): return lax.ppermute(block, axis, route)  13.1 us
    dot_general x8, matrix products, head_scores(): lax.dot_general(query_part, key_part, (((1,), (1,)), ((), ())), preferred...  7.39 us
    dot_general x8, matrix products, attend(): jnp.dot(weights.astype(jnp.bfloat16), values[:, low:high], preferred_elem...  5.98 us
    reduce_sum x8, other arithmetic, attend(): totals = jnp.sum(weights, axis=1, keepdims=True)  4.71 us
    dot_general x1, matrix products, local(): jnp.dot(normed.reshape(2 * group, width), w_qkv, preferred_element_type=j...  3.52 us
    convert_element_type x2, other arithmetic, normalize(): return (wide * factor).astype(jnp.bfloat16)  2.8 us
    dot_general x1, matrix products, local(): jnp.dot(received.reshape(2 * WIN * group, width), w_qkv[:, width:], prefe...  2.35 us
  transfers between devices with their start and end apart: 4, of which 2 were waited for; matrix products, arithmetic and copies ran while one was open for 11% of the time, Pallas kernels for 0%

commit v1 on v0

v1 whole, which is shorter than its diff:
```python
import functools

import jax
import jax.numpy as jnp
from jax import lax
from jax.experimental import pallas as pl
from jax.experimental.pallas import tpu as pltpu
from jax.sharding import PartitionSpec as P


HEADS = 4
HEAD_DIM = 128
LANES = 128
WIDE = HEAD_DIM + LANES
SCALE2 = HEAD_DIM ** (-0.5) * 1.4426950408889634
VMEM = pl.BlockSpec(memory_space=pltpu.VMEM)
SMEM = pl.BlockSpec(memory_space=pltpu.SMEM)
F32 = jnp.float32
BF16 = jnp.bfloat16


def normalize(rows):
    wide = rows.astype(F32)
    factor = lax.rsqrt(jnp.mean(wide * wide, axis=-1, keepdims=True) + 1e-06)
    return (wide * factor).astype(BF16)


def matmul(left, right):
    return jnp.dot(left, right, preferred_element_type=F32)


def where_am_i():
    place = lax.axis_index("ctx")
    return place, lax.rem(place // 2, 2), lax.rem(place, 2)


def block_first(half, place, count, group):
    return jnp.where(half == 0, place, 2 * count - 1 - place) * group


def start_of(position, lengths_ref, zero):
    def step(e, carry):
        end, start = carry
        end = end + lengths_ref[e]
        return end, jnp.where(end <= position, end, start)

    return lax.fori_loop(0, lengths_ref.shape[0], step, (jnp.int32(0), zero))[1]


def fill_starts(starts_ref, lengths_ref, first):
    for low in range(0, starts_ref.shape[0], LANES):
        position = first + low + lax.broadcasted_iota(jnp.int32, (8, LANES), 1)
        start = start_of(position, lengths_ref, jnp.zeros_like(position))
        wide = jnp.concatenate([start] * (LANES // 8), axis=0)
        starts_ref[low : low + LANES, :] = jnp.transpose(wide)


def across(column, width):
    return jnp.concatenate([column] * (width // LANES), axis=1)


def attend_tile(q_ref, starts_ref, keys_ref, values_ref, old, new, row, rows, low, size, key_first, diag):
    rs = pl.ds(row, rows)
    key = key_first + low + lax.broadcasted_iota(jnp.int32, (rows, size), 1)
    allowed = key >= across(starts_ref[rs, :], size)
    if diag:
        query = key_first + row + lax.broadcasted_iota(jnp.int32, (rows, size), 0)
        allowed = allowed & (key <= query)
    for head in range(HEADS):
        hs = pl.ds(head * HEAD_DIM, HEAD_DIM)
        ws = pl.ds(head * WIDE, WIDE)
        scores = lax.dot_general(
            q_ref[rs, hs],
            keys_ref[pl.ds(low, size), hs],
            (((1,), (1,)), ((), ())),
            preferred_element_type=F32,
        )
        scores = jnp.where(allowed, scores, -jnp.inf)
        peak = jnp.broadcast_to(jnp.max(scores, axis=1, keepdims=True), (rows, LANES))
        if old is not None:
            before = old[1][rs, hs]
            peak = jnp.maximum(before, peak)
        weights = jnp.exp2((scores - across(peak, size)) * SCALE2)
        mixed = matmul(weights.astype(BF16), values_ref[pl.ds(low, size), ws])
        if old is not None:
            fade = jnp.exp2((before - peak) * SCALE2)
            mixed = mixed + across(fade, WIDE) * old[0][rs, ws]
        new[1][rs, hs] = peak
        new[0][rs, ws] = mixed


def project_pair(normed, w_ref, keys_ref, values_ref):
    rows, width = normed.shape
    keys_ref[...] = matmul(normed, w_ref[:, width : 2 * width]).astype(BF16)
    values = matmul(normed, w_ref[:, 2 * width :]).astype(BF16)
    for head in range(HEADS):
        values_ref[:, head * WIDE : head * WIDE + HEAD_DIM] = values[
            :, head * HEAD_DIM : (head + 1) * HEAD_DIM
        ]
        values_ref[:, head * WIDE + HEAD_DIM : (head + 1) * WIDE] = jnp.ones((rows, LANES), BF16)


def attend_block(q_ref, starts_ref, keys_ref, values_ref, old, new, first, behind, lengths_ref):
    group = keys_ref.shape[0]
    rows = group // 2
    key_first = first - behind * group
    for row in range(0, group, rows):
        low = row if behind == 2 else 0
        reach = start_of(first + row, lengths_ref, jnp.int32(0))

        @pl.when(reach < key_first + group)
        def _():
            attend_tile(
                q_ref, starts_ref, keys_ref, values_ref, old, new,
                row, rows, low, group - low, key_first, False,
            )

        if old is not new:
            @pl.when(reach >= key_first + group)
            def _():
                for o, n in zip(old, new):
                    n[pl.ds(row, rows), :] = o[pl.ds(row, rows), :]


def finish(acc_ref, w_out_ref):
    parts = []
    for head in range(HEADS):
        low = head * WIDE
        mixed = acc_ref[:, low : low + HEAD_DIM] / acc_ref[:, low + HEAD_DIM : low + WIDE]
        parts.append(mixed.astype(BF16))
    return matmul(jnp.concatenate(parts, axis=1), w_out_ref[...]).astype(BF16)


def prepare_kernel(frames_ref, straight_ref, cross_a_ref, cross_b_ref):
    side = lax.rem(lax.axis_index("ctx") // 2, 2)
    straight_ref[...] = normalize(frames_ref[0, side])
    rows = cross_a_ref.shape[0]
    cross_a_ref[...] = normalize(frames_ref[0, 1 - side, :rows])
    cross_b_ref[...] = normalize(frames_ref[0, 1 - side, rows:])


def own_kernel(count, late, lengths_ref, *refs):
    parts, (partner_ref, w_ref, q_ref, acc_ref, m_ref, starts_ref, keys_ref, values_ref, block_ref) = (
        refs[:-9], refs[-9:],
    )
    place, side, core = where_am_i()
    half = side if late else 1 - side
    group, width = block_ref.shape
    first = block_first(half, place, count, group)
    fill_starts(starts_ref, lengths_ref, first)
    low = 0
    for part in parts:
        block_ref[low : low + part.shape[0], :] = part[...]
        low += part.shape[0]
    normed = block_ref[...]
    q_ref[...] = matmul(normed, w_ref[:, :width]).astype(BF16)
    project_pair(normed, w_ref, keys_ref, values_ref)
    state = (acc_ref, m_ref)
    rows = group // 2
    for row in range(0, group, rows):
        attend_tile(
            q_ref, starts_ref, keys_ref, values_ref, None, state, row, rows, 0, row + rows, first, True
        )

    @pl.when(half == 1 - core)
    def _():
        project_pair(normalize(partner_ref[0, half]), w_ref, keys_ref, values_ref)
        attend_block(
            q_ref, starts_ref, keys_ref, values_ref, state, state, first, 1, lengths_ref
        )


def far_kernel(count, late, lengths_ref, *refs):
    parts, (partner_ref, w_ref, q_ref, acc_in, m_in, starts_ref, acc_ref, m_ref, keys_ref, values_ref, block_ref) = (
        refs[:-11], refs[-11:],
    )
    place, side, _ = where_am_i()
    half = side if late else 1 - side
    group, _ = block_ref.shape
    first = block_first(half, place, count, group)
    low = 0
    for part in parts:
        block_ref[low : low + part.shape[0], :] = part[...]
        low += part.shape[0]
    if late:
        @pl.when(place // 2 == count // 2 - 1)
        def _():
            block_ref[...] = normalize(partner_ref[0, 0])

    project_pair(block_ref[...], w_ref, keys_ref, values_ref)
    attend_block(
        q_ref, starts_ref, keys_ref, values_ref,
        (acc_in, m_in), (acc_ref, m_ref), first, 2, lengths_ref,
    )


def near_kernel(count, late, lengths_ref, *refs):
    n = 2 if late else 1
    parts = refs[:n]
    own = refs[n : n + 2]
    w_ref, w_out_ref, q_ref, acc_in, m_in, starts_ref = refs[n + 2 : n + 8]
    out_ref, acc_ref, m_ref, keys_ref, values_ref, block_ref = refs[-6:]
    place, side, core = where_am_i()
    half = side if late else 1 - side
    group, _ = block_ref.shape
    first = block_first(half, place, count, group)
    state = (acc_ref, m_ref)

    @pl.when(half == core)
    def _():
        low = 0
        for part in parts:
            block_ref[low : low + part.shape[0], :] = part[...]
            low += part.shape[0]
        if late:
            @pl.when(place == count - 1)
            def _():
                low = 0
                for part in own:
                    block_ref[low : low + part.shape[0], :] = part[...]
                    low += part.shape[0]

        project_pair(block_ref[...], w_ref, keys_ref, values_ref)
        attend_block(
            q_ref, starts_ref, keys_ref, values_ref,
            (acc_in, m_in), state, first, 1, lengths_ref,
        )

    @pl.when(half != core)
    def _():
        acc_ref[...] = acc_in[...]

    out = finish(acc_ref, w_out_ref)
    if late:
        out_ref[0, half] = out
        out_ref[0, 1 - half] = refs[n + 8][...]
    else:
        out_ref[...] = out


def params(mib):
    return pltpu.CompilerParams(vmem_limit_bytes=mib * 1024 * 1024)


def local(frames, episode_lengths, w_qkv, w_out):
    width = w_out.shape[0]
    group = frames.shape[2]
    count = lax.axis_size("ctx")
    chips = count // 2
    pair = [(i, i ^ 1) for i in range(count)]

    def route(links):
        return [(2 * a + c, 2 * b + c) for a, b in links for c in range(2)]

    even = [(c, c + 1) for c in range(0, chips - 1, 2)]
    odd = [(c, c + 1) for c in range(1, chips - 1, 2)]
    swap_x = route(even + [(b, a) for a, b in even])
    swap_d = route(odd + [(b, a) for a, b in odd])
    relay_out = route([(a, b + 1) for a, b in odd] + [(b, a - 1) for a, b in odd])
    relay_in = route([(b + 1, b) for a, b in odd] + [(a - 1, a) for a, b in odd])

    def send(block, links):
        return lax.ppermute(block, "ctx", links)

    def shape(*dims, dtype=BF16):
        return jax.ShapeDtypeStruct(dims, dtype)

    block = shape(group, width)
    part = shape(group // 2, width)
    q_type = shape(group, width)
    acc_type = shape(group, HEADS * WIDE, dtype=F32)
    m_type = shape(group, width, dtype=F32)
    starts_type = shape(group, LANES, dtype=jnp.int32)
    scratch = [
        pltpu.VMEM((group, width), BF16),
        pltpu.VMEM((group, HEADS * WIDE), BF16),
        pltpu.VMEM((group, width), BF16),
    ]

    def call(kernel, late, outs, operands, more=(), flops=2):
        return pl.pallas_call(
            functools.partial(kernel, count, late),
            out_shape=outs,
            in_specs=[SMEM] + [VMEM] * (len(operands) - 1),
            out_specs=jax.tree.map(lambda _: VMEM, outs),
            scratch_shapes=list(more) + scratch,
            compiler_params=params(12),
            cost_estimate=pl.CostEstimate(
                flops=flops * 10**8, bytes_accessed=10**6, transcendentals=0
            ),
        )(*operands)

    partner = send(frames, pair)
    straight, cross_a, cross_b = pl.pallas_call(
        prepare_kernel,
        out_shape=(block, part, part),
        in_specs=[VMEM],
        out_specs=(VMEM,) * 3,
        compiler_params=params(4),
    )(frames)
    hop_in = send(cross_a, relay_out)
    x_in = send(straight, swap_x)
    d_in = send(cross_b, swap_d)
    states = (q_type, acc_type, m_type, starts_type)
    q_x, acc_x, m_x, starts_x = call(
        own_kernel, False, states, (episode_lengths, cross_a, cross_b, partner, w_qkv)
    )
    hop_in, q_x = lax.optimization_barrier((hop_in, q_x))
    r_in = send(hop_in, relay_in)
    q_d, acc_d, m_d, starts_d = call(
        own_kernel, True, states, (episode_lengths, straight, partner, w_qkv)
    )
    x_in, q_d = lax.optimization_barrier((x_in, q_d))
    near_x = send(x_in, pair)
    acc_x, m_x = call(
        far_kernel, False, (acc_type, m_type),
        (episode_lengths, x_in, partner, w_qkv, q_x, acc_x, m_x, starts_x),
    )
    state_scratch = (pltpu.VMEM(acc_type.shape, F32), pltpu.VMEM(m_type.shape, F32))
    out_x = call(
        near_kernel, False, block,
        (episode_lengths, near_x, cross_a, cross_b, w_qkv, w_out, q_x, acc_x, m_x, starts_x),
        state_scratch,
    )
    r_in, d_in, out_x = lax.optimization_barrier((r_in, d_in, out_x))
    near_b = send(d_in, pair)
    near_a = send(r_in, pair)
    acc_d, m_d = call(
        far_kernel, True, (acc_type, m_type),
        (episode_lengths, r_in, d_in, partner, w_qkv, q_d, acc_d, m_d, starts_d),
    )
    return call(
        near_kernel, True, jax.ShapeDtypeStruct(frames.shape, BF16),
        (episode_lengths, near_a, near_b, cross_a, cross_b, w_qkv, w_out, q_d, acc_d, m_d, starts_d, out_x),
        state_scratch,
    )


def solution(mesh):
    in_specs = (P(("dp", "ctx"), None, None, None), P("dp"), P(), P())
    out_specs = P(("dp", "ctx"), None, None, None)
    return jax.shard_map(local, mesh=mesh, in_specs=in_specs, out_specs=out_specs, check_vma=False)
```

time: 61.2 us -> 47.3 us (0.77)
  the two profiles are of different devices: /device:TPU:19 before, /device:TPU:31 now
where the time goes in v1:
time: 47.3 us; the launch traced here: 47.1 us
  Pallas kernels  23 us (49%)
  starting transfers between devices  12.3 us (26%)
  waiting for transfers between devices  8.31 us (18%)
  local copies, waits for them, and re-layouts  3.3 us (7%)
    pallas_call x6, Pallas kernels, call(): pl.pallas_call(functools.partial(kernel, count, late), out_shape=outs, in...  22.7 us
    ppermute x8, starting transfers between devices, send(): return lax.ppermute(block, 'ctx', links)  12.3 us
    ppermute x8, waiting for transfers between devices, send(): return lax.ppermute(block, 'ctx', links)  8.31 us
    unnamed x10, local copies, waits for them, and re-layouts  3.3 us
  transfers between devices with their start and end apart: 8, of which 4 were waited for; matrix products, arithmetic and copies ran while one was open for 0% of the time, Pallas kernels for 38%

profile of v1, /device:TPU:31, one launch (start us, length us, event | category | flops | bytes accessed | tf_op | source)
XLA Modules:
  0.0 47.1 jit_solution(2272221978414812583)
XLA Ops:
  0.0 0.7 %collective-permute-start.1 = (bf16[1,2,512,512]{3,2,1,0:T(8,128)(2,1)}, bf16[1,2,512,512]{3,2,1,0:T(8,128)(2,1)S(1)}, u32[]{:S(2)}, u32[]{:S(2)}) collective-permute-start(bf16[1,2,512,512]{3,2,1,0:T(8,128)(2,1)} %frames_ref.1), channel_id=1, source_target_pairs={{0,1},{1,0},{2,3},{3,2},{4,5},{5,4},{6,7},{7,6},{8,9},{9,8},{10,11... | collective-permute-start | bytes 3145736 | tf_op jit(solution)/shard_map/ppermute | solution.py:263
  0.7 0.0 copy-start.3
  0.7 1.2 %copy-done.3 = bf16[1,2,512,512]{3,2,1,0:T(8,128)(2,1)S(1)} copy-done((bf16[1,2,512,512]{3,2,1,0:T(8,128)(2,1)S(1)}, bf16[1,2,512,512]{3,2,1,0:T(8,128)(2,1)}, u32[]{:S(2)}) %copy-start.3) | copy-done | bytes 1048600
  1.9 0.3 shard_map.46
  2.2 0.3 collective-permute-start.4
  2.6 0.6 %collective-permute-done.1.refs_2_.refs_1_ = bf16[1,2,512,512]{3,2,1,0:T(8,128)(2,1)S(1)} collective-permute-done((bf16[1,2,512,512]{3,2,1,0:T(8,128)(2,1)}, bf16[1,2,512,512]{3,2,1,0:T(8,128)(2,1)S(1)}, u32[]{:S(2)}, u32[]{:S(2)}) %collective-permute-start.1) | collective-permute-done | bytes 1048608 | tf_op jit(solution)/shard_map/ppermute | solution.py:263
  3.2 0.0 copy-start
  3.2 1.4 %copy-done = bf16[512,1536]{1,0:T(8,128)(2,1)S(1)} copy-done((bf16[512,1536]{1,0:T(8,128)(2,1)S(1)}, bf16[512,1536]{1,0:T(8,128)(2,1)}, u32[]{:S(2)}) %copy-start) | copy-done | bytes 1572888
  4.6 0.7 %copy-done.4 = s32[16]{0:T(128)S(1)} copy-done((s32[16]{0:T(128)S(1)}, s32[16]{0:T(128)}, u32[]{:S(2)}) %copy-start.4) | copy-done | bytes 88
  5.2 3.7 %shard_map.48 = (bf16[512,512]{1,0:T(8,128)(2,1)S(1)}, f32[512,1024]{1,0:T(8,128)S(1)}, f32[512,512]{1,0:T(8,128)S(1)}, s32[512,128]{1,0:T(8,128)S(1)}) custom-call(s32[16]{0:T(128)S(1)} %copy-done.4, bf16[512,512]{1,0:T(8,128)(2,1)S(1)} %get-tuple-element.31.refs_0_, bf16[1,2,512,512]{3,2,1,0:T(8,128)(2,1)S(1)} %collective-permute-done.1.refs_2_.refs_1_, ...), custom_call_target="tpu_custom_call" | custom-call | flops 200000000 | bytes 1000000 | tf_op jit(solution)/shard_map/pallas_call | solution.py:281
  8.9 0.0 copy-start.1
  8.9 6.8 %collective-permute-done.4.refs_0_ = bf16[512,512]{1,0:T(8,128)(2,1)S(1)} collective-permute-done((bf16[512,512]{1,0:T(8,128)(2,1)S(1)}, bf16[512,512]{1,0:T(8,128)(2,1)S(1)}, u32[]{:S(2)}, u32[]{:S(2)}) %collective-permute-start.4) | collective-permute-done | bytes 524320 | tf_op jit(solution)/shard_map/ppermute | solution.py:263
  15.8 0.9 %collective-permute-start.5 = (bf16[512,512]{1,0:T(8,128)(2,1)S(1)}, bf16[512,512]{1,0:T(8,128)(2,1)S(1)}, u32[]{:S(2)}, u32[]{:S(2)}) collective-permute-start(bf16[512,512]{1,0:T(8,128)(2,1)S(1)} %collective-permute-done.4.refs_0_), channel_id=1, source_target_pairs={{0,1},{1,0},{2,3},{3,2},{4,5},{5,4},{6,7},{7,6},{8,9},{9,8},{10,11... | collective-permute-start | bytes 1572872 | tf_op jit(solution)/shard_map/ppermute | solution.py:263
  16.7 1.3 %collective-permute-start = (bf16[256,512]{1,0:T(8,128)(2,1)S(1)}, bf16[256,512]{1,0:T(8,128)(2,1)S(1)}, u32[]{:S(2)}, u32[]{:S(2)}) collective-permute-start(bf16[256,512]{1,0:T(8,128)(2,1)S(1)} %get-tuple-element.27.refs_0_.refs_1_.refs_2_), channel_id=1, source_target_pairs={{2,6},{3,7},{4,0},{5,1},{10,14},{11,15},{12,8},{13,9},{18,22},{19,... | collective-permute-start | bytes 786440 | tf_op jit(solution)/shard_map/ppermute | solution.py:263
  17.9 0.7 %collective-permute-start.3 = (bf16[256,512]{1,0:T(8,128)(2,1)S(1)}, bf16[256,512]{1,0:T(8,128)(2,1)S(1)}, u32[]{:S(2)}, u32[]{:S(2)}) collective-permute-start(bf16[256,512]{1,0:T(8,128)(2,1)S(1)} %get-tuple-element.28.refs_1_.refs_2_.refs_3_), channel_id=1, source_target_pairs={{2,4},{3,5},{4,2},{5,3},{10,12},{11,13},{12,10},{13,11},{18,20},{1... | collective-permute-start | bytes 786440 | tf_op jit(solution)/shard_map/ppermute | solution.py:263
  18.6 7.0 %shard_map.47 = (bf16[512,512]{1,0:T(8,128)(2,1)S(1)}, f32[512,1024]{1,0:T(8,128)S(1)}, f32[512,512]{1,0:T(8,128)S(1)}, s32[512,128]{1,0:T(8,128)S(1)}) custom-call(s32[16]{0:T(128)S(1)} %copy-done.4, bf16[256,512]{1,0:T(8,128)(2,1)S(1)} %get-tuple-element.27.refs_0_.refs_1_.refs_2_, bf16[256,512]{1,0:T(8,128)(2,1)S(1)} %get-tuple-element.28.refs_1_.refs_2_.refs_3_, ...), custom_call_target="tpu_custom_call" | custom-call | flops 200000000 | bytes 1000000 | tf_op jit(solution)/shard_map/pallas_call | solution.py:281
  25.7 0.7 %collective-permute-done = bf16[256,512]{1,0:T(8,128)(2,1)S(1)} collective-permute-done((bf16[256,512]{1,0:T(8,128)(2,1)S(1)}, bf16[256,512]{1,0:T(8,128)(2,1)S(1)}, u32[]{:S(2)}, u32[]{:S(2)}) %collective-permute-start) | collective-permute-done | bytes 262176 | tf_op jit(solution)/shard_map/ppermute | solution.py:263
  26.4 2.4 %collective-permute-start.2 = (bf16[256,512]{1,0:T(8,128)(2,1)S(1)}, bf16[256,512]{1,0:T(8,128)(2,1)S(1)}, u32[]{:S(2)}, u32[]{:S(2)}) collective-permute-start(bf16[256,512]{1,0:T(8,128)(2,1)S(1)} %collective-permute-done), channel_id=1, source_target_pairs={{6,4},{7,5},{0,2},{1,3},{14,12},{15,13},{8,10},{9,11},{22,20},{23,... | collective-permute-start | bytes 786440 | tf_op jit(solution)/shard_map/ppermute | solution.py:263
  28.8 0.0 copy-done.1
  28.8 0.0 copy-start.2
  28.8 1.9 %shard_map.49 = (f32[512,1024]{1,0:T(8,128)S(1)}, f32[512,512]{1,0:T(8,128)S(1)}) custom-call(s32[16]{0:T(128)S(1)} %copy-done.4, bf16[512,512]{1,0:T(8,128)(2,1)S(1)} %collective-permute-done.4.refs_0_, bf16[1,2,512,512]{3,2,1,0:T(8,128)(2,1)S(1)} %collective-permute-done.1.refs_2_.refs_1_, bf16[512,1536]{1,0:T(8,128)(2,1)S(1)} %copy-done.1, ...), custom_call_target="tpu_custom_call" | custom-call | flops 200000000 | bytes 1000000 | tf_op jit(solution)/shard_map/pallas_call | solution.py:281
  30.7 0.0 collective-permute-done.5.refs_0_
  30.7 0.0 copy-done.2
  30.8 1.2 %shard_map.50.refs_10_ = bf16[512,512]{1,0:T(8,128)(2,1)S(1)} custom-call(s32[16]{0:T(128)S(1)} %copy-done.4, bf16[512,512]{1,0:T(8,128)(2,1)S(1)} %collective-permute-done.5.refs_0_, bf16[256,512]{1,0:T(8,128)(2,1)S(1)} %get-tuple-element.27.refs_0_.refs_1_.refs_2_, bf16[256,512]{1,0:T(8,128)(2,1)S(1)} %get-tuple-element.28.refs_1_.refs_2_.refs_3_, ...), custom_call_target="tpu_custom_call" | custom-call | flops 200000000 | bytes 1000000 | tf_op jit(solution)/shard_map/pallas_call | solution.py:281
  31.9 0.0 collective-permute-done.3.refs_1_
  31.9 0.1 collective-permute-done.2.refs_0_
  32.1 6.1 %collective-permute-start.6 = (bf16[256,512]{1,0:T(8,128)(2,1)S(1)}, bf16[256,512]{1,0:T(8,128)(2,1)S(1)}, u32[]{:S(2)}, u32[]{:S(2)}) collective-permute-start(bf16[256,512]{1,0:T(8,128)(2,1)S(1)} %collective-permute-done.2.refs_0_), channel_id=1, source_target_pairs={{0,1},{1,0},{2,3},{3,2},{4,5},{5,4},{6,7},{7,6},{8,9},{9,8},{10,11... | collective-permute-start | bytes 786440 | tf_op jit(solution)/shard_map/ppermute | solution.py:263
  38.1 0.1 collective-permute-start.7
  38.2 3.6 %shard_map.51 = (f32[512,1024]{1,0:T(8,128)S(1)}, f32[512,512]{1,0:T(8,128)S(1)}) custom-call(s32[16]{0:T(128)S(1)} %copy-done.4, bf16[256,512]{1,0:T(8,128)(2,1)S(1)} %collective-permute-done.2.refs_0_, bf16[256,512]{1,0:T(8,128)(2,1)S(1)} %collective-permute-done.3.refs_1_, bf16[1,2,512,512]{3,2,1,0:T(8,128)(2,1)S(1)} %collective-permute-done.1.refs_2_.refs_1_, ...), custom_call_target="tpu_custom_call" | custom-call | flops 200000000 | bytes 1000000 | tf_op jit(solution)/shard_map/pallas_call | solution.py:281
  41.8 0.0 collective-permute-done.6.refs_0_
  41.8 0.0 collective-permute-done.7.refs_1_
  41.8 5.3 %shard_map.52 = bf16[1,2,512,512]{3,2,1,0:T(8,128)(2,1)} custom-call(s32[16]{0:T(128)S(1)} %copy-done.4, bf16[256,512]{1,0:T(8,128)(2,1)S(1)} %collective-permute-done.6.refs_0_, bf16[256,512]{1,0:T(8,128)(2,1)S(1)} %collective-permute-done.7.refs_1_, bf16[256,512]{1,0:T(8,128)(2,1)S(1)} %get-tuple-element.27.refs_0_.refs_1_.refs_2_, ...), custom_call_target="tpu_custom_call" | custom-call | flops 200000000 | bytes 1000000 | tf_op jit(solution)/shard_map/pallas_call | solution.py:281
  (1 shorter events, 0.0 us)
Async XLA Ops:
  0.0 3.2 %collective-permute-start.1 = (bf16[1,2,512,512]{3,2,1,0:T(8,128)(2,1)}, bf16[1,2,512,512]{3,2,1,0:T(8,128)(2,1)S(1)}, u32[]{:S(2)}, u32[]{:S(2)}) collective-permute-start(bf16[1,2,512,512]{3,2,1,0:T(8,128)(2,1)} %frames_ref.1), channel_id=1, source_target_pairs={{0,1},{1,0},{2,3},{3,2},{4,5},{5,4},{6,7},{7,6},{8,9},{9,8},{10,11... | collective-permute-start | bytes 3145736 | tf_op jit(solution)/shard_map/ppermute | solution.py:263
  0.7 1.2 %copy-start.3 = (bf16[1,2,512,512]{3,2,1,0:T(8,128)(2,1)S(1)}, bf16[1,2,512,512]{3,2,1,0:T(8,128)(2,1)}, u32[]{:S(2)}) copy-start(bf16[1,2,512,512]{3,2,1,0:T(8,128)(2,1)} %frames_ref.1) | copy-start | bytes 3145732
  2.2 13.5 %collective-permute-start.4 = (bf16[512,512]{1,0:T(8,128)(2,1)S(1)}, bf16[512,512]{1,0:T(8,128)(2,1)S(1)}, u32[]{:S(2)}, u32[]{:S(2)}) collective-permute-start(bf16[512,512]{1,0:T(8,128)(2,1)S(1)} %get-tuple-element.31.refs_0_), channel_id=1, source_target_pairs={{0,2},{1,3},{4,6},{5,7},{2,0},{3,1},{6,4},{7,5},{8,10},{9,11},{12,... | collective-permute-start | bytes 1572872 | tf_op jit(solution)/shard_map/ppermute | solution.py:263
  3.2 1.4 %copy-start = (bf16[512,1536]{1,0:T(8,128)(2,1)S(1)}, bf16[512,1536]{1,0:T(8,128)(2,1)}, u32[]{:S(2)}) copy-start(bf16[512,1536]{1,0:T(8,128)(2,1)} %refs_4_.3) | copy-start | bytes 4718596
  4.6 0.7 %copy-start.4 = (s32[16]{0:T(128)S(1)}, s32[16]{0:T(128)}, u32[]{:S(2)}) copy-start(s32[16]{0:T(128)} %lengths_ref.11) | copy-start | bytes 196
  8.9 19.8 %copy-start.1 = (bf16[512,1536]{1,0:T(8,128)(2,1)S(1)}, bf16[512,1536]{1,0:T(8,128)(2,1)}, u32[]{:S(2)}) copy-start(bf16[512,1536]{1,0:T(8,128)(2,1)} %refs_4_.3) | copy-start | bytes 4718596
  15.8 14.9 %collective-permute-start.5 = (bf16[512,512]{1,0:T(8,128)(2,1)S(1)}, bf16[512,512]{1,0:T(8,128)(2,1)S(1)}, u32[]{:S(2)}, u32[]{:S(2)}) collective-permute-start(bf16[512,512]{1,0:T(8,128)(2,1)S(1)} %collective-permute-done.4.refs_0_), channel_id=1, source_target_pairs={{0,1},{1,0},{2,3},{3,2},{4,5},{5,4},{6,7},{7,6},{8,9},{9,8},{10,11... | collective-permute-start | bytes 1572872 | tf_op jit(solution)/shard_map/ppermute | solution.py:263
  16.7 9.7 %collective-permute-start = (bf16[256,512]{1,0:T(8,128)(2,1)S(1)}, bf16[256,512]{1,0:T(8,128)(2,1)S(1)}, u32[]{:S(2)}, u32[]{:S(2)}) collective-permute-start(bf16[256,512]{1,0:T(8,128)(2,1)S(1)} %get-tuple-element.27.refs_0_.refs_1_.refs_2_), channel_id=1, source_target_pairs={{2,6},{3,7},{4,0},{5,1},{10,14},{11,15},{12,8},{13,9},{18,22},{19,... | collective-permute-start | bytes 786440 | tf_op jit(solution)/shard_map/ppermute | solution.py:263
  17.9 14.0 %collective-permute-start.3 = (bf16[256,512]{1,0:T(8,128)(2,1)S(1)}, bf16[256,512]{1,0:T(8,128)(2,1)S(1)}, u32[]{:S(2)}, u32[]{:S(2)}) collective-permute-start(bf16[256,512]{1,0:T(8,128)(2,1)S(1)} %get-tuple-element.28.refs_1_.refs_2_.refs_3_), channel_id=1, source_target_pairs={{2,4},{3,5},{4,2},{5,3},{10,12},{11,13},{12,10},{13,11},{18,20},{1... | collective-permute-start | bytes 786440 | tf_op jit(solution)/shard_map/ppermute | solution.py:263
  26.4 5.7 %collective-permute-start.2 = (bf16[256,512]{1,0:T(8,128)(2,1)S(1)}, bf16[256,512]{1,0:T(8,128)(2,1)S(1)}, u32[]{:S(2)}, u32[]{:S(2)}) collective-permute-start(bf16[256,512]{1,0:T(8,128)(2,1)S(1)} %collective-permute-done), channel_id=1, source_target_pairs={{6,4},{7,5},{0,2},{1,3},{14,12},{15,13},{8,10},{9,11},{22,20},{23,... | collective-permute-start | bytes 786440 | tf_op jit(solution)/shard_map/ppermute | solution.py:263
  28.8 2.0 %copy-start.2 = (bf16[512,512]{1,0:T(8,128)(2,1)S(1)}, bf16[512,512]{1,0:T(8,128)(2,1)}, u32[]{:S(2)}) copy-start(bf16[512,512]{1,0:T(8,128)(2,1)} %refs_5_.1) | copy-start | bytes 1572868
  32.1 9.7 %collective-permute-start.6 = (bf16[256,512]{1,0:T(8,128)(2,1)S(1)}, bf16[256,512]{1,0:T(8,128)(2,1)S(1)}, u32[]{:S(2)}, u32[]{:S(2)}) collective-permute-start(bf16[256,512]{1,0:T(8,128)(2,1)S(1)} %collective-permute-done.2.refs_0_), channel_id=1, source_target_pairs={{0,1},{1,0},{2,3},{3,2},{4,5},{5,4},{6,7},{7,6},{8,9},{9,8},{10,11... | collective-permute-start | bytes 786440 | tf_op jit(solution)/shard_map/ppermute | solution.py:263
  38.1 3.7 %collective-permute-start.7 = (bf16[256,512]{1,0:T(8,128)(2,1)S(1)}, bf16[256,512]{1,0:T(8,128)(2,1)S(1)}, u32[]{:S(2)}, u32[]{:S(2)}) collective-permute-start(bf16[256,512]{1,0:T(8,128)(2,1)S(1)} %collective-permute-done.3.refs_1_), channel_id=1, source_target_pairs={{0,1},{1,0},{2,3},{3,2},{4,5},{5,4},{6,7},{7,6},{8,9},{9,8},{10,11... | collective-permute-start | bytes 786440 | tf_op jit(solution)/shard_map/ppermute | solution.py:263

commit v2 on v0

v2 whole, which is shorter than its diff:
```python
import functools

import jax
import jax.numpy as jnp
from jax import lax
from jax.experimental import pallas as pl
from jax.experimental.pallas import tpu as pltpu
from jax.sharding import PartitionSpec as P


HEADS = 4
HEAD_DIM = 128
LANES = 128
WIDE = HEAD_DIM + LANES
SCALE2 = HEAD_DIM ** (-0.5) * 1.4426950408889634
APART = -1e30
VMEM = pl.BlockSpec(memory_space=pltpu.VMEM)
SMEM = pl.BlockSpec(memory_space=pltpu.SMEM)
HBM = pl.BlockSpec(memory_space=pltpu.HBM)
F32 = jnp.float32
BF16 = jnp.bfloat16


def normalize(rows):
    wide = rows.astype(F32)
    factor = lax.rsqrt(jnp.mean(wide * wide, axis=-1, keepdims=True) + 1e-06)
    return (wide * factor).astype(BF16)


def matmul(left, right):
    return jnp.dot(left, right, preferred_element_type=F32)


def where_am_i():
    place = lax.axis_index("ctx")
    return place, lax.rem(place // 2, 2), lax.rem(place, 2)


def block_first(half, place, count, group):
    return jnp.where(half == 0, place, 2 * count - 1 - place) * group


def beside(left, right):
    return jnp.concatenate([left, right], axis=1)


def across(column, width):
    return jnp.concatenate([column] * (width // LANES), axis=1)


def inside(bounds_ref, first, rows):
    position = first + lax.broadcasted_iota(jnp.int32, (rows, LANES), 0)
    return (position >= bounds_ref[0:1, :]) & (position < bounds_ref[1:2, :])


def query_marks(bounds_ref, first, rows):
    return jnp.where(inside(bounds_ref, first, rows), 1.0, 0.0).astype(BF16)


def key_marks(bounds_ref, first, rows):
    return jnp.where(inside(bounds_ref, first, rows), 0.0, APART).astype(BF16)


def attend(q_ref, marks, pair, old, tiles):
    keys_ref, values_ref, key_marks_ref = pair
    rows = marks.shape[0]
    out = []
    for head in range(HEADS):
        hs = pl.ds(head * HEAD_DIM, HEAD_DIM)
        ws = pl.ds(head * WIDE, WIDE)
        query = beside(q_ref[:, hs], marks)
        scores, peaks = [], []
        for low, size, top, bottom, causal in tiles:
            cs = pl.ds(low, size)
            tile = lax.dot_general(
                query[top:bottom],
                beside(keys_ref[cs, hs], key_marks_ref[cs, :]),
                (((1,), (1,)), ((), ())),
                preferred_element_type=F32,
            )
            if causal:
                here = lax.broadcasted_iota(jnp.int32, (size, size), 0)
                there = lax.broadcasted_iota(jnp.int32, (size, size), 1)
                edge = jnp.where(there <= here, tile[:size], APART)
                tile = jnp.concatenate([edge, tile[size:]], axis=0) if bottom - top > size else edge
            scores.append(tile)
            peak = jnp.max(tile, axis=1, keepdims=True)
            peaks.append(jnp.broadcast_to(peak, (bottom - top, LANES)))
        peak = spread(jnp.maximum, [(p, t[2], t[3]) for p, t in zip(peaks, tiles)], rows)
        if old is not None:
            before = old[1][:, hs]
            peak = jnp.maximum(before, peak)
        mixes = []
        for tile, (low, size, top, bottom, _) in zip(scores, tiles):
            weights = jnp.exp2(tile - across(peak[top:bottom], size)).astype(BF16)
            ones = jnp.ones((size, LANES), BF16)
            mix = matmul(weights, beside(values_ref[pl.ds(low, size), hs], ones))
            mixes.append((mix, top, bottom))
        mixed = spread(jnp.add, mixes, rows)
        if old is not None:
            mixed = mixed + across(jnp.exp2(before - peak), WIDE) * old[0][:, ws]
        out.append((mixed, peak))
    return out


def spread(combine, items, rows):
    whole = [item for item, top, bottom in items if bottom - top == rows]
    total = whole[0]
    for item, top, bottom in items:
        if bottom - top == rows:
            continue
        pieces = [total[:top]] if top else []
        pieces.append(combine(total[top:bottom], item))
        if bottom < rows:
            pieces.append(total[bottom:])
        total = jnp.concatenate(pieces, axis=0)
    return total


def keep(out, new):
    for head, (mixed, peak) in enumerate(out):
        new[0][:, head * WIDE : (head + 1) * WIDE] = mixed
        new[1][:, head * HEAD_DIM : (head + 1) * HEAD_DIM] = peak


def project_pair(normed, first, bounds_ref, w_ref, pair):
    rows, width = normed.shape
    keys_ref, values_ref, key_marks_ref = pair
    keys_ref[...] = matmul(normed, w_ref[:, width : 2 * width]).astype(BF16)
    values_ref[...] = matmul(normed, w_ref[:, 2 * width :]).astype(BF16)
    key_marks_ref[...] = key_marks(bounds_ref, first, rows)


def gather(parts, block_ref):
    low = 0
    for part in parts:
        block_ref[low : low + part.shape[0], :] = part[...]
        low += part.shape[0]


def prepare_kernel(frames_ref, lengths_ref, straight_ref, cross_a_ref, cross_b_ref, bounds_ref):
    _, side, _ = where_am_i()
    straight_ref[...] = normalize(frames_ref[0, side])
    rows = cross_a_ref.shape[0]
    cross_a_ref[...] = normalize(frames_ref[0, 1 - side, :rows])
    cross_b_ref[...] = normalize(frames_ref[0, 1 - side, rows:])
    lane = lax.broadcasted_iota(jnp.int32, (8, LANES), 1)
    row = lax.broadcasted_iota(jnp.int32, (8, LANES), 0)

    def step(e, carry):
        begin, bounds = carry
        end = begin + lengths_ref[e]
        return end, jnp.where(lane == e, jnp.where(row == 0, begin, end), bounds)

    bounds_ref[...] = lax.fori_loop(
        0, lengths_ref.shape[0], step, (jnp.int32(0), jnp.zeros((8, LANES), jnp.int32)),
        unroll=True,
    )[1]


def own_block(normed, first, bounds_ref, w_ref, q_ref, state, pair):
    group, width = normed.shape
    rows = group // 2
    q_ref[...] = (matmul(normed, w_ref[:, :width]) * SCALE2).astype(BF16)
    project_pair(normed, first, bounds_ref, w_ref, pair)
    marks = query_marks(bounds_ref, first, group)
    tiles = ((0, rows, 0, group, True), (rows, rows, rows, group, True))
    keep(attend(q_ref, marks, pair, None, tiles), state)


def own_x_kernel(
    count, bounds_ref, cross_a_ref, cross_b_ref, w_ref, q_ref, acc_ref, m_ref, block_ref, *pair
):
    place, side, _ = where_am_i()
    half = 1 - side
    first = block_first(half, place, count, block_ref.shape[0])
    gather((cross_a_ref, cross_b_ref), block_ref)
    own_block(block_ref[...], first, bounds_ref, w_ref, q_ref, (acc_ref, m_ref), pair)


def own_d_kernel(
    count, bounds_ref, straight_ref, partner_ref, w_ref, q_x_ref, acc_in, m_in,
    q_ref, acc_ref, m_ref, acc_x_ref, m_x_ref, block_ref, *pair
):
    place, side, core = where_am_i()
    group = straight_ref.shape[0]
    first = block_first(side, place, count, group)
    state = (acc_ref, m_ref)
    own_block(straight_ref[...], first, bounds_ref, w_ref, q_ref, state, pair)
    half = 1 - core
    first = block_first(half, place, count, group)
    project_pair(normalize(partner_ref[0, half]), first - group, bounds_ref, w_ref, pair)
    marks = query_marks(bounds_ref, first, group)
    tiles = ((0, group, 0, group, False),)

    @pl.when(half == side)
    def _():
        keep(attend(q_ref, marks, pair, state, tiles), state)
        acc_x_ref[...] = acc_in[...]
        m_x_ref[...] = m_in[...]

    @pl.when(half != side)
    def _():
        keep(attend(q_x_ref, marks, pair, (acc_in, m_in), tiles), (acc_x_ref, m_x_ref))


def far_kernel(
    count, late, bounds_ref, far_ref, partner_ref, w_ref, q_ref, acc_in, m_in,
    acc_ref, m_ref, block_ref, *pair
):
    place, side, _ = where_am_i()
    half = side if late else 1 - side
    group, _ = far_ref.shape
    first = block_first(half, place, count, group)
    rows = group // 2
    block_ref[...] = far_ref[...]
    if late:
        @pl.when(place // 2 == count // 2 - 1)
        def _():
            block_ref[...] = normalize(partner_ref[0, 0])

    project_pair(block_ref[...], first - 2 * group, bounds_ref, w_ref, pair)
    marks = query_marks(bounds_ref, first, group)
    tiles = ((rows, rows, 0, group, False), (0, rows, 0, rows, False))
    keep(attend(q_ref, marks, pair, (acc_in, m_in), tiles), (acc_ref, m_ref))


def near_kernel(count, late, bounds_ref, near_ref, cross_a_ref, cross_b_ref, *refs):
    w_ref, w_out_ref, q_ref, acc_in, m_in = refs[:5]
    out_ref, stage_ref, sems, block_ref = refs[-7:-3]
    pair = refs[-3:]
    place, side, core = where_am_i()
    half = side if late else 1 - side
    group, _ = block_ref.shape
    first = block_first(half, place, count, group)
    rows = group // 2

    def emit(wide):
        for row in range(0, group, rows):
            rs = slice(row, row + rows)
            mixed = [(m[rs, :HEAD_DIM] / m[rs, HEAD_DIM:]).astype(BF16) for m in wide]
            out = matmul(jnp.concatenate(mixed, axis=1), w_out_ref[...])
            stage_ref[rs, :] = out.astype(BF16)
            copy_out(row).start()

    def copy_out(row):
        rs = pl.ds(row, rows)
        return pltpu.make_async_copy(
            stage_ref.at[rs], out_ref.at[0, half, rs], sems.at[row // rows]
        )

    @pl.when(half == core)
    def _():
        block_ref[...] = near_ref[...]
        if late:
            @pl.when(place == count - 1)
            def _():
                gather((cross_a_ref, cross_b_ref), block_ref)

        project_pair(block_ref[...], first - group, bounds_ref, w_ref, pair)
        marks = query_marks(bounds_ref, first, group)
        out = attend(q_ref, marks, pair, (acc_in, m_in), ((0, group, 0, group, False),))
        emit([mixed for mixed, _ in out])

    @pl.when(half != core)
    def _():
        emit([acc_in[:, h * WIDE : (h + 1) * WIDE] for h in range(HEADS)])

    for row in range(0, group, rows):
        copy_out(row).wait()


def params(mib):
    return pltpu.CompilerParams(vmem_limit_bytes=mib * 1024 * 1024)


def local(frames, episode_lengths, w_qkv, w_out):
    width = w_out.shape[0]
    group = frames.shape[2]
    count = lax.axis_size("ctx")
    chips = count // 2
    pair = [(i, i ^ 1) for i in range(count)]

    def route(links):
        return [(2 * a + c, 2 * b + c) for a, b in links for c in range(2)]

    even = [(c, c + 1) for c in range(0, chips - 1, 2)]
    odd = [(c, c + 1) for c in range(1, chips - 1, 2)]
    swap_x = route(even + [(b, a) for a, b in even])
    swap_d = route(odd + [(b, a) for a, b in odd])
    relay_out = route([(a, b + 1) for a, b in odd] + [(b, a - 1) for a, b in odd])
    relay_in = route([(b + 1, b) for a, b in odd] + [(a - 1, a) for a, b in odd])

    def send(block, links):
        return lax.ppermute(block, "ctx", links)

    def shape(*dims, dtype=BF16):
        return jax.ShapeDtypeStruct(dims, dtype)

    block = shape(group, width)
    part = shape(group // 2, width)
    acc_type = shape(group, HEADS * WIDE, dtype=F32)
    m_type = shape(group, width, dtype=F32)
    scratch = [pltpu.VMEM((group, width), BF16)] * 3 + [pltpu.VMEM((group, LANES), BF16)]

    def call(kernel, outs, operands, aliased=None):
        specs = [VMEM] * len(operands)
        options = dict(out_specs=(VMEM,) * len(outs), scratch_shapes=scratch)
        if aliased is not None:
            options["out_specs"] = (HBM,)
            options["scratch_shapes"] = [
                pltpu.VMEM((group, width), BF16), pltpu.SemaphoreType.DMA((2,)),
            ] + scratch
        if aliased:
            specs.append(HBM)
            options["input_output_aliases"] = {len(operands): 0}
            operands = operands + aliased
        return pl.pallas_call(
            kernel,
            out_shape=outs,
            in_specs=specs,
            compiler_params=params(14),
            cost_estimate=pl.CostEstimate(flops=10**8, bytes_accessed=10**6, transcendentals=0),
            **options,
        )(*operands)

    partner = send(frames, pair)
    straight, cross_a, cross_b, bounds = pl.pallas_call(
        prepare_kernel,
        out_shape=(block, part, part, shape(8, LANES, dtype=jnp.int32)),
        in_specs=[VMEM, SMEM],
        out_specs=(VMEM,) * 4,
        compiler_params=params(4),
        cost_estimate=pl.CostEstimate(flops=10**10, bytes_accessed=10**6, transcendentals=0),
    )(frames, episode_lengths)
    w = w_qkv
    hop_in = send(cross_a, relay_out)
    x_in = send(straight, swap_x)
    d_in = send(cross_b, swap_d)
    bind = functools.partial
    state = (acc_type, m_type)
    q_x, acc_x, m_x = call(
        bind(own_x_kernel, count), (block,) + state, (bounds, cross_a, cross_b, w)
    )
    hop_in, q_x = lax.optimization_barrier((hop_in, q_x))
    r_in = send(hop_in, relay_in)
    q_d, acc_d, m_d, acc_x, m_x = call(
        bind(own_d_kernel, count), (block,) + state + state,
        (bounds, straight, partner, w, q_x, acc_x, m_x),
    )
    x_in, q_d = lax.optimization_barrier((x_in, q_d))
    near_x = send(x_in, pair)
    acc_x, m_x = call(
        bind(far_kernel, count, False), state,
        (bounds, x_in, partner, w, q_x, acc_x, m_x),
    )
    whole = (jax.ShapeDtypeStruct(frames.shape, BF16),)
    (out,) = call(
        bind(near_kernel, count, False), whole,
        (bounds, near_x, cross_a, cross_b, w, w_out, q_x, acc_x, m_x), (),
    )
    r_in, d_in, out = lax.optimization_barrier((r_in, d_in, out))
    d_block = jnp.concatenate([r_in, d_in], axis=0)
    near_d = send(d_block, pair)
    acc_d, m_d = call(
        bind(far_kernel, count, True), state,
        (bounds, d_block, partner, w, q_d, acc_d, m_d),
    )
    (out,) = call(
        bind(near_kernel, count, True), whole,
        (bounds, near_d, cross_a, cross_b, w, w_out, q_d, acc_d, m_d), (out,),
    )
    return out


def solution(mesh):
    in_specs = (P(("dp", "ctx"), None, None, None), P("dp"), P(), P())
    out_specs = P(("dp", "ctx"), None, None, None)
    return jax.shard_map(local, mesh=mesh, in_specs=in_specs, out_specs=out_specs, check_vma=False)
```

time: 61.2 us -> 38.2 us (0.62)
  matrix products: 20.2 us -> 0 us
  Pallas kernels: 0 us -> 17.2 us
  other arithmetic: 11.9 us -> 0 us
  waiting for transfers between devices: 13.5 us -> 7.52 us
  starting transfers between devices: 13.1 us -> 11 us
    dot_general x20 -> x0, matrix products: 20.2 us -> none  [the longest x8 7.39 us: head_scores(): lax.dot_general(query_part, key_part, (((1,), (1,)), ((), ())), preferred...]
    pallas_call x0 -> x7, Pallas kernels: none -> 17.2 us  [the longest x6 16.3 us: call(): pl.pallas_call(kernel, out_shape=outs, in_specs=specs, compiler_params=pa...]
    reduce_sum x10 -> x0, other arithmetic: 6.42 us -> none  [the longest x8 4.71 us: attend(): totals = jnp.sum(weights, axis=1, keepdims=True)]
    ppermute x4 -> x7, waiting for transfers between devices: 13.5 us -> 7.52 us  [send(): return lax.ppermute(block, 'ctx', links)]
    convert_element_type x2 -> x0, other arithmetic: 2.8 us -> none  [normalize(): return (wide * factor).astype(jnp.bfloat16)]
    ppermute x4 -> x7, starting transfers between devices: 13.1 us -> 11 us  [send(): return lax.ppermute(block, 'ctx', links)]
    unnamed x9, local copies, waits for them, and re-layouts: 0.02 us -> 1.91 us
    squeeze x3 -> x0, local copies, waits for them, and re-layouts: 1.44 us -> none  [the longest x1 1.06 us: local(): low_now = normed[0]]
  transfers between devices with their start and end apart: 4 -> 7, of which waited for: 2 -> 3; matrix products, arithmetic and copies ran while one was open for 11% -> 0% of each run, Pallas kernels for 0% -> 36%
where the time goes in v2:
time: 38.2 us; the launch traced here: 38 us
  Pallas kernels  17.2 us (45%)
  starting transfers between devices  11 us (29%)
  waiting for transfers between devices  7.52 us (20%)
  local copies, waits for them, and re-layouts  1.93 us (5%)
    pallas_call x6, Pallas kernels, call(): pl.pallas_call(kernel, out_shape=outs, in_specs=specs, compiler_params=pa...  16.3 us
    ppermute x7, starting transfers between devices, send(): return lax.ppermute(block, 'ctx', links)  11 us
    ppermute x7, waiting for transfers between devices, send(): return lax.ppermute(block, 'ctx', links)  7.52 us
    unnamed x9, local copies, waits for them, and re-layouts  1.91 us
    pallas_call x1, Pallas kernels, local(): pl.pallas_call(prepare_kernel, out_shape=(block, part, part, shape(8, LAN...  0.9 us
  transfers between devices with their start and end apart: 7, of which 3 were waited for; matrix products, arithmetic and copies ran while one was open for 0% of the time, Pallas kernels for 36%

profile of v2, /device:TPU:19, one launch (start us, length us, event | category | flops | bytes accessed | tf_op | source)
XLA Modules:
  0.0 38.0 jit_solution(1586891737951052027)
XLA Ops:
  0.0 0.0 copy-start
  0.0 0.7 %collective-permute-start.4 = (bf16[1,2,512,512]{3,2,1,0:T(8,128)(2,1)}, bf16[1,2,512,512]{3,2,1,0:T(8,128)(2,1)S(1)}, u32[]{:S(2)}, u32[]{:S(2)}) collective-permute-start(bf16[1,2,512,512]{3,2,1,0:T(8,128)(2,1)} %frames_ref.1), channel_id=1, source_target_pairs={{0,1},{1,0},{2,3},{3,2},{4,5},{5,4},{6,7},{7,6},{8,9},{9,8},{10,11... | collective-permute-start | bytes 3145736 | tf_op jit(solution)/shard_map/ppermute | solution.py:295
  0.7 0.0 copy-start.2
  0.7 1.2 %copy-done.2 = bf16[1,2,512,512]{3,2,1,0:T(8,128)(2,1)S(1)} copy-done((bf16[1,2,512,512]{3,2,1,0:T(8,128)(2,1)S(1)}, bf16[1,2,512,512]{3,2,1,0:T(8,128)(2,1)}, u32[]{:S(2)}) %copy-start.2) | copy-done | bytes 1048600
  1.9 0.0 copy-start.3
  1.9 0.7 %copy-done.3 = s32[16]{0:T(128)S(1)} copy-done((s32[16]{0:T(128)S(1)}, s32[16]{0:T(128)}, u32[]{:S(2)}) %copy-start.3) | copy-done | bytes 88
  2.6 0.9 %shard_map.46 = (bf16[512,512]{1,0:T(8,128)(2,1)S(1)}, bf16[256,512]{1,0:T(8,128)(2,1)S(1)}, bf16[256,512]{1,0:T(8,128)(2,1)S(1)}, s32[8,128]{1,0:T(8,128)S(1)}) custom-call(bf16[1,2,512,512]{3,2,1,0:T(8,128)(2,1)S(1)} %copy-done.2, s32[16]{0:T(128)S(1)} %copy-done.3), custom_call_target="tpu_custom_call" | custom-call | flops 10000000000 | bytes 1000000 | tf_op jit(solution)/shard_map/pallas_call | solution.py:328
  3.5 0.3 collective-permute-start.3
  3.8 3.1 %collective-permute-start = (bf16[256,512]{1,0:T(8,128)(2,1)S(1)}, bf16[256,512]{1,0:T(8,128)(2,1)S(1)}, u32[]{:S(2)}, u32[]{:S(2)}) collective-permute-start(bf16[256,512]{1,0:T(8,128)(2,1)S(1)} %get-tuple-element.29.cross_a_ref), channel_id=1, source_target_pairs={{2,6},{3,7},{4,0},{5,1},{10,14},{11,15},{12,8},{13,9},{18,22},{19,... | collective-permute-start | bytes 786440 | tf_op jit(solution)/shard_map/ppermute | solution.py:295
  6.9 0.0 copy-done
  7.0 2.2 %shard_map.47 = (bf16[512,512]{1,0:T(8,128)(2,1)S(1)}, f32[512,1024]{1,0:T(8,128)S(1)}, f32[512,512]{1,0:T(8,128)S(1)}) custom-call(s32[8,128]{1,0:T(8,128)S(1)} %get-tuple-element.28.bounds_ref, bf16[256,512]{1,0:T(8,128)(2,1)S(1)} %get-tuple-element.29.cross_a_ref, bf16[256,512]{1,0:T(8,128)(2,1)S(1)} %get-tuple-element.30.cross_b_ref, ...), custom_call_target="tpu_custom_call" | custom-call | flops 100000000 | bytes 1000000 | tf_op jit(solution)/shard_map/pallas_call | solution.py:318
  9.2 3.0 %collective-permute-done = bf16[256,512]{1,0:T(8,128)(2,1)S(1)} collective-permute-done((bf16[256,512]{1,0:T(8,128)(2,1)S(1)}, bf16[256,512]{1,0:T(8,128)(2,1)S(1)}, u32[]{:S(2)}, u32[]{:S(2)}) %collective-permute-start) | collective-permute-done | bytes 262176 | tf_op jit(solution)/shard_map/ppermute | solution.py:295
  12.2 0.0 collective-permute-done.4.partner_ref
  12.2 4.7 %shard_map.48 = (bf16[512,512]{1,0:T(8,128)(2,1)S(1)}, f32[512,1024]{1,0:T(8,128)S(1)}, f32[512,512]{1,0:T(8,128)S(1)}, f32[512,1024]{1,0:T(8,128)S(1)}, f32[512,512]{1,0:T(8,128)S(1)}) custom-call(s32[8,128]{1,0:T(8,128)S(1)} %get-tuple-element.28.bounds_ref, bf16[512,512]{1,0:T(8,128)(2,1)S(1)} %get-tuple-element.33.straight_ref, ...), custom_call_target="tpu_custom_call" | custom-call | flops 100000000 | bytes 1000000 | tf_op jit(solution)/shard_map/pallas_call | solution.py:318
  16.9 0.0 collective-permute-done.3.far_ref
  16.9 1.5 %collective-permute-start.5 = (bf16[512,512]{1,0:T(8,128)(2,1)S(1)}, bf16[512,512]{1,0:T(8,128)(2,1)S(1)}, u32[]{:S(2)}, u32[]{:S(2)}) collective-permute-start(bf16[512,512]{1,0:T(8,128)(2,1)S(1)} %collective-permute-done.3.far_ref), channel_id=1, source_target_pairs={{0,1},{1,0},{2,3},{3,2},{4,5},{5,4},{6,7},{7,6},{8,9},{9,8},{10,11... | collective-permute-start | bytes 1572872 | tf_op jit(solution)/shard_map/ppermute | solution.py:295
  18.4 2.9 %collective-permute-start.2 = (bf16[256,512]{1,0:T(8,128)(2,1)S(1)}, bf16[256,512]{1,0:T(8,128)(2,1)S(1)}, u32[]{:S(2)}, u32[]{:S(2)}) collective-permute-start(bf16[256,512]{1,0:T(8,128)(2,1)S(1)} %get-tuple-element.30.cross_b_ref), channel_id=1, source_target_pairs={{2,4},{3,5},{4,2},{5,3},{10,12},{11,13},{12,10},{13,11},{18,20},{1... | collective-permute-start | bytes 786440 | tf_op jit(solution)/shard_map/ppermute | solution.py:295
  21.3 1.3 %collective-permute-start.1 = (bf16[256,512]{1,0:T(8,128)(2,1)S(1)}, bf16[256,512]{1,0:T(8,128)(2,1)S(1)}, u32[]{:S(2)}, u32[]{:S(2)}) collective-permute-start(bf16[256,512]{1,0:T(8,128)(2,1)S(1)} %collective-permute-done), channel_id=1, source_target_pairs={{6,4},{7,5},{0,2},{1,3},{14,12},{15,13},{8,10},{9,11},{22,20},{23,... | collective-permute-start | bytes 786440 | tf_op jit(solution)/shard_map/ppermute | solution.py:295
  22.6 0.0 copy-start.1
  22.6 2.2 %shard_map.49 = (f32[512,1024]{1,0:T(8,128)S(1)}, f32[512,512]{1,0:T(8,128)S(1)}) custom-call(s32[8,128]{1,0:T(8,128)S(1)} %get-tuple-element.28.bounds_ref, bf16[512,512]{1,0:T(8,128)(2,1)S(1)} %collective-permute-done.3.far_ref, bf16[1,2,512,512]{3,2,1,0:T(8,128)(2,1)S(1)} %collective-permute-done.4.partner_ref, bf16[512,1536]{1,0:T(8,128)(2,1)S(1)} %copy-done, ...), custom_call_target="tpu_custom_call" | custom-call | flops 100000000 | bytes 1000000 | tf_op jit(solution)/shard_map/pallas_call | solution.py:318
  24.9 0.0 collective-permute-done.5.near_ref
  24.9 0.0 copy-done.1
  24.9 1.4 %shard_map.50.refs_5_ = bf16[1,2,512,512]{3,2,1,0:T(8,128)(2,1)} custom-call(s32[8,128]{1,0:T(8,128)S(1)} %get-tuple-element.28.bounds_ref, bf16[512,512]{1,0:T(8,128)(2,1)S(1)} %collective-permute-done.5.near_ref, bf16[256,512]{1,0:T(8,128)(2,1)S(1)} %get-tuple-element.29.cross_a_ref, bf16[256,512]{1,0:T(8,128)(2,1)S(1)} %get-tuple-element.30.cross_b_ref, ...), custom_call_target="tpu_custom_call" | custom-call | flops 100000000 | bytes 1000000 | tf_op jit(solution)/shard_map/pallas_call | solution.py:318
  26.3 2.8 %collective-permute-done.2 = bf16[256,512]{1,0:T(8,128)(2,1)S(1)} collective-permute-done((bf16[256,512]{1,0:T(8,128)(2,1)S(1)}, bf16[256,512]{1,0:T(8,128)(2,1)S(1)}, u32[]{:S(2)}, u32[]{:S(2)}) %collective-permute-start.2) | collective-permute-done | bytes 262176 | tf_op jit(solution)/shard_map/ppermute | solution.py:295
  29.0 1.7 %collective-permute-done.1 = bf16[256,512]{1,0:T(8,128)(2,1)S(1)} collective-permute-done((bf16[256,512]{1,0:T(8,128)(2,1)S(1)}, bf16[256,512]{1,0:T(8,128)(2,1)S(1)}, u32[]{:S(2)}, u32[]{:S(2)}) %collective-permute-start.1) | collective-permute-done | bytes 262176 | tf_op jit(solution)/shard_map/ppermute | solution.py:295
  30.8 1.2 %collective-permute-start.6 = (bf16[512,512]{1,0:T(8,128)(2,1)S(1)}, bf16[512,512]{1,0:T(8,128)(2,1)S(1)}, u32[]{:S(2)}, u32[]{:S(2)}) collective-permute-start(bf16[512,512]{1,0:T(8,128)(2,1)S(1)} %constant_dynamic-update-slice_fusion.far_ref), channel_id=1, source_target_pairs={{0,1},{1,0},{2,3},{3,2},{4,5},{5,4},{6,7},{7,6},{8,9},{9,8},{10,11... | collective-permute-start | bytes 1572872 | tf_op jit(solution)/shard_map/ppermute | solution.py:295
  32.1 2.3 %shard_map.51 = (f32[512,1024]{1,0:T(8,128)S(1)}, f32[512,512]{1,0:T(8,128)S(1)}) custom-call(s32[8,128]{1,0:T(8,128)S(1)} %get-tuple-element.28.bounds_ref, bf16[512,512]{1,0:T(8,128)(2,1)S(1)} %constant_dynamic-update-slice_fusion.far_ref, bf16[1,2,512,512]{3,2,1,0:T(8,128)(2,1)S(1)} %collective-permute-done.4.partner_ref, bf16[512,1536]{1,0:T(8,128)(2,1)S(1)} %copy-done, ...), custom_call_target="tpu_custom_call" | custom-call | flops 100000000 | bytes 1000000 | tf_op jit(solution)/shard_map/pallas_call | solution.py:318
  34.3 0.0 collective-permute-done.6.near_ref
  34.3 3.5 %shard_map.52 = bf16[1,2,512,512]{3,2,1,0:T(8,128)(2,1)} custom-call(s32[8,128]{1,0:T(8,128)S(1)} %get-tuple-element.28.bounds_ref, bf16[512,512]{1,0:T(8,128)(2,1)S(1)} %collective-permute-done.6.near_ref, bf16[256,512]{1,0:T(8,128)(2,1)S(1)} %get-tuple-element.29.cross_a_ref, ...), custom_call_target="tpu_custom_call", output_to_operand_aliasing={{}: (9, {})} | custom-call | flops 100000000 | bytes 1000000 | tf_op jit(solution)/shard_map/pallas_call | solution.py:318
  (2 shorter events, 0.0 us)
Async XLA Ops:
  0.0 6.9 %copy-start = (bf16[512,1536]{1,0:T(8,128)(2,1)S(1)}, bf16[512,1536]{1,0:T(8,128)(2,1)}, u32[]{:S(2)}) copy-start(bf16[512,1536]{1,0:T(8,128)(2,1)} %refs_0_.3) | copy-start | bytes 4718596
  0.0 12.2 %collective-permute-start.4 = (bf16[1,2,512,512]{3,2,1,0:T(8,128)(2,1)}, bf16[1,2,512,512]{3,2,1,0:T(8,128)(2,1)S(1)}, u32[]{:S(2)}, u32[]{:S(2)}) collective-permute-start(bf16[1,2,512,512]{3,2,1,0:T(8,128)(2,1)} %frames_ref.1), channel_id=1, source_target_pairs={{0,1},{1,0},{2,3},{3,2},{4,5},{5,4},{6,7},{7,6},{8,9},{9,8},{10,11... | collective-permute-start | bytes 3145736 | tf_op jit(solution)/shard_map/ppermute | solution.py:295
  0.7 1.2 %copy-start.2 = (bf16[1,2,512,512]{3,2,1,0:T(8,128)(2,1)S(1)}, bf16[1,2,512,512]{3,2,1,0:T(8,128)(2,1)}, u32[]{:S(2)}) copy-start(bf16[1,2,512,512]{3,2,1,0:T(8,128)(2,1)} %frames_ref.1) | copy-start | bytes 3145732
  1.9 0.7 %copy-start.3 = (s32[16]{0:T(128)S(1)}, s32[16]{0:T(128)}, u32[]{:S(2)}) copy-start(s32[16]{0:T(128)} %lengths_ref.1) | copy-start | bytes 196
  3.5 13.5 %collective-permute-start.3 = (bf16[512,512]{1,0:T(8,128)(2,1)S(1)}, bf16[512,512]{1,0:T(8,128)(2,1)S(1)}, u32[]{:S(2)}, u32[]{:S(2)}) collective-permute-start(bf16[512,512]{1,0:T(8,128)(2,1)S(1)} %get-tuple-element.33.straight_ref), channel_id=1, source_target_pairs={{0,2},{1,3},{4,6},{5,7},{2,0},{3,1},{6,4},{7,5},{8,10},{9,11},{12,... | collective-permute-start | bytes 1572872 | tf_op jit(solution)/shard_map/ppermute | solution.py:295
  3.8 8.4 %collective-permute-start = (bf16[256,512]{1,0:T(8,128)(2,1)S(1)}, bf16[256,512]{1,0:T(8,128)(2,1)S(1)}, u32[]{:S(2)}, u32[]{:S(2)}) collective-permute-start(bf16[256,512]{1,0:T(8,128)(2,1)S(1)} %get-tuple-element.29.cross_a_ref), channel_id=1, source_target_pairs={{2,6},{3,7},{4,0},{5,1},{10,14},{11,15},{12,8},{13,9},{18,22},{19,... | collective-permute-start | bytes 786440 | tf_op jit(solution)/shard_map/ppermute | solution.py:295
  16.9 7.9 %collective-permute-start.5 = (bf16[512,512]{1,0:T(8,128)(2,1)S(1)}, bf16[512,512]{1,0:T(8,128)(2,1)S(1)}, u32[]{:S(2)}, u32[]{:S(2)}) collective-permute-start(bf16[512,512]{1,0:T(8,128)(2,1)S(1)} %collective-permute-done.3.far_ref), channel_id=1, source_target_pairs={{0,1},{1,0},{2,3},{3,2},{4,5},{5,4},{6,7},{7,6},{8,9},{9,8},{10,11... | collective-permute-start | bytes 1572872 | tf_op jit(solution)/shard_map/ppermute | solution.py:295
  18.4 10.6 %collective-permute-start.2 = (bf16[256,512]{1,0:T(8,128)(2,1)S(1)}, bf16[256,512]{1,0:T(8,128)(2,1)S(1)}, u32[]{:S(2)}, u32[]{:S(2)}) collective-permute-start(bf16[256,512]{1,0:T(8,128)(2,1)S(1)} %get-tuple-element.30.cross_b_ref), channel_id=1, source_target_pairs={{2,4},{3,5},{4,2},{5,3},{10,12},{11,13},{12,10},{13,11},{18,20},{1... | collective-permute-start | bytes 786440 | tf_op jit(solution)/shard_map/ppermute | solution.py:295
  21.3 9.5 %collective-permute-start.1 = (bf16[256,512]{1,0:T(8,128)(2,1)S(1)}, bf16[256,512]{1,0:T(8,128)(2,1)S(1)}, u32[]{:S(2)}, u32[]{:S(2)}) collective-permute-start(bf16[256,512]{1,0:T(8,128)(2,1)S(1)} %collective-permute-done), channel_id=1, source_target_pairs={{6,4},{7,5},{0,2},{1,3},{14,12},{15,13},{8,10},{9,11},{22,20},{23,... | collective-permute-start | bytes 786440 | tf_op jit(solution)/shard_map/ppermute | solution.py:295
  22.6 2.2 %copy-start.1 = (bf16[512,512]{1,0:T(8,128)(2,1)S(1)}, bf16[512,512]{1,0:T(8,128)(2,1)}, u32[]{:S(2)}) copy-start(bf16[512,512]{1,0:T(8,128)(2,1)} %refs_1_.3) | copy-start | bytes 1572868
  30.8 3.5 %collective-permute-start.6 = (bf16[512,512]{1,0:T(8,128)(2,1)S(1)}, bf16[512,512]{1,0:T(8,128)(2,1)S(1)}, u32[]{:S(2)}, u32[]{:S(2)}) collective-permute-start(bf16[512,512]{1,0:T(8,128)(2,1)S(1)} %constant_dynamic-update-slice_fusion.far_ref), channel_id=1, source_target_pairs={{0,1},{1,0},{2,3},{3,2},{4,5},{5,4},{6,7},{7,6},{8,9},{9,8},{10,11... | collective-permute-start | bytes 1572872 | tf_op jit(solution)/shard_map/ppermute | solution.py:295

commit v3 on v2

v3 whole, which is shorter than its diff:
```python
import functools

import jax
import jax.numpy as jnp
from jax import lax
from jax.experimental import pallas as pl
from jax.experimental.pallas import tpu as pltpu
from jax.sharding import PartitionSpec as P


HEADS = 4
HEAD_DIM = 128
LANES = 128
WIDE = HEAD_DIM + LANES
SCALE2 = HEAD_DIM ** (-0.5) * 1.4426950408889634
APART = -1e30
VMEM = pl.BlockSpec(memory_space=pltpu.VMEM)
HBM = pl.BlockSpec(memory_space=pltpu.HBM)
F32 = jnp.float32
BF16 = jnp.bfloat16


def normalize(rows):
    wide = rows.astype(F32)
    factor = lax.rsqrt(jnp.mean(wide * wide, axis=-1, keepdims=True) + 1e-06)
    return (wide * factor).astype(BF16)


def matmul(left, right):
    return jnp.dot(left, right, preferred_element_type=F32)


def where_am_i():
    place = lax.axis_index("ctx")
    return place, lax.rem(place // 2, 2), lax.rem(place, 2)


def block_first(half, place, count, group):
    return jnp.where(half == 0, place, 2 * count - 1 - place) * group


def beside(left, right):
    return jnp.concatenate([left, right], axis=1)


def across(column, width):
    return jnp.concatenate([column] * (width // LANES), axis=1)


def inside(bounds, first, rows):
    position = first + lax.broadcasted_iota(jnp.int32, (rows, LANES), 0)
    return (position >= bounds[0:1, :]) & (position < bounds[1:2, :])


def fill_starts(starts_ref, bounds, first):
    rows = starts_ref.shape[0]
    chosen = jnp.where(inside(bounds, first, rows), bounds[0:1, :], 0)
    start = jnp.sum(chosen.astype(F32), axis=1, keepdims=True).astype(jnp.int32)
    starts_ref[...] = jnp.broadcast_to(start, starts_ref.shape)


def attend(q_ref, starts_ref, kv_ref, key_first, old, tiles):
    rows, width = q_ref.shape
    out = []
    for head in range(HEADS):
        hs = pl.ds(head * HEAD_DIM, HEAD_DIM)
        vs = pl.ds(width + head * HEAD_DIM, HEAD_DIM)
        ws = pl.ds(head * WIDE, WIDE)
        scores, peaks = [], []
        for low, size, top, bottom, causal in tiles:
            tile = lax.dot_general(
                q_ref[pl.ds(top, bottom - top), hs],
                kv_ref[pl.ds(low, size), hs],
                (((1,), (1,)), ((), ())),
                preferred_element_type=F32,
            )
            reach = starts_ref[pl.ds(top, bottom - top), :] - (key_first + low)
            there = lax.broadcasted_iota(jnp.int32, tile.shape, 1)
            allowed = there >= across(reach, size)
            if causal:
                here = lax.broadcasted_iota(jnp.int32, tile.shape, 0)
                allowed = allowed & (there <= here)
            tile = jnp.where(allowed, tile, APART)
            scores.append(tile)
            peak = jnp.max(tile, axis=1, keepdims=True)
            peaks.append(jnp.broadcast_to(peak, (bottom - top, LANES)))
        peak = spread(jnp.maximum, [(p, t[2], t[3]) for p, t in zip(peaks, tiles)], rows)
        if old is not None:
            before = old[1][:, hs]
            peak = jnp.maximum(before, peak)
        mixes = []
        for tile, (low, size, top, bottom, _) in zip(scores, tiles):
            weights = jnp.exp2(tile - across(peak[top:bottom], size)).astype(BF16)
            ones = jnp.ones((size, LANES), BF16)
            mix = matmul(weights, beside(kv_ref[pl.ds(low, size), vs], ones))
            mixes.append((mix, top, bottom))
        mixed = spread(jnp.add, mixes, rows)
        if old is not None:
            mixed = mixed + across(jnp.exp2(before - peak), WIDE) * old[0][:, ws]
        out.append((mixed, peak))
    return out


def spread(combine, items, rows):
    whole = [item for item, top, bottom in items if bottom - top == rows]
    total = whole[0]
    for item, top, bottom in items:
        if bottom - top == rows:
            continue
        pieces = [total[:top]] if top else []
        pieces.append(combine(total[top:bottom], item))
        if bottom < rows:
            pieces.append(total[bottom:])
        total = jnp.concatenate(pieces, axis=0)
    return total


def keep(out, new):
    for head, (mixed, peak) in enumerate(out):
        new[0][:, head * WIDE : (head + 1) * WIDE] = mixed
        new[1][:, head * HEAD_DIM : (head + 1) * HEAD_DIM] = peak


def diagonal(group):
    rows = group // 2
    return ((0, rows, 0, group, True), (rows, rows, rows, group, True))


def full(group):
    return ((0, group, 0, group, False),)


def beyond(group):
    rows = group // 2
    return ((rows, rows, 0, group, False), (0, rows, 0, rows, False))


def gather(parts, block_ref):
    low = 0
    for part in parts:
        block_ref[low : low + part.shape[0], :] = part[...]
        low += part.shape[0]


def prepare_kernel(frames_ref, straight_ref, cross_a_ref, cross_b_ref):
    _, side, _ = where_am_i()
    straight_ref[...] = normalize(frames_ref[0, side])
    rows = cross_a_ref.shape[0]
    cross_a_ref[...] = normalize(frames_ref[0, 1 - side, :rows])
    cross_b_ref[...] = normalize(frames_ref[0, 1 - side, rows:])


def bounds_of(lengths_ref):
    lengths = jnp.broadcast_to(lengths_ref[...], (8, lengths_ref.shape[1]))
    high = (lengths >> 5).astype(F32).astype(BF16)
    rest = (lengths & 31).astype(F32).astype(BF16)
    episode = lax.broadcasted_iota(jnp.int32, (lengths.shape[1], LANES), 0)
    lane = lax.broadcasted_iota(jnp.int32, (lengths.shape[1], LANES), 1)

    def total(chosen):
        picks = jnp.where(chosen, 1.0, 0.0).astype(BF16)
        return (32 * matmul(high, picks) + matmul(rest, picks)).astype(jnp.int32)

    row = lax.broadcasted_iota(jnp.int32, (8, LANES), 0)
    return jnp.where(row == 0, total(episode < lane), total(episode <= lane))


def project_kernel(
    count, lengths_ref, straight_ref, cross_a_ref, cross_b_ref, w_ref,
    q_x_ref, kv_x_ref, q_d_ref, kv_d_ref, give_ref, starts_x_ref, starts_d_ref, block_ref,
):
    place, side, core = where_am_i()
    group, width = block_ref.shape
    gather((cross_a_ref, cross_b_ref), block_ref)
    for normed, q_ref, kv_ref in (
        (block_ref[...], q_x_ref, kv_x_ref), (straight_ref[...], q_d_ref, kv_d_ref)
    ):
        q_ref[...] = (matmul(normed, w_ref[:, :width]) * SCALE2).astype(BF16)
        kv_ref[...] = matmul(normed, w_ref[:, width:]).astype(BF16)
    give_ref[:, 2 * width :] = block_ref[...]

    @pl.when(side == core)
    def _():
        give_ref[:, : 2 * width] = kv_d_ref[...]

    @pl.when(side != core)
    def _():
        give_ref[:, : 2 * width] = kv_x_ref[...]

    bounds = bounds_of(lengths_ref)
    fill_starts(starts_x_ref, bounds, block_first(1 - side, place, count, group))
    fill_starts(starts_d_ref, bounds, block_first(side, place, count, group))


def own_kernel(
    count, starts_x_ref, starts_d_ref, q_x_ref, kv_x_ref, q_d_ref, kv_d_ref,
    acc_x_ref, m_x_ref, acc_d_ref, m_d_ref,
):
    tiles = diagonal(q_x_ref.shape[0])
    place, side, _ = where_am_i()
    group = q_x_ref.shape[0]
    first = block_first(1 - side, place, count, group)
    keep(attend(q_x_ref, starts_x_ref, kv_x_ref, first, None, tiles), (acc_x_ref, m_x_ref))
    first = block_first(side, place, count, group)
    keep(attend(q_d_ref, starts_d_ref, kv_d_ref, first, None, tiles), (acc_d_ref, m_d_ref))


def partner_kernel(
    count, starts_x_ref, starts_d_ref, given_ref, q_x_ref, q_d_ref, acc_x_in, m_x_in, acc_d_in, m_d_in,
    acc_x_ref, m_x_ref, acc_d_ref, m_d_ref,
):
    place, side, core = where_am_i()
    group = q_x_ref.shape[0]
    half = 1 - core
    key_first = block_first(half, place, count, group) - group
    tiles = full(group)

    @pl.when(half == side)
    def _():
        out = attend(q_d_ref, starts_d_ref, given_ref, key_first, (acc_d_in, m_d_in), tiles)
        keep(out, (acc_d_ref, m_d_ref))
        acc_x_ref[...] = acc_x_in[...]
        m_x_ref[...] = m_x_in[...]

    @pl.when(half != side)
    def _():
        out = attend(q_x_ref, starts_x_ref, given_ref, key_first, (acc_x_in, m_x_in), tiles)
        keep(out, (acc_x_ref, m_x_ref))
        acc_d_ref[...] = acc_d_in[...]
        m_d_ref[...] = m_d_in[...]


def far_kernel(
    count, late, starts_ref, far_ref, given_ref, w_ref, q_ref, acc_in, m_in,
    acc_ref, m_ref, kv_ref, block_ref,
):
    place, side, _ = where_am_i()
    half = side if late else 1 - side
    group, width = far_ref.shape
    first = block_first(half, place, count, group)
    block_ref[...] = far_ref[...]
    if late:
        @pl.when(place // 2 == count // 2 - 1)
        def _():
            block_ref[...] = given_ref[:, 2 * width :]

    bare = (place < 2) if late else (place < 0)

    @pl.when(jnp.logical_not(bare))
    def _():
        kv_ref[...] = matmul(block_ref[...], w_ref[:, width:]).astype(BF16)
        out = attend(q_ref, starts_ref, kv_ref, first - 2 * group, (acc_in, m_in), beyond(group))
        keep(out, (acc_ref, m_ref))

    @pl.when(bare)
    def _():
        acc_ref[...] = acc_in[...]
        m_ref[...] = m_in[...]


def near_kernel(count, late, starts_ref, near_ref, cross_a_ref, cross_b_ref, *refs):
    w_ref, w_out_ref, q_ref, acc_in, m_in = refs[:5]
    out_ref, stage_ref, sems, kv_ref, block_ref = refs[-5:]
    place, side, core = where_am_i()
    half = side if late else 1 - side
    group, width = block_ref.shape
    first = block_first(half, place, count, group)
    rows = group // 2

    def emit(wide):
        for row in range(0, group, rows):
            rs = slice(row, row + rows)
            mixed = [(m[rs, :HEAD_DIM] / m[rs, HEAD_DIM:]).astype(BF16) for m in wide]
            out = matmul(jnp.concatenate(mixed, axis=1), w_out_ref[...])
            stage_ref[rs, :] = out.astype(BF16)
            copy_out(row).start()

    def copy_out(row):
        rs = pl.ds(row, rows)
        return pltpu.make_async_copy(
            stage_ref.at[rs], out_ref.at[0, half, rs], sems.at[row // rows]
        )

    wanted = half == core
    if late:
        wanted = wanted & (place >= 2)

    @pl.when(wanted)
    def _():
        block_ref[...] = near_ref[...]
        if late:
            @pl.when(place == count - 1)
            def _():
                gather((cross_a_ref, cross_b_ref), block_ref)

        kv_ref[...] = matmul(block_ref[...], w_ref[:, width:]).astype(BF16)
        out = attend(q_ref, starts_ref, kv_ref, first - group, (acc_in, m_in), full(group))
        emit([mixed for mixed, _ in out])

    @pl.when(jnp.logical_not(wanted))
    def _():
        emit([acc_in[:, h * WIDE : (h + 1) * WIDE] for h in range(HEADS)])

    for row in range(0, group, rows):
        copy_out(row).wait()


def params(mib):
    return pltpu.CompilerParams(vmem_limit_bytes=mib * 1024 * 1024)


def local(frames, episode_lengths, w_qkv, w_out):
    width = w_out.shape[0]
    group = frames.shape[2]
    count = lax.axis_size("ctx")
    chips = count // 2
    pair = [(i, i ^ 1) for i in range(count)]

    def route(links):
        return [(2 * a + c, 2 * b + c) for a, b in links for c in range(2)]

    even = [(c, c + 1) for c in range(0, chips - 1, 2)]
    odd = [(c, c + 1) for c in range(1, chips - 1, 2)]
    swap_x = route(even + [(b, a) for a, b in even])
    swap_d = route(odd + [(b, a) for a, b in odd])
    relay_out = route([(a, b + 1) for a, b in odd] + [(b, a - 1) for a, b in odd])
    relay_in = route([(b + 1, b) for a, b in odd] + [(a - 1, a) for a, b in odd])

    def send(block, links):
        return lax.ppermute(block, "ctx", links)

    def shape(*dims, dtype=BF16):
        return jax.ShapeDtypeStruct(dims, dtype)

    block = shape(group, width)
    part = shape(group // 2, width)
    kv_type = shape(group, 2 * width)
    state = (shape(group, HEADS * WIDE, dtype=F32), shape(group, width, dtype=F32))
    kv_scratch = [pltpu.VMEM((group, 2 * width), BF16), pltpu.VMEM((group, width), BF16)]

    def call(kernel, outs, operands, scratch=(), aliased=None):
        specs = [VMEM] * len(operands)
        options = dict(out_specs=(VMEM,) * len(outs), scratch_shapes=list(scratch))
        if aliased is not None:
            options["out_specs"] = (HBM,)
            options["scratch_shapes"] = [
                pltpu.VMEM((group, width), BF16), pltpu.SemaphoreType.DMA((2,)),
            ] + list(scratch)
        if aliased:
            specs.append(HBM)
            options["input_output_aliases"] = {len(operands): 0}
            operands = operands + aliased
        return pl.pallas_call(
            kernel,
            out_shape=outs,
            in_specs=specs,
            compiler_params=params(14),
            cost_estimate=pl.CostEstimate(flops=10**8, bytes_accessed=10**6, transcendentals=0),
            **options,
        )(*operands)

    straight, cross_a, cross_b = pl.pallas_call(
        prepare_kernel,
        out_shape=(block, part, part),
        in_specs=[VMEM],
        out_specs=(VMEM,) * 3,
        compiler_params=params(4),
        cost_estimate=pl.CostEstimate(flops=10**10, bytes_accessed=10**6, transcendentals=0),
    )(frames)
    x_in = send(straight, swap_x)
    hop_in = send(cross_a, relay_out)
    bind = functools.partial
    lengths = episode_lengths.reshape(1, -1)
    starts_type = shape(group, LANES, dtype=jnp.int32)
    q_x, kv_x, q_d, kv_d, give, starts_x, starts_d = call(
        bind(project_kernel, count),
        (block, kv_type, block, kv_type, shape(group, 3 * width), starts_type, starts_type),
        (lengths, straight, cross_a, cross_b, w_qkv), kv_scratch[1:],
    )
    d_in = send(cross_b, swap_d)
    given = send(give, pair)
    acc_x, m_x, acc_d, m_d = call(
        bind(own_kernel, count), state + state,
        (starts_x, starts_d, q_x, kv_x, q_d, kv_d),
    )
    hop_in, acc_x = lax.optimization_barrier((hop_in, acc_x))
    r_in = send(hop_in, relay_in)
    acc_x, m_x, acc_d, m_d = call(
        bind(partner_kernel, count), state + state,
        (starts_x, starts_d, given, q_x, q_d, acc_x, m_x, acc_d, m_d),
    )
    x_in, acc_d = lax.optimization_barrier((x_in, acc_d))
    near_x = send(x_in, pair)
    acc_x, m_x = call(
        bind(far_kernel, count, False), state,
        (starts_x, x_in, given, w_qkv, q_x, acc_x, m_x), kv_scratch,
    )
    whole = (jax.ShapeDtypeStruct(frames.shape, BF16),)
    (out,) = call(
        bind(near_kernel, count, False), whole,
        (starts_x, near_x, cross_a, cross_b, w_qkv, w_out, q_x, acc_x, m_x), kv_scratch, (),
    )
    r_in, d_in, out = lax.optimization_barrier((r_in, d_in, out))
    d_block = jnp.concatenate([r_in, d_in], axis=0)
    near_d = send(d_block, pair)
    acc_d, m_d = call(
        bind(far_kernel, count, True), state,
        (starts_d, d_block, given, w_qkv, q_d, acc_d, m_d), kv_scratch,
    )
    (out,) = call(
        bind(near_kernel, count, True), whole,
        (starts_d, near_d, cross_a, cross_b, w_qkv, w_out, q_d, acc_d, m_d), kv_scratch, (out,),
    )
    return out


def solution(mesh):
    in_specs = (P(("dp", "ctx"), None, None, None), P("dp"), P(), P())
    out_specs = P(("dp", "ctx"), None, None, None)
    return jax.shard_map(local, mesh=mesh, in_specs=in_specs, out_specs=out_specs, check_vma=False)
```

time: 38.2 us -> 38.8 us (1.016)
  waiting for transfers between devices: 7.52 us -> 10.4 us
  Pallas kernels: 17.2 us -> 15.8 us
  local copies, waits for them, and re-layouts: 1.93 us -> 1.42 us
    ppermute x7, waiting for transfers between devices: 7.52 us -> 10.4 us  [send(): return lax.ppermute(block, 'ctx', links)]
    pallas_call x6 -> x7, Pallas kernels: 16.3 us -> 15.5 us  [call(): pl.pallas_call(kernel, out_shape=outs, in_specs=specs, compiler_params=pa...]
    pallas_call x1, Pallas kernels: 0.9 us -> 0.35 us  [local(): pl.pallas_call(prepare_kernel, out_shape=(block, part, part), in_specs=[V...]
    unnamed x9, local copies, waits for them, and re-layouts: 1.91 us -> 1.4 us
  transfers between devices with their start and end apart: 7 -> 7, of which waited for: 3 -> 4; matrix products, arithmetic and copies ran while one was open for 0% -> 0% of each run, Pallas kernels for 36% -> 25%
where the time goes in v3:
time: 38.8 us; the launch traced here: 38.6 us
  Pallas kernels  15.8 us (41%)
  starting transfers between devices  10.7 us (28%)
  waiting for transfers between devices  10.4 us (27%)
  local copies, waits for them, and re-layouts  1.42 us (4%)
    pallas_call x7, Pallas kernels, call(): pl.pallas_call(kernel, out_shape=outs, in_specs=specs, compiler_params=pa...  15.5 us
    ppermute x7, starting transfers between devices, send(): return lax.ppermute(block, 'ctx', links)  10.7 us
    ppermute x7, waiting for transfers between devices, send(): return lax.ppermute(block, 'ctx', links)  10.4 us
    unnamed x9, local copies, waits for them, and re-layouts  1.4 us
  transfers between devices with their start and end apart: 7, of which 4 were waited for; matrix products, arithmetic and copies ran while one was open for 0% of the time, Pallas kernels for 25%

profile of v3, /device:TPU:19, one launch (start us, length us, event | category | flops | bytes accessed | tf_op | source)
XLA Modules:
  0.0 38.6 jit_solution(8709537521691806046)
XLA Ops:
  0.0 0.0 copy-start.2
  0.0 0.0 copy-start
  0.0 0.0 copy-start.3
  0.0 1.3 %copy-done.3 = bf16[1,2,512,512]{3,2,1,0:T(8,128)(2,1)S(1)} copy-done((bf16[1,2,512,512]{3,2,1,0:T(8,128)(2,1)S(1)}, bf16[1,2,512,512]{3,2,1,0:T(8,128)(2,1)}, u32[]{:S(2)}) %copy-start.3) | copy-done | bytes 1048600
  1.3 0.4 shard_map.46
  1.7 0.0 copy-done.2
  1.7 0.0 copy-done
  1.7 2.2 %shard_map.47 = (bf16[512,512]{1,0:T(8,128)(2,1)S(1)}, bf16[512,1024]{1,0:T(8,128)(2,1)S(1)}, bf16[512,512]{1,0:T(8,128)(2,1)S(1)}, bf16[512,1024]{1,0:T(8,128)(...) custom-call(s32[1,16]{1,0:T(1,128)S(1)} %bitcast.1, ...), custom_call_target="tpu_custom_call" | custom-call | flops 100000000 | bytes 1000000 | tf_op jit(solution)/shard_map/pallas_call | solution.py:353
  3.9 0.8 %collective-permute-start.4 = (bf16[512,1536]{1,0:T(8,128)(2,1)S(1)}, bf16[512,1536]{1,0:T(8,128)(2,1)S(1)}, u32[]{:S(2)}, u32[]{:S(2)}) collective-permute-start(bf16[512,1536]{1,0:T(8,128)(2,1)S(1)} %get-tuple-element.45), channel_id=1, source_target_pairs={{0,1},{1,0},{2,3},{3,2},{4,5},{5,4},{6,7},{7,6},{8,9},{9,8},{10,11... | collective-permute-start | bytes 4718600 | tf_op jit(solution)/shard_map/ppermute | solution.py:330
  4.7 0.2 collective-permute-start.3
  4.9 3.1 %collective-permute-start = (bf16[256,512]{1,0:T(8,128)(2,1)S(1)}, bf16[256,512]{1,0:T(8,128)(2,1)S(1)}, u32[]{:S(2)}, u32[]{:S(2)}) collective-permute-start(bf16[256,512]{1,0:T(8,128)(2,1)S(1)} %get-tuple-element.35.cross_a_ref), channel_id=1, source_target_pairs={{2,6},{3,7},{4,0},{5,1},{10,14},{11,15},{12,8},{13,9},{18,22},{19,... | collective-permute-start | bytes 786440 | tf_op jit(solution)/shard_map/ppermute | solution.py:330
  8.1 2.2 %shard_map.48 = (f32[512,1024]{1,0:T(8,128)S(1)}, f32[512,512]{1,0:T(8,128)S(1)}, f32[512,1024]{1,0:T(8,128)S(1)}, f32[512,512]{1,0:T(8,128)S(1)}) custom-call(s32[512,128]{1,0:T(8,128)S(1)} %get-tuple-element.38.starts_x_ref.starts_ref, s32[512,128]{1,0:T(8,128)S(1)} %get-tuple-element.37.starts_d_ref.starts_ref, ...), custom_call_target="tpu_custom_call" | custom-call | flops 100000000 | bytes 1000000 | tf_op jit(solution)/shard_map/pallas_call | solution.py:353
  10.3 3.0 %collective-permute-done = bf16[256,512]{1,0:T(8,128)(2,1)S(1)} collective-permute-done((bf16[256,512]{1,0:T(8,128)(2,1)S(1)}, bf16[256,512]{1,0:T(8,128)(2,1)S(1)}, u32[]{:S(2)}, u32[]{:S(2)}) %collective-permute-start) | collective-permute-done | bytes 262176 | tf_op jit(solution)/shard_map/ppermute | solution.py:330
  13.3 0.0 collective-permute-done.4.given_ref
  13.4 2.0 %shard_map.49 = (f32[512,1024]{1,0:T(8,128)S(1)}, f32[512,512]{1,0:T(8,128)S(1)}, f32[512,1024]{1,0:T(8,128)S(1)}, f32[512,512]{1,0:T(8,128)S(1)}) custom-call(s32[512,128]{1,0:T(8,128)S(1)} %get-tuple-element.38.starts_x_ref.starts_ref, s32[512,128]{1,0:T(8,128)S(1)} %get-tuple-element.37.starts_d_ref.starts_ref, ...), custom_call_target="tpu_custom_call" | custom-call | flops 100000000 | bytes 1000000 | tf_op jit(solution)/shard_map/pallas_call | solution.py:353
  15.3 2.8 %collective-permute-done.3.far_ref = bf16[512,512]{1,0:T(8,128)(2,1)S(1)} collective-permute-done((bf16[512,512]{1,0:T(8,128)(2,1)S(1)}, bf16[512,512]{1,0:T(8,128)(2,1)S(1)}, u32[]{:S(2)}, u32[]{:S(2)}) %collective-permute-start.3) | collective-permute-done | bytes 524320 | tf_op jit(solution)/shard_map/ppermute | solution.py:330
  18.1 0.9 %collective-permute-start.5 = (bf16[512,512]{1,0:T(8,128)(2,1)S(1)}, bf16[512,512]{1,0:T(8,128)(2,1)S(1)}, u32[]{:S(2)}, u32[]{:S(2)}) collective-permute-start(bf16[512,512]{1,0:T(8,128)(2,1)S(1)} %collective-permute-done.3.far_ref), channel_id=1, source_target_pairs={{0,1},{1,0},{2,3},{3,2},{4,5},{5,4},{6,7},{7,6},{8,9},{9,8},{10,11... | collective-permute-start | bytes 1572872 | tf_op jit(solution)/shard_map/ppermute | solution.py:330
  19.0 3.1 %collective-permute-start.2 = (bf16[256,512]{1,0:T(8,128)(2,1)S(1)}, bf16[256,512]{1,0:T(8,128)(2,1)S(1)}, u32[]{:S(2)}, u32[]{:S(2)}) collective-permute-start(bf16[256,512]{1,0:T(8,128)(2,1)S(1)} %get-tuple-element.36.cross_b_ref), channel_id=1, source_target_pairs={{2,4},{3,5},{4,2},{5,3},{10,12},{11,13},{12,10},{13,11},{18,20},{1... | collective-permute-start | bytes 786440 | tf_op jit(solution)/shard_map/ppermute | solution.py:330
  22.1 1.3 %collective-permute-start.1 = (bf16[256,512]{1,0:T(8,128)(2,1)S(1)}, bf16[256,512]{1,0:T(8,128)(2,1)S(1)}, u32[]{:S(2)}, u32[]{:S(2)}) collective-permute-start(bf16[256,512]{1,0:T(8,128)(2,1)S(1)} %collective-permute-done), channel_id=1, source_target_pairs={{6,4},{7,5},{0,2},{1,3},{14,12},{15,13},{8,10},{9,11},{22,20},{23,... | collective-permute-start | bytes 786440 | tf_op jit(solution)/shard_map/ppermute | solution.py:330
  23.4 0.0 copy-start.1
  23.4 2.1 %shard_map.50 = (f32[512,1024]{1,0:T(8,128)S(1)}, f32[512,512]{1,0:T(8,128)S(1)}) custom-call(s32[512,128]{1,0:T(8,128)S(1)} %get-tuple-element.38.starts_x_ref.starts_ref, bf16[512,512]{1,0:T(8,128)(2,1)S(1)} %collective-permute-done.3.far_ref, bf16[512,1536]{1,0:T(8,128)(2,1)S(1)} %collective-permute-done.4.given_ref, bf16[512,1536]{1,0:T(8,128)(2,1)S(1)} %copy-done, ...), custom_call_target="tpu_custom_call" | custom-call | flops 100000000 | bytes 1000000 | tf_op jit(solution)/shard_map/pallas_call | solution.py:353
  25.5 0.0 collective-permute-done.5.near_ref
  25.6 0.0 copy-done.1
  25.6 1.4 %shard_map.51.refs_5_ = bf16[1,2,512,512]{3,2,1,0:T(8,128)(2,1)} custom-call(s32[512,128]{1,0:T(8,128)S(1)} %get-tuple-element.38.starts_x_ref.starts_ref, bf16[512,512]{1,0:T(8,128)(2,1)S(1)} %collective-permute-done.5.near_ref, bf16[256,512]{1,0:T(8,128)(2,1)S(1)} %get-tuple-element.35.cross_a_ref, bf16[256,512]{1,0:T(8,128)(2,1)S(1)} %get-tuple-element.36.cross_b_ref, ...), custom_call_target="tpu_custom_call" | custom-call | flops 100000000 | bytes 1000000 | tf_op jit(solution)/shard_map/pallas_call | solution.py:353
  27.0 2.7 %collective-permute-done.2 = bf16[256,512]{1,0:T(8,128)(2,1)S(1)} collective-permute-done((bf16[256,512]{1,0:T(8,128)(2,1)S(1)}, bf16[256,512]{1,0:T(8,128)(2,1)S(1)}, u32[]{:S(2)}, u32[]{:S(2)}) %collective-permute-start.2) | collective-permute-done | bytes 262176 | tf_op jit(solution)/shard_map/ppermute | solution.py:330
  29.7 1.9 %collective-permute-done.1 = bf16[256,512]{1,0:T(8,128)(2,1)S(1)} collective-permute-done((bf16[256,512]{1,0:T(8,128)(2,1)S(1)}, bf16[256,512]{1,0:T(8,128)(2,1)S(1)}, u32[]{:S(2)}, u32[]{:S(2)}) %collective-permute-start.1) | collective-permute-done | bytes 262176 | tf_op jit(solution)/shard_map/ppermute | solution.py:330
  31.6 1.2 %collective-permute-start.6 = (bf16[512,512]{1,0:T(8,128)(2,1)S(1)}, bf16[512,512]{1,0:T(8,128)(2,1)S(1)}, u32[]{:S(2)}, u32[]{:S(2)}) collective-permute-start(bf16[512,512]{1,0:T(8,128)(2,1)S(1)} %constant_dynamic-update-slice_fusion.far_ref), channel_id=1, source_target_pairs={{0,1},{1,0},{2,3},{3,2},{4,5},{5,4},{6,7},{7,6},{8,9},{9,8},{10,11... | collective-permute-start | bytes 1572872 | tf_op jit(solution)/shard_map/ppermute | solution.py:330
  32.9 2.1 %shard_map.52 = (f32[512,1024]{1,0:T(8,128)S(1)}, f32[512,512]{1,0:T(8,128)S(1)}) custom-call(s32[512,128]{1,0:T(8,128)S(1)} %get-tuple-element.37.starts_d_ref.starts_ref, bf16[512,512]{1,0:T(8,128)(2,1)S(1)} %constant_dynamic-update-slice_fusion.far_ref, bf16[512,1536]{1,0:T(8,128)(2,1)S(1)} %collective-permute-done.4.given_ref, ...), custom_call_target="tpu_custom_call" | custom-call | flops 100000000 | bytes 1000000 | tf_op jit(solution)/shard_map/pallas_call | solution.py:353
  35.0 0.0 collective-permute-done.6.near_ref
  35.0 3.5 %shard_map.53 = bf16[1,2,512,512]{3,2,1,0:T(8,128)(2,1)} custom-call(s32[512,128]{1,0:T(8,128)S(1)} %get-tuple-element.37.starts_d_ref.starts_ref, bf16[512,512]{1,0:T(8,128)(2,1)S(1)} %collective-permute-done.6.near_ref, bf16[256,512]{1,0:T(8,128)(2,1)S(1)} %get-tuple-element.35.cross_a_ref, ...), custom_call_target="tpu_custom_call", output_to_operand_aliasing={{}: (9, {})} | custom-call | flops 100000000 | bytes 1000000 | tf_op jit(solution)/shard_map/pallas_call | solution.py:353
  (2 shorter events, 0.0 us)
Async XLA Ops:
  0.0 1.7 %copy-start.2 = (s32[16]{0:T(128)S(1)}, s32[16]{0:T(128)}, u32[]{:S(2)}) copy-start(s32[16]{0:T(128)} %param.5) | copy-start | bytes 196
  0.0 1.7 %copy-start = (bf16[512,1536]{1,0:T(8,128)(2,1)S(1)}, bf16[512,1536]{1,0:T(8,128)(2,1)}, u32[]{:S(2)}) copy-start(bf16[512,1536]{1,0:T(8,128)(2,1)} %refs_0_.3) | copy-start | bytes 4718596
  0.0 1.3 %copy-start.3 = (bf16[1,2,512,512]{3,2,1,0:T(8,128)(2,1)S(1)}, bf16[1,2,512,512]{3,2,1,0:T(8,128)(2,1)}, u32[]{:S(2)}) copy-start(bf16[1,2,512,512]{3,2,1,0:T(8,128)(2,1)} %frames_ref.1) | copy-start | bytes 3145732
  3.9 9.4 %collective-permute-start.4 = (bf16[512,1536]{1,0:T(8,128)(2,1)S(1)}, bf16[512,1536]{1,0:T(8,128)(2,1)S(1)}, u32[]{:S(2)}, u32[]{:S(2)}) collective-permute-start(bf16[512,1536]{1,0:T(8,128)(2,1)S(1)} %get-tuple-element.45), channel_id=1, source_target_pairs={{0,1},{1,0},{2,3},{3,2},{4,5},{5,4},{6,7},{7,6},{8,9},{9,8},{10,11... | collective-permute-start | bytes 4718600 | tf_op jit(solution)/shard_map/ppermute | solution.py:330
  4.7 13.4 %collective-permute-start.3 = (bf16[512,512]{1,0:T(8,128)(2,1)S(1)}, bf16[512,512]{1,0:T(8,128)(2,1)S(1)}, u32[]{:S(2)}, u32[]{:S(2)}) collective-permute-start(bf16[512,512]{1,0:T(8,128)(2,1)S(1)} %get-tuple-element.34.straight_ref), channel_id=1, source_target_pairs={{0,2},{1,3},{4,6},{5,7},{2,0},{3,1},{6,4},{7,5},{8,10},{9,11},{12,... | collective-permute-start | bytes 1572872 | tf_op jit(solution)/shard_map/ppermute | solution.py:330
  4.9 8.4 %collective-permute-start = (bf16[256,512]{1,0:T(8,128)(2,1)S(1)}, bf16[256,512]{1,0:T(8,128)(2,1)S(1)}, u32[]{:S(2)}, u32[]{:S(2)}) collective-permute-start(bf16[256,512]{1,0:T(8,128)(2,1)S(1)} %get-tuple-element.35.cross_a_ref), channel_id=1, source_target_pairs={{2,6},{3,7},{4,0},{5,1},{10,14},{11,15},{12,8},{13,9},{18,22},{19,... | collective-permute-start | bytes 786440 | tf_op jit(solution)/shard_map/ppermute | solution.py:330
  18.1 7.5 %collective-permute-start.5 = (bf16[512,512]{1,0:T(8,128)(2,1)S(1)}, bf16[512,512]{1,0:T(8,128)(2,1)S(1)}, u32[]{:S(2)}, u32[]{:S(2)}) collective-permute-start(bf16[512,512]{1,0:T(8,128)(2,1)S(1)} %collective-permute-done.3.far_ref), channel_id=1, source_target_pairs={{0,1},{1,0},{2,3},{3,2},{4,5},{5,4},{6,7},{7,6},{8,9},{9,8},{10,11... | collective-permute-start | bytes 1572872 | tf_op jit(solution)/shard_map/ppermute | solution.py:330
  19.0 10.6 %collective-permute-start.2 = (bf16[256,512]{1,0:T(8,128)(2,1)S(1)}, bf16[256,512]{1,0:T(8,128)(2,1)S(1)}, u32[]{:S(2)}, u32[]{:S(2)}) collective-permute-start(bf16[256,512]{1,0:T(8,128)(2,1)S(1)} %get-tuple-element.36.cross_b_ref), channel_id=1, source_target_pairs={{2,4},{3,5},{4,2},{5,3},{10,12},{11,13},{12,10},{13,11},{18,20},{1... | collective-permute-start | bytes 786440 | tf_op jit(solution)/shard_map/ppermute | solution.py:330
  22.1 9.5 %collective-permute-start.1 = (bf16[256,512]{1,0:T(8,128)(2,1)S(1)}, bf16[256,512]{1,0:T(8,128)(2,1)S(1)}, u32[]{:S(2)}, u32[]{:S(2)}) collective-permute-start(bf16[256,512]{1,0:T(8,128)(2,1)S(1)} %collective-permute-done), channel_id=1, source_target_pairs={{6,4},{7,5},{0,2},{1,3},{14,12},{15,13},{8,10},{9,11},{22,20},{23,... | collective-permute-start | bytes 786440 | tf_op jit(solution)/shard_map/ppermute | solution.py:330
  23.4 2.1 %copy-start.1 = (bf16[512,512]{1,0:T(8,128)(2,1)S(1)}, bf16[512,512]{1,0:T(8,128)(2,1)}, u32[]{:S(2)}) copy-start(bf16[512,512]{1,0:T(8,128)(2,1)} %refs_1_.3) | copy-start | bytes 1572868
  31.6 3.3 %collective-permute-start.6 = (bf16[512,512]{1,0:T(8,128)(2,1)S(1)}, bf16[512,512]{1,0:T(8,128)(2,1)S(1)}, u32[]{:S(2)}, u32[]{:S(2)}) collective-permute-start(bf16[512,512]{1,0:T(8,128)(2,1)S(1)} %constant_dynamic-update-slice_fusion.far_ref), channel_id=1, source_target_pairs={{0,1},{1,0},{2,3},{3,2},{4,5},{5,4},{6,7},{7,6},{8,9},{9,8},{10,11... | collective-permute-start | bytes 1572872 | tf_op jit(solution)/shard_map/ppermute | solution.py:330

commit v4 on v3

v4 whole, which is shorter than its diff:
```python
import functools

import jax
import jax.numpy as jnp
from jax import lax
from jax.experimental import pallas as pl
from jax.experimental.pallas import tpu as pltpu
from jax.sharding import PartitionSpec as P


HEADS = 4
HEAD_DIM = 128
LANES = 128
WIDE = HEAD_DIM + LANES
SCALE2 = HEAD_DIM ** (-0.5) * 1.4426950408889634
APART = -1e30
VMEM = pl.BlockSpec(memory_space=pltpu.VMEM)
HBM = pl.BlockSpec(memory_space=pltpu.HBM)
F32 = jnp.float32
BF16 = jnp.bfloat16


def normalize(rows):
    wide = rows.astype(F32)
    factor = lax.rsqrt(jnp.mean(wide * wide, axis=-1, keepdims=True) + 1e-06)
    return (wide * factor).astype(BF16)


def matmul(left, right):
    return jnp.dot(left, right, preferred_element_type=F32)


def where_am_i():
    place = lax.axis_index("ctx")
    return place, lax.rem(place // 2, 2), lax.rem(place, 2)


def block_first(half, place, count, group):
    return jnp.where(half == 0, place, 2 * count - 1 - place) * group


def beside(left, right):
    return jnp.concatenate([left, right], axis=1)


def across(column, width):
    return jnp.concatenate([column] * (width // LANES), axis=1)


def inside(bounds, first, rows):
    position = first + lax.broadcasted_iota(jnp.int32, (rows, LANES), 0)
    return (position >= bounds[0:1, :]) & (position < bounds[1:2, :])


def fill_starts(starts_ref, bounds, first):
    rows = starts_ref.shape[0]
    chosen = jnp.where(inside(bounds, first, rows), bounds[0:1, :], 0)
    start = jnp.sum(chosen.astype(F32), axis=1, keepdims=True).astype(jnp.int32)
    starts_ref[...] = jnp.broadcast_to(start, starts_ref.shape)


def attend(q_ref, starts_ref, old, tiles, heads=range(HEADS)):
    rows, width = q_ref.shape
    out = []
    for head in heads:
        hs = pl.ds(head * HEAD_DIM, HEAD_DIM)
        vs = pl.ds(width + head * HEAD_DIM, HEAD_DIM)
        ws = pl.ds(head * WIDE, WIDE)
        scores, peaks = [], []
        for kv_ref, key_first, low, size, top, bottom, causal in tiles:
            tile = lax.dot_general(
                q_ref[pl.ds(top, bottom - top), hs],
                kv_ref[pl.ds(low, size), hs],
                (((1,), (1,)), ((), ())),
                preferred_element_type=F32,
            )
            reach = starts_ref[pl.ds(top, bottom - top), :] - (key_first + low)
            there = lax.broadcasted_iota(jnp.int32, tile.shape, 1)
            allowed = there >= across(reach, size)
            if causal:
                here = lax.broadcasted_iota(jnp.int32, tile.shape, 0)
                allowed = allowed & (there <= here)
            tile = jnp.where(allowed, tile, APART)
            scores.append(tile)
            peak = jnp.max(tile, axis=1, keepdims=True)
            peaks.append((jnp.broadcast_to(peak, (bottom - top, LANES)), top, bottom))
        peak = spread(jnp.maximum, peaks, rows)
        if old is not None:
            before = old[1][:, hs]
            peak = jnp.maximum(before, peak)
        mixes = []
        for tile, (kv_ref, _, low, size, top, bottom, _) in zip(scores, tiles):
            weights = jnp.exp2(tile - across(peak[top:bottom], size)).astype(BF16)
            ones = jnp.ones((size, LANES), BF16)
            mix = matmul(weights, beside(kv_ref[pl.ds(low, size), vs], ones))
            mixes.append((mix, top, bottom))
        mixed = spread(jnp.add, mixes, rows)
        if old is not None:
            mixed = mixed + across(jnp.exp2(before - peak), WIDE) * old[0][:, ws]
        out.append((mixed, peak))
    return out


def spread(combine, items, rows):
    whole = [item for item, top, bottom in items if bottom - top == rows]
    total = functools.reduce(combine, whole)
    for item, top, bottom in items:
        if bottom - top == rows:
            continue
        pieces = [total[:top]] if top else []
        pieces.append(combine(total[top:bottom], item))
        if bottom < rows:
            pieces.append(total[bottom:])
        total = jnp.concatenate(pieces, axis=0)
    return total


def keep(out, acc_ref, m_ref):
    for head, (mixed, peak) in enumerate(out):
        acc_ref[:, head * WIDE : (head + 1) * WIDE] = mixed
        m_ref[:, head * HEAD_DIM : (head + 1) * HEAD_DIM] = peak


def own_tiles(kv_ref, first):
    group = kv_ref.shape[0]
    rows = group // 2
    return [
        (kv_ref, first, 0, rows, 0, group, True),
        (kv_ref, first, rows, rows, rows, group, True),
    ]


def near_tiles(kv_ref, first):
    group = kv_ref.shape[0]
    return [(kv_ref, first - group, 0, group, 0, group, False)]


def far_tiles(kv_ref, first):
    group = kv_ref.shape[0]
    rows = group // 2
    return [
        (kv_ref, first - 2 * group, rows, rows, 0, group, False),
        (kv_ref, first - 2 * group, 0, rows, 0, rows, False),
    ]


def prepare_kernel(frames_ref, straight_ref, cross_a_ref, cross_b_ref):
    _, side, _ = where_am_i()
    straight_ref[...] = normalize(frames_ref[0, side])
    rows = cross_a_ref.shape[0]
    cross_a_ref[...] = normalize(frames_ref[0, 1 - side, :rows])
    cross_b_ref[...] = normalize(frames_ref[0, 1 - side, rows:])


def bounds_of(lengths_ref):
    lengths = jnp.broadcast_to(lengths_ref[...], (8, lengths_ref.shape[1]))
    high = (lengths >> 5).astype(F32).astype(BF16)
    rest = (lengths & 31).astype(F32).astype(BF16)
    episode = lax.broadcasted_iota(jnp.int32, (lengths.shape[1], LANES), 0)
    lane = lax.broadcasted_iota(jnp.int32, (lengths.shape[1], LANES), 1)

    def total(chosen):
        picks = jnp.where(chosen, 1.0, 0.0).astype(BF16)
        return (32 * matmul(high, picks) + matmul(rest, picks)).astype(jnp.int32)

    row = lax.broadcasted_iota(jnp.int32, (8, LANES), 0)
    return jnp.where(row == 0, total(episode < lane), total(episode <= lane))


def project_kernel(
    count, lengths_ref, straight_ref, cross_a_ref, cross_b_ref, w_ref,
    q_ref, give_ref, kv_ref, starts_ref, blocks_ref,
):
    place, side, core = where_am_i()
    _, group, width = blocks_ref.shape
    rows = cross_a_ref.shape[0]
    blocks_ref[side] = straight_ref[...]
    blocks_ref[1 - side, :rows] = cross_a_ref[...]
    blocks_ref[1 - side, rows:] = cross_b_ref[...]
    for half, pair_ref in ((core, give_ref), (1 - core, kv_ref)):
        normed = blocks_ref[half]
        pair_ref[...] = matmul(normed, w_ref[:, width:]).astype(BF16)
        q_ref[half] = (matmul(normed, w_ref[:, :width]) * SCALE2).astype(BF16)
    bounds = bounds_of(lengths_ref)
    for half in range(2):
        fill_starts(starts_ref.at[half], bounds, block_first(half, place, count, group))


def base_kernel(count, starts_ref, q_ref, give_ref, kv_ref, given_ref, acc_ref, m_ref):
    place, _, core = where_am_i()
    group = give_ref.shape[0]
    first = block_first(1 - core, place, count, group)
    tiles = own_tiles(kv_ref, first) + near_tiles(given_ref, first)
    out = attend(q_ref.at[1 - core], starts_ref.at[1 - core], None, tiles)
    keep(out, acc_ref.at[1 - core], m_ref.at[1 - core])
    first = block_first(core, place, count, group)
    out = attend(q_ref.at[core], starts_ref.at[core], None, own_tiles(give_ref, first))
    keep(out, acc_ref.at[core], m_ref.at[core])


def emitter(half, w_out_ref, out_ref, stage_ref, sems):
    group = stage_ref.shape[0]
    rows = group // 2

    def copy_out(row):
        rs = pl.ds(row, rows)
        return pltpu.make_async_copy(
            stage_ref.at[rs], out_ref.at[0, half, rs], sems.at[row // rows]
        )

    def emit(wide):
        for row in range(0, group, rows):
            rs = slice(row, row + rows)
            mixed = [(m[rs, :HEAD_DIM] / m[rs, HEAD_DIM:]).astype(BF16) for m in wide]
            out = matmul(jnp.concatenate(mixed, axis=1), w_out_ref[...])
            stage_ref[rs, :] = out.astype(BF16)
            copy_out(row).start()

    def settle():
        for row in range(0, group, rows):
            copy_out(row).wait()

    return emit, settle


def heads_of(acc_ref):
    return [acc_ref[:, h * WIDE : (h + 1) * WIDE] for h in range(HEADS)]


def merge_kernel(count, r_ref, d_ref, cross_a_ref, cross_b_ref, block_ref):
    place, _, _ = where_am_i()
    rows = r_ref.shape[0]
    at_end = place // 2 == count // 2 - 1

    @pl.when(at_end)
    def _():
        block_ref[:rows] = cross_a_ref[...]
        block_ref[rows:] = cross_b_ref[...]

    @pl.when(jnp.logical_not(at_end))
    def _():
        block_ref[:rows] = r_ref[...]
        block_ref[rows:] = d_ref[...]


def far_kernel(
    count, late, starts_ref, far_ref, given_ref, w_ref, w_out_ref, q_ref, acc_in, m_in, *refs
):
    acc_ref, m_ref, out_ref, stage_ref, sems, kv_ref = refs[-6:]
    place, side, core = where_am_i()
    half = side if late else 1 - side
    group, width = far_ref.shape
    first = block_first(half, place, count, group)
    emit, settle = emitter(half, w_out_ref, out_ref, stage_ref, sems)
    old = (acc_in.at[half], m_in.at[half])
    bare = late & (place < 2)
    waits = late & (place == count - 2)
    ends = late & (place == count - 1)
    idle = bare | waits
    emits = ((half != core) & jnp.logical_not(waits)) | bare

    @pl.when(jnp.logical_not(idle | ends))
    def _():
        kv_ref[...] = matmul(far_ref[...], w_ref[:, width:]).astype(BF16)

    if late:
        @pl.when(ends)
        def _():
            kv_ref[...] = given_ref[...]

    @pl.when(jnp.logical_not(idle))
    def _():
        out = attend(q_ref.at[half], starts_ref.at[half], old, far_tiles(kv_ref, first))
        keep(out, acc_ref, m_ref)

    if late:
        @pl.when(idle)
        def _():
            acc_ref[...] = old[0][...]
            m_ref[...] = old[1][...]

    @pl.when(emits)
    def _():
        emit(heads_of(acc_ref))
        settle()


def near_half_kernel(
    count, starts_ref, near_ref, w_ref, q_ref, acc_in, m_in, kv_ref, part_ref
):
    place, side, core = where_am_i()
    half = 1 - side
    group, width = near_ref.shape
    first = block_first(half, place, count, group)

    @pl.when(half == core)
    def _():
        kv_ref[...] = matmul(near_ref[...], w_ref[:, width:]).astype(BF16)
        out = attend(
            q_ref.at[half], starts_ref.at[half], (acc_in, m_in), near_tiles(kv_ref, first),
            range(HEADS // 2),
        )
        for head, (mixed, _) in enumerate(out):
            part_ref[:, head * WIDE : (head + 1) * WIDE] = mixed


def finish_x_kernel(
    count, starts_ref, kv_ref, part_ref, w_out_ref, q_ref, acc_in, m_in, whole_ref,
    out_ref, stage_ref, sems,
):
    place, side, core = where_am_i()
    half = 1 - side
    group = stage_ref.shape[0]
    first = block_first(half, place, count, group)
    emit, settle = emitter(half, w_out_ref, out_ref, stage_ref, sems)

    @pl.when(half == core)
    def _():
        out = attend(
            q_ref.at[half], starts_ref.at[half], (acc_in, m_in), near_tiles(kv_ref, first),
            range(HEADS // 2, HEADS),
        )
        done = [part_ref[:, h * WIDE : (h + 1) * WIDE] for h in range(HEADS // 2)]
        emit(done + [mixed for mixed, _ in out])
        settle()


def finish_d_kernel(
    count, starts_ref, near_ref, block_ref, w_ref, w_out_ref, q_ref, acc_in, m_in, whole_ref,
    out_ref, stage_ref, sems, kv_ref, source_ref,
):
    place, side, core = where_am_i()
    half = side
    group, width = near_ref.shape
    first = block_first(half, place, count, group)
    emit, settle = emitter(half, w_out_ref, out_ref, stage_ref, sems)
    waits = place == count - 2
    runs = ((half == core) & (place >= 2)) | waits

    @pl.when(runs)
    def _():
        source_ref[...] = near_ref[...]

        @pl.when(place == count - 1)
        def _():
            source_ref[...] = block_ref[...]

        kv_ref[...] = matmul(source_ref[...], w_ref[:, width:]).astype(BF16)
        tiles = near_tiles(kv_ref, first - jnp.where(waits, group, 0))
        out = attend(q_ref.at[half], starts_ref.at[half], (acc_in, m_in), tiles)
        emit([mixed for mixed, _ in out])
        settle()


def params(mib):
    return pltpu.CompilerParams(vmem_limit_bytes=mib * 1024 * 1024)


def local(frames, episode_lengths, w_qkv, w_out):
    width = w_out.shape[0]
    group = frames.shape[2]
    count = lax.axis_size("ctx")
    chips = count // 2
    pair = [(i, i ^ 1) for i in range(count)]

    def route(links):
        return [(2 * a + c, 2 * b + c) for a, b in links for c in range(2)]

    even = [(c, c + 1) for c in range(0, chips - 1, 2)]
    odd = [(c, c + 1) for c in range(1, chips - 1, 2)]
    swap_x = route(even + [(b, a) for a, b in even])
    swap_d = route(odd + [(b, a) for a, b in odd])
    relay_out = route([(a, b + 1) for a, b in odd] + [(b, a - 1) for a, b in odd])
    relay_in = route([(b + 1, b) for a, b in odd] + [(a - 1, a) for a, b in odd])

    def send(block, links):
        return lax.ppermute(block, "ctx", links)

    def shape(*dims, dtype=BF16):
        return jax.ShapeDtypeStruct(dims, dtype)

    block = shape(group, width)
    part = shape(group // 2, width)
    kv_type = shape(group, 2 * width)
    state = (shape(group, HEADS * WIDE, dtype=F32), shape(group, width, dtype=F32))
    states = tuple(shape(2, *s.shape, dtype=F32) for s in state)
    block_scratch = pltpu.VMEM(block.shape, BF16)
    kv_scratch = pltpu.VMEM(kv_type.shape, BF16)

    def call(kernel, outs, operands, scratch=(), writes=False, aliased=None):
        specs = [VMEM] * len(operands)
        out_specs = [VMEM] * len(outs)
        scratch = list(scratch)
        options = {}
        if writes:
            outs = tuple(outs) + (jax.ShapeDtypeStruct(frames.shape, BF16),)
            out_specs.append(HBM)
            scratch = [block_scratch, pltpu.SemaphoreType.DMA((2,))] + scratch
        if aliased is not None:
            specs.append(HBM)
            options["input_output_aliases"] = {len(operands): len(outs) - 1}
            operands = operands + (aliased,)
        return pl.pallas_call(
            functools.partial(kernel, count),
            out_shape=outs,
            in_specs=specs,
            out_specs=tuple(out_specs),
            scratch_shapes=scratch,
            compiler_params=params(14),
            cost_estimate=pl.CostEstimate(flops=10**8, bytes_accessed=10**6, transcendentals=0),
            **options,
        )(*operands)

    straight, cross_a, cross_b = pl.pallas_call(
        prepare_kernel,
        out_shape=(block, part, part),
        in_specs=[VMEM],
        out_specs=(VMEM,) * 3,
        compiler_params=params(4),
        cost_estimate=pl.CostEstimate(flops=10**10, bytes_accessed=10**6, transcendentals=0),
    )(frames)
    x_in = send(straight, swap_x)
    hop_in = send(cross_a, relay_out)
    lengths = episode_lengths.reshape(1, -1)
    q, give, kv, starts = call(
        project_kernel,
        (shape(2, group, width), kv_type, kv_type, shape(2, group, LANES, dtype=jnp.int32)),
        (lengths, straight, cross_a, cross_b, w_qkv), (pltpu.VMEM((2, group, width), BF16),),
    )
    given = send(give, pair)
    d_in = send(cross_b, swap_d)
    r_in = send(hop_in, relay_in)
    acc, m = call(base_kernel, states, (starts, q, give, kv, given))
    x_in, acc = lax.optimization_barrier((x_in, acc))
    near_x = send(x_in, pair)

    def far(count, *refs):
        return far_kernel(count, False, *refs)

    def far_late(count, *refs):
        return far_kernel(count, True, *refs)

    acc_x, m_x, out = call(
        far, state, (starts, x_in, given, w_qkv, w_out, q, acc, m), (kv_scratch,), True
    )
    kv_near, part_x = call(
        near_half_kernel, (kv_type, shape(group, HEADS // 2 * WIDE, dtype=F32)),
        (starts, near_x, w_qkv, q, acc_x, m_x),
    )
    r_in, d_in, part_x = lax.optimization_barrier((r_in, d_in, part_x))
    (d_block,) = call(merge_kernel, (block,), (r_in, d_in, cross_a, cross_b))
    near_d = send(d_block, pair)
    (out,) = call(
        finish_x_kernel, (), (starts, kv_near, part_x, w_out, q, acc_x, m_x),
        (), True, out,
    )
    acc_d, m_d, out = call(
        far_late, state, (starts, d_block, given, w_qkv, w_out, q, acc, m),
        (kv_scratch,), True, out,
    )
    (out,) = call(
        finish_d_kernel, (), (starts, near_d, d_block, w_qkv, w_out, q, acc_d, m_d),
        (kv_scratch, block_scratch), True, out,
    )
    return out


def solution(mesh):
    in_specs = (P(("dp", "ctx"), None, None, None), P("dp"), P(), P())
    out_specs = P(("dp", "ctx"), None, None, None)
    return jax.shard_map(local, mesh=mesh, in_specs=in_specs, out_specs=out_specs, check_vma=False)
```

time: 38.8 us -> 44.7 us (1.15)
  waiting for transfers between devices: 10.4 us -> 17 us
  starting transfers between devices: 10.7 us -> 10.2 us
    ppermute x7, waiting for transfers between devices: 10.4 us -> 17 us  [send(): return lax.ppermute(block, 'ctx', links)]
    pallas_call x7 -> x8, Pallas kernels: 15.5 us -> 15.3 us  [call(): pl.pallas_call(functools.partial(kernel, count), out_shape=outs, in_specs...]
    unnamed x9 -> x8, local copies, waits for them, and re-layouts: 1.4 us -> 1.38 us
  transfers between devices with their start and end apart: 7 -> 7, of which waited for: 4 -> 5; matrix products, arithmetic and copies ran while one was open for 0% -> 0% of each run, Pallas kernels for 25% -> 22%
where the time goes in v4:
time: 44.7 us; the launch traced here: 44.5 us
  waiting for transfers between devices  17 us (38%)
  Pallas kernels  15.6 us (35%)
  starting transfers between devices  10.2 us (23%)
  local copies, waits for them, and re-layouts  1.38 us (3%)
    ppermute x7, waiting for transfers between devices, send(): return lax.ppermute(block, 'ctx', links)  17 us
    pallas_call x8, Pallas kernels, call(): pl.pallas_call(functools.partial(kernel, count), out_shape=outs, in_specs...  15.3 us
    ppermute x7, starting transfers between devices, send(): return lax.ppermute(block, 'ctx', links)  10.2 us
    unnamed x8, local copies, waits for them, and re-layouts  1.38 us
  transfers between devices with their start and end apart: 7, of which 5 were waited for; matrix products, arithmetic and copies ran while one was open for 0% of the time, Pallas kernels for 22%

profile of v4, /device:TPU:19, one launch (start us, length us, event | category | flops | bytes accessed | tf_op | source)
XLA Modules:
  0.0 44.5 jit_solution(2693513784393373436)
XLA Ops:
  0.0 0.0 copy-start.2
  0.0 0.0 copy-start
  0.0 0.0 copy-start.3
  0.0 1.3 %copy-done.3 = bf16[1,2,512,512]{3,2,1,0:T(8,128)(2,1)S(1)} copy-done((bf16[1,2,512,512]{3,2,1,0:T(8,128)(2,1)S(1)}, bf16[1,2,512,512]{3,2,1,0:T(8,128)(2,1)}, u32[]{:S(2)}) %copy-start.3) | copy-done | bytes 1048600
  1.3 0.3 shard_map.46
  1.7 0.0 copy-done.2
  1.7 0.0 copy-done
  1.7 2.1 %shard_map.47 = (bf16[2,512,512]{2,1,0:T(8,128)(2,1)S(1)}, bf16[512,1024]{1,0:T(8,128)(2,1)S(1)}, bf16[512,1024]{1,0:T(8,128)(2,1)S(1)}, s32[2,512,128]{2,1,0:T(8,128)S(1)}) custom-call(s32[1,16]{1,0:T(1,128)S(1)} %bitcast.1, bf16[512,512]{1,0:T(8,128)(2,1)S(1)} %get-tuple-element.27.straight_ref, bf16[256,512]{1,0:T(8,128)(2,1)S(1)} %get-tuple-element.28.cross_a_ref, ...), custom_call_target="tpu_custom_call" | custom-call | flops 100000000 | bytes 1000000 | tf_op jit(solution)/shard_map/pallas_call | solution.py:403
  3.8 0.7 %collective-permute-start.4 = (bf16[512,1024]{1,0:T(8,128)(2,1)S(1)}, bf16[512,1024]{1,0:T(8,128)(2,1)S(1)}, u32[]{:S(2)}, u32[]{:S(2)}) collective-permute-start(bf16[512,1024]{1,0:T(8,128)(2,1)S(1)} %get-tuple-element.32.give_ref), channel_id=1, source_target_pairs={{0,1},{1,0},{2,3},{3,2},{4,5},{5,4},{6,7},{7,6},{8,9},{9,8},{10,11... | collective-permute-start | bytes 3145736 | tf_op jit(solution)/shard_map/ppermute | solution.py:377
  4.6 0.3 collective-permute-start.3
  4.8 2.0 %collective-permute-done.4.given_ref.refs_2_ = bf16[512,1024]{1,0:T(8,128)(2,1)S(1)} collective-permute-done((bf16[512,1024]{1,0:T(8,128)(2,1)S(1)}, bf16[512,1024]{1,0:T(8,128)(2,1)S(1)}, u32[]{:S(2)}, u32[]{:S(2)}) %collective-permute-start.4) | collective-permute-done | bytes 1048608 | tf_op jit(solution)/shard_map/ppermute | solution.py:377
  6.8 0.0 copy-start.1
  6.8 4.0 %shard_map.48 = (f32[2,512,1024]{2,1,0:T(8,128)S(1)}, f32[2,512,512]{2,1,0:T(8,128)S(1)}) custom-call(s32[2,512,128]{2,1,0:T(8,128)S(1)} %get-tuple-element.30.starts_ref.refs_0_, bf16[2,512,512]{2,1,0:T(8,128)(2,1)S(1)} %get-tuple-element.31.q_ref.refs_5_, bf16[512,1024]{1,0:T(8,128)(2,1)S(1)} %get-tuple-element.32.give_ref, ...), custom_call_target="tpu_custom_call" | custom-call | flops 100000000 | bytes 1000000 | tf_op jit(solution)/shard_map/pallas_call | solution.py:403
  10.8 7.1 %collective-permute-done.3.refs_1_ = bf16[512,512]{1,0:T(8,128)(2,1)S(1)} collective-permute-done((bf16[512,512]{1,0:T(8,128)(2,1)S(1)}, bf16[512,512]{1,0:T(8,128)(2,1)S(1)}, u32[]{:S(2)}, u32[]{:S(2)}) %collective-permute-start.3) | collective-permute-done | bytes 524320 | tf_op jit(solution)/shard_map/ppermute | solution.py:377
  18.0 0.9 %collective-permute-start.5 = (bf16[512,512]{1,0:T(8,128)(2,1)S(1)}, bf16[512,512]{1,0:T(8,128)(2,1)S(1)}, u32[]{:S(2)}, u32[]{:S(2)}) collective-permute-start(bf16[512,512]{1,0:T(8,128)(2,1)S(1)} %collective-permute-done.3.refs_1_), channel_id=1, source_target_pairs={{0,1},{1,0},{2,3},{3,2},{4,5},{5,4},{6,7},{7,6},{8,9},{9,8},{10,11... | collective-permute-start | bytes 1572872 | tf_op jit(solution)/shard_map/ppermute | solution.py:377
  18.9 3.1 %collective-permute-start = (bf16[256,512]{1,0:T(8,128)(2,1)S(1)}, bf16[256,512]{1,0:T(8,128)(2,1)S(1)}, u32[]{:S(2)}, u32[]{:S(2)}) collective-permute-start(bf16[256,512]{1,0:T(8,128)(2,1)S(1)} %get-tuple-element.28.cross_a_ref), channel_id=1, source_target_pairs={{2,6},{3,7},{4,0},{5,1},{10,14},{11,15},{12,8},{13,9},{18,22},{19,... | collective-permute-start | bytes 786440 | tf_op jit(solution)/shard_map/ppermute | solution.py:377
  22.0 2.1 %collective-permute-start.2 = (bf16[256,512]{1,0:T(8,128)(2,1)S(1)}, bf16[256,512]{1,0:T(8,128)(2,1)S(1)}, u32[]{:S(2)}, u32[]{:S(2)}) collective-permute-start(bf16[256,512]{1,0:T(8,128)(2,1)S(1)} %get-tuple-element.29.cross_b_ref), channel_id=1, source_target_pairs={{2,4},{3,5},{4,2},{5,3},{10,12},{11,13},{12,10},{13,11},{18,20},{1... | collective-permute-start | bytes 786440 | tf_op jit(solution)/shard_map/ppermute | solution.py:377
  24.2 3.5 %collective-permute-done = bf16[256,512]{1,0:T(8,128)(2,1)S(1)} collective-permute-done((bf16[256,512]{1,0:T(8,128)(2,1)S(1)}, bf16[256,512]{1,0:T(8,128)(2,1)S(1)}, u32[]{:S(2)}, u32[]{:S(2)}) %collective-permute-start) | collective-permute-done | bytes 262176 | tf_op jit(solution)/shard_map/ppermute | solution.py:377
  27.7 1.3 %collective-permute-start.1 = (bf16[256,512]{1,0:T(8,128)(2,1)S(1)}, bf16[256,512]{1,0:T(8,128)(2,1)S(1)}, u32[]{:S(2)}, u32[]{:S(2)}) collective-permute-start(bf16[256,512]{1,0:T(8,128)(2,1)S(1)} %collective-permute-done), channel_id=1, source_target_pairs={{6,4},{7,5},{0,2},{1,3},{14,12},{15,13},{8,10},{9,11},{22,20},{23,... | collective-permute-start | bytes 786440 | tf_op jit(solution)/shard_map/ppermute | solution.py:377
  29.0 0.0 copy-done.1
  29.0 3.2 %shard_map.49 = (f32[512,1024]{1,0:T(8,128)S(1)}, f32[512,512]{1,0:T(8,128)S(1)}, bf16[1,2,512,512]{3,2,1,0:T(8,128)(2,1)}) custom-call(s32[2,512,128]{2,1,0:T(8,128)S(1)} %get-tuple-element.30.starts_ref.refs_0_, bf16[512,512]{1,0:T(8,128)(2,1)S(1)} %collective-permute-done.3.refs_1_, bf16[512,1024]{1,0:T(8,128)(2,1)S(1)} %collective-permute-done.4.given_ref.refs_2_, ...), custom_call_target="tpu_custom_call" | custom-call | flops 100000000 | bytes 1000000 | tf_op jit(solution)/shard_map/pallas_call | solution.py:403
  32.2 0.0 collective-permute-done.5.near_ref
  32.2 0.2 collective-permute-done.2.d_ref
  32.4 4.1 %collective-permute-done.1.r_ref = bf16[256,512]{1,0:T(8,128)(2,1)S(1)} collective-permute-done((bf16[256,512]{1,0:T(8,128)(2,1)S(1)}, bf16[256,512]{1,0:T(8,128)(2,1)S(1)}, u32[]{:S(2)}, u32[]{:S(2)}) %collective-permute-start.1) | collective-permute-done | bytes 262176 | tf_op jit(solution)/shard_map/ppermute | solution.py:377
  36.6 1.8 %collective-permute-start.6 = (bf16[512,512]{1,0:T(8,128)(2,1)S(1)}, bf16[512,512]{1,0:T(8,128)(2,1)S(1)}, u32[]{:S(2)}, u32[]{:S(2)}) collective-permute-start(bf16[512,512]{1,0:T(8,128)(2,1)S(1)} %shard_map.51.refs_1_.block_ref), channel_id=1, source_target_pairs={{0,1},{1,0},{2,3},{3,2},{4,5},{5,4},{6,7},{7,6},{8,9},{9,8},{10,11... | collective-permute-start | bytes 1572872 | tf_op jit(solution)/shard_map/ppermute | solution.py:377
  38.4 2.5 %shard_map.53 = (f32[512,1024]{1,0:T(8,128)S(1)}, f32[512,512]{1,0:T(8,128)S(1)}, bf16[1,2,512,512]{3,2,1,0:T(8,128)(2,1)}) custom-call(s32[2,512,128]{2,1,0:T(8,128)S(1)} %get-tuple-element.30.starts_ref.refs_0_, bf16[512,512]{1,0:T(8,128)(2,1)S(1)} %shard_map.51.refs_1_.block_ref, ...), custom_call_target="tpu_custom_call", output_to_operand_aliasing={{2}: (8, {})} | custom-call | flops 100000000 | bytes 1000000 | tf_op jit(solution)/shard_map/pallas_call | solution.py:403
  40.9 0.0 collective-permute-done.6.near_ref
  40.9 3.5 %shard_map.54 = bf16[1,2,512,512]{3,2,1,0:T(8,128)(2,1)} custom-call(s32[2,512,128]{2,1,0:T(8,128)S(1)} %get-tuple-element.30.starts_ref.refs_0_, bf16[512,512]{1,0:T(8,128)(2,1)S(1)} %collective-permute-done.6.near_ref, bf16[512,512]{1,0:T(8,128)(2,1)S(1)} %shard_map.51.refs_1_.block_ref, ...), custom_call_target="tpu_custom_call", output_to_operand_aliasing={{}: (8, {})} | custom-call | flops 100000000 | bytes 1000000 | tf_op jit(solution)/shard_map/pallas_call | solution.py:403
  (3 shorter events, 0.1 us)
Async XLA Ops:
  0.0 1.7 %copy-start.2 = (s32[16]{0:T(128)S(1)}, s32[16]{0:T(128)}, u32[]{:S(2)}) copy-start(s32[16]{0:T(128)} %param.5) | copy-start | bytes 196
  0.0 1.7 %copy-start = (bf16[512,1536]{1,0:T(8,128)(2,1)S(1)}, bf16[512,1536]{1,0:T(8,128)(2,1)}, u32[]{:S(2)}) copy-start(bf16[512,1536]{1,0:T(8,128)(2,1)} %w_ref.5) | copy-start | bytes 4718596
  0.0 1.3 %copy-start.3 = (bf16[1,2,512,512]{3,2,1,0:T(8,128)(2,1)S(1)}, bf16[1,2,512,512]{3,2,1,0:T(8,128)(2,1)}, u32[]{:S(2)}) copy-start(bf16[1,2,512,512]{3,2,1,0:T(8,128)(2,1)} %frames_ref.1) | copy-start | bytes 3145732
  3.8 3.0 %collective-permute-start.4 = (bf16[512,1024]{1,0:T(8,128)(2,1)S(1)}, bf16[512,1024]{1,0:T(8,128)(2,1)S(1)}, u32[]{:S(2)}, u32[]{:S(2)}) collective-permute-start(bf16[512,1024]{1,0:T(8,128)(2,1)S(1)} %get-tuple-element.32.give_ref), channel_id=1, source_target_pairs={{0,1},{1,0},{2,3},{3,2},{4,5},{5,4},{6,7},{7,6},{8,9},{9,8},{10,11... | collective-permute-start | bytes 3145736 | tf_op jit(solution)/shard_map/ppermute | solution.py:377
  4.6 13.4 %collective-permute-start.3 = (bf16[512,512]{1,0:T(8,128)(2,1)S(1)}, bf16[512,512]{1,0:T(8,128)(2,1)S(1)}, u32[]{:S(2)}, u32[]{:S(2)}) collective-permute-start(bf16[512,512]{1,0:T(8,128)(2,1)S(1)} %get-tuple-element.27.straight_ref), channel_id=1, source_target_pairs={{0,2},{1,3},{4,6},{5,7},{2,0},{3,1},{6,4},{7,5},{8,10},{9,11},{12,... | collective-permute-start | bytes 1572872 | tf_op jit(solution)/shard_map/ppermute | solution.py:377
  6.8 22.1 %copy-start.1 = (bf16[512,512]{1,0:T(8,128)(2,1)S(1)}, bf16[512,512]{1,0:T(8,128)(2,1)}, u32[]{:S(2)}) copy-start(bf16[512,512]{1,0:T(8,128)(2,1)} %w_out_ref.3) | copy-start | bytes 1572868
  18.0 14.2 %collective-permute-start.5 = (bf16[512,512]{1,0:T(8,128)(2,1)S(1)}, bf16[512,512]{1,0:T(8,128)(2,1)S(1)}, u32[]{:S(2)}, u32[]{:S(2)}) collective-permute-start(bf16[512,512]{1,0:T(8,128)(2,1)S(1)} %collective-permute-done.3.refs_1_), channel_id=1, source_target_pairs={{0,1},{1,0},{2,3},{3,2},{4,5},{5,4},{6,7},{7,6},{8,9},{9,8},{10,11... | collective-permute-start | bytes 1572872 | tf_op jit(solution)/shard_map/ppermute | solution.py:377
  18.9 8.8 %collective-permute-start = (bf16[256,512]{1,0:T(8,128)(2,1)S(1)}, bf16[256,512]{1,0:T(8,128)(2,1)S(1)}, u32[]{:S(2)}, u32[]{:S(2)}) collective-permute-start(bf16[256,512]{1,0:T(8,128)(2,1)S(1)} %get-tuple-element.28.cross_a_ref), channel_id=1, source_target_pairs={{2,6},{3,7},{4,0},{5,1},{10,14},{11,15},{12,8},{13,9},{18,22},{19,... | collective-permute-start | bytes 786440 | tf_op jit(solution)/shard_map/ppermute | solution.py:377
  22.0 10.4 %collective-permute-start.2 = (bf16[256,512]{1,0:T(8,128)(2,1)S(1)}, bf16[256,512]{1,0:T(8,128)(2,1)S(1)}, u32[]{:S(2)}, u32[]{:S(2)}) collective-permute-start(bf16[256,512]{1,0:T(8,128)(2,1)S(1)} %get-tuple-element.29.cross_b_ref), channel_id=1, source_target_pairs={{2,4},{3,5},{4,2},{5,3},{10,12},{11,13},{12,10},{13,11},{18,20},{1... | collective-permute-start | bytes 786440 | tf_op jit(solution)/shard_map/ppermute | solution.py:377
  27.7 8.9 %collective-permute-start.1 = (bf16[256,512]{1,0:T(8,128)(2,1)S(1)}, bf16[256,512]{1,0:T(8,128)(2,1)S(1)}, u32[]{:S(2)}, u32[]{:S(2)}) collective-permute-start(bf16[256,512]{1,0:T(8,128)(2,1)S(1)} %collective-permute-done), channel_id=1, source_target_pairs={{6,4},{7,5},{0,2},{1,3},{14,12},{15,13},{8,10},{9,11},{22,20},{23,... | collective-permute-start | bytes 786440 | tf_op jit(solution)/shard_map/ppermute | solution.py:377
  36.6 4.3 %collective-permute-start.6 = (bf16[512,512]{1,0:T(8,128)(2,1)S(1)}, bf16[512,512]{1,0:T(8,128)(2,1)S(1)}, u32[]{:S(2)}, u32[]{:S(2)}) collective-permute-start(bf16[512,512]{1,0:T(8,128)(2,1)S(1)} %shard_map.51.refs_1_.block_ref), channel_id=1, source_target_pairs={{0,1},{1,0},{2,3},{3,2},{4,5},{5,4},{6,7},{7,6},{8,9},{9,8},{10,11... | collective-permute-start | bytes 1572872 | tf_op jit(solution)/shard_map/ppermute | solution.py:377

commit v5 on v4

--- a/solution.py
+++ b/solution.py
@@ -144,12 +144,29 @@
     ]
 
 
-def prepare_kernel(frames_ref, straight_ref, cross_a_ref, cross_b_ref):
+def prepare_kernel(frames_ref, straight_ref, other_ref, raw_ref, sems):
     _, side, _ = where_am_i()
-    straight_ref[...] = normalize(frames_ref[0, side])
+    rows = raw_ref.shape[1]
+    copies = []
+    for index in range(2):
+        piece = pl.ds(index * rows, rows)
+        copies.append(
+            pltpu.make_async_copy(frames_ref.at[0, side, piece], raw_ref.at[index], sems.at[index])
+        )
+    rest = pltpu.make_async_copy(frames_ref.at[0, 1 - side], other_ref, sems.at[2])
+    for copy in copies:
+        copy.start()
+    rest.start()
+    for index, copy in enumerate(copies):
+        copy.wait()
+        straight_ref[index * rows : (index + 1) * rows] = normalize(raw_ref[index])
+    rest.wait()
+
+
+def cross_kernel(count, other_ref, cross_a_ref, cross_b_ref):
     rows = cross_a_ref.shape[0]
-    cross_a_ref[...] = normalize(frames_ref[0, 1 - side, :rows])
-    cross_b_ref[...] = normalize(frames_ref[0, 1 - side, rows:])
+    cross_a_ref[...] = normalize(other_ref[:rows])
+    cross_b_ref[...] = normalize(other_ref[rows:])
 
 
 def bounds_of(lengths_ref):
@@ -227,7 +244,7 @@
     return [acc_ref[:, h * WIDE : (h + 1) * WIDE] for h in range(HEADS)]
 
 
-def merge_kernel(count, r_ref, d_ref, cross_a_ref, cross_b_ref, block_ref):
+def merge_kernel(count, r_ref, d_ref, cross_a_ref, cross_b_ref, w_ref, kv_ref, block_ref):
     place, _, _ = where_am_i()
     rows = r_ref.shape[0]
     at_end = place // 2 == count // 2 - 1
@@ -242,44 +259,70 @@
         block_ref[:rows] = r_ref[...]
         block_ref[rows:] = d_ref[...]
 
-
-def far_kernel(
-    count, late, starts_ref, far_ref, given_ref, w_ref, w_out_ref, q_ref, acc_in, m_in, *refs
+    width = block_ref.shape[1]
+
+    @pl.when(place >= 2)
+    def _():
+        kv_ref[...] = matmul(block_ref[...], w_ref[:, width:]).astype(BF16)
+
+    @pl.when(place < 2)
+    def _():
+        kv_ref[...] = jnp.zeros_like(kv_ref)
+
+
+def far_x_kernel(
+    count, starts_ref, far_ref, w_ref, w_out_ref, q_ref, acc_in, m_in,
+    acc_ref, m_ref, out_ref, stage_ref, sems, kv_ref,
 ):
-    acc_ref, m_ref, out_ref, stage_ref, sems, kv_ref = refs[-6:]
     place, side, core = where_am_i()
-    half = side if late else 1 - side
+    half = 1 - side
     group, width = far_ref.shape
     first = block_first(half, place, count, group)
     emit, settle = emitter(half, w_out_ref, out_ref, stage_ref, sems)
+    kv_ref[...] = matmul(far_ref[...], w_ref[:, width:]).astype(BF16)
     old = (acc_in.at[half], m_in.at[half])
-    bare = late & (place < 2)
-    waits = late & (place == count - 2)
-    ends = late & (place == count - 1)
+    keep(attend(q_ref.at[half], starts_ref.at[half], old, far_tiles(kv_ref, first)), acc_ref, m_ref)
+
+    @pl.when(half != core)
+    def _():
+        emit(heads_of(acc_ref))
+        settle()
+
+
+def far_d_kernel(
+    count, starts_ref, far_ref, given_ref, w_out_ref, q_ref, acc_in, m_in, whole_ref,
+    acc_ref, m_ref, out_ref, stage_ref, sems,
+):
+    place, side, core = where_am_i()
+    half = side
+    group = far_ref.shape[0]
+    first = block_first(half, place, count, group)
+    emit, settle = emitter(half, w_out_ref, out_ref, stage_ref, sems)
+    old = (acc_in.at[half], m_in.at[half])
+    bare = place < 2
+    waits = place == count - 2
     idle = bare | waits
-    emits = ((half != core) & jnp.logical_not(waits)) | bare
-
-    @pl.when(jnp.logical_not(idle | ends))
-    def _():
-        kv_ref[...] = matmul(far_ref[...], w_ref[:, width:]).astype(BF16)
-
-    if late:
-        @pl.when(ends)
-        def _():
-            kv_ref[...] = given_ref[...]
-
-    @pl.when(jnp.logical_not(idle))
-    def _():
+
+    ends = place == count - 1
+
+    def run(kv_ref):
         out = attend(q_ref.at[half], starts_ref.at[half], old, far_tiles(kv_ref, first))
         keep(out, acc_ref, m_ref)
 
-    if late:
-        @pl.when(idle)
-        def _():
-            acc_ref[...] = old[0][...]
-            m_ref[...] = old[1][...]
-
-    @pl.when(emits)
+    @pl.when(jnp.logical_not(idle | ends))
+    def _():
+        run(far_ref)
+
+    @pl.when(ends)
+    def _():
+        run(given_ref)
+
+    @pl.when(idle)
+    def _():
+        acc_ref[...] = old[0][...]
+        m_ref[...] = old[1][...]
+
+    @pl.when(((half != core) & jnp.logical_not(waits)) | bare)
     def _():
         emit(heads_of(acc_ref))
         settle()
@@ -326,30 +369,31 @@
 
 
 def finish_d_kernel(
-    count, starts_ref, near_ref, block_ref, w_ref, w_out_ref, q_ref, acc_in, m_in, whole_ref,
-    out_ref, stage_ref, sems, kv_ref, source_ref,
+    count, starts_ref, swapped_ref, kept_ref, w_out_ref, q_ref, acc_in, m_in, whole_ref,
+    out_ref, stage_ref, sems,
 ):
     place, side, core = where_am_i()
     half = side
-    group, width = near_ref.shape
+    group = swapped_ref.shape[0]
     first = block_first(half, place, count, group)
     emit, settle = emitter(half, w_out_ref, out_ref, stage_ref, sems)
     waits = place == count - 2
+    ends = place == count - 1
     runs = ((half == core) & (place >= 2)) | waits
 
-    @pl.when(runs)
-    def _():
-        source_ref[...] = near_ref[...]
-
-        @pl.when(place == count - 1)
-        def _():
-            source_ref[...] = block_ref[...]
-
-        kv_ref[...] = matmul(source_ref[...], w_ref[:, width:]).astype(BF16)
+    def run(kv_ref):
         tiles = near_tiles(kv_ref, first - jnp.where(waits, group, 0))
         out = attend(q_ref.at[half], starts_ref.at[half], (acc_in, m_in), tiles)
         emit([mixed for mixed, _ in out])
         settle()
+
+    @pl.when(runs & ends)
+    def _():
+        run(kept_ref)
+
+    @pl.when(runs & jnp.logical_not(ends))
+    def _():
+        run(swapped_ref)
 
 
 def params(mib):
@@ -411,15 +455,19 @@
             **options,
         )(*operands)
 
-    straight, cross_a, cross_b = pl.pallas_call(
+    straight, other = pl.pallas_call(
         prepare_kernel,
-        out_shape=(block, part, part),
-        in_specs=[VMEM],
-        out_specs=(VMEM,) * 3,
-        compiler_params=params(4),
+        out_shape=(block, block),
+        in_specs=[HBM],
+        out_specs=(VMEM,) * 2,
+        scratch_shapes=[
+            pltpu.VMEM((2, group // 2, width), BF16), pltpu.SemaphoreType.DMA((3,)),
+        ],
+        compiler_params=params(52),
         cost_estimate=pl.CostEstimate(flops=10**10, bytes_accessed=10**6, transcendentals=0),
     )(frames)
     x_in = send(straight, swap_x)
+    cross_a, cross_b = call(cross_kernel, (part, part), (other,))
     hop_in = send(cross_a, relay_out)
     lengths = episode_lengths.reshape(1, -1)
     q, give, kv, starts = call(
@@ -433,34 +481,29 @@
     acc, m = call(base_kernel, states, (starts, q, give, kv, given))
     x_in, acc = lax.optimization_barrier((x_in, acc))
     near_x = send(x_in, pair)
-
-    def far(count, *refs):
-        return far_kernel(count, False, *refs)
-
-    def far_late(count, *refs):
-        return far_kernel(count, True, *refs)
-
     acc_x, m_x, out = call(
-        far, state, (starts, x_in, given, w_qkv, w_out, q, acc, m), (kv_scratch,), True
+        far_x_kernel, state, (starts, x_in, w_qkv, w_out, q, acc, m), (kv_scratch,), True
     )
     kv_near, part_x = call(
         near_half_kernel, (kv_type, shape(group, HEADS // 2 * WIDE, dtype=F32)),
         (starts, near_x, w_qkv, q, acc_x, m_x),
     )
     r_in, d_in, part_x = lax.optimization_barrier((r_in, d_in, part_x))
-    (d_block,) = call(merge_kernel, (block,), (r_in, d_in, cross_a, cross_b))
-    near_d = send(d_block, pair)
+    (kv_d,) = call(
+        merge_kernel, (kv_type,), (r_in, d_in, cross_a, cross_b, w_qkv), (block_scratch,)
+    )
+    near_d = send(kv_d, pair)
     (out,) = call(
         finish_x_kernel, (), (starts, kv_near, part_x, w_out, q, acc_x, m_x),
         (), True, out,
     )
     acc_d, m_d, out = call(
-        far_late, state, (starts, d_block, given, w_qkv, w_out, q, acc, m),
-        (kv_scratch,), True, out,
+        far_d_kernel, state, (starts, kv_d, given, w_out, q, acc, m),
+        (), True, out,
     )
     (out,) = call(
-        finish_d_kernel, (), (starts, near_d, d_block, w_qkv, w_out, q, acc_d, m_d),
-        (kv_scratch, block_scratch), True, out,
+        finish_d_kernel, (), (starts, near_d, kv_d, w_out, q, acc_d, m_d),
+        (), True, out,
     )
     return out
 

time: 44.7 us -> 44.6 us (level)
  local copies, waits for them, and re-layouts: 1.38 us -> 0.16 us
  waiting for transfers between devices: 17 us -> 17.7 us
    unnamed x8 -> x6, local copies, waits for them, and re-layouts: 1.38 us -> 0.16 us
    pallas_call x1, Pallas kernels: 0.35 us -> 1.37 us  [local(): pl.pallas_call(prepare_kernel, out_shape=(block, block), in_specs=[HBM],...]
    ppermute x7, waiting for transfers between devices: 17 us -> 17.7 us  [send(): return lax.ppermute(block, 'ctx', links)]
    pallas_call x8 -> x9, Pallas kernels: 15.3 us -> 14.6 us  [call(): pl.pallas_call(functools.partial(kernel, count), out_shape=outs, in_specs...]
  transfers between devices with their start and end apart: 7 -> 7, of which waited for: 5 -> 6; matrix products, arithmetic and copies ran while one was open for 0% -> 0% of each run, Pallas kernels for 22% -> 20%
where the time goes in v5:
time: 44.6 us; the launch traced here: 44.4 us
  waiting for transfers between devices  17.7 us (40%)
  Pallas kernels  16 us (36%)
  starting transfers between devices  10.2 us (23%)
    ppermute x7, waiting for transfers between devices, send(): return lax.ppermute(block, 'ctx', links)  17.7 us
    pallas_call x9, Pallas kernels, call(): pl.pallas_call(functools.partial(kernel, count), out_shape=outs, in_specs...  14.6 us
    ppermute x7, starting transfers between devices, send(): return lax.ppermute(block, 'ctx', links)  10.2 us
    pallas_call x1, Pallas kernels, local(): pl.pallas_call(prepare_kernel, out_shape=(block, block), in_specs=[HBM],...  1.37 us
  transfers between devices with their start and end apart: 7, of which 6 were waited for; matrix products, arithmetic and copies ran while one was open for 0% of the time, Pallas kernels for 20%

profile of v5, /device:TPU:19, one launch (start us, length us, event | category | flops | bytes accessed | tf_op | source)
XLA Modules:
  0.0 44.4 jit_solution(9883960163200777533)
XLA Ops:
  0.0 0.0 copy-start
  0.0 0.0 copy-start.2
  0.0 1.4 %shard_map.46 = (bf16[512,512]{1,0:T(8,128)(2,1)S(1)}, bf16[512,512]{1,0:T(8,128)(2,1)S(1)}) custom-call(bf16[1,2,512,512]{3,2,1,0:T(8,128)(2,1)} %frames_ref.1), custom_call_target="tpu_custom_call" | custom-call | flops 10000000000 | bytes 1000000 | tf_op jit(solution)/shard_map/pallas_call | solution.py:458
  1.4 0.2 shard_map.47
  1.6 0.1 copy-done
  1.7 0.0 copy-done.2
  1.7 2.1 %shard_map.48 = (bf16[2,512,512]{2,1,0:T(8,128)(2,1)S(1)}, bf16[512,1024]{1,0:T(8,128)(2,1)S(1)}, bf16[512,1024]{1,0:T(8,128)(2,1)S(1)}, s32[2,512,128]{2,1,0:T(8,128)S(1)}) custom-call(s32[1,16]{1,0:T(1,128)S(1)} %bitcast.1, bf16[512,512]{1,0:T(8,128)(2,1)S(1)} %get-tuple-element.28.straight_ref, bf16[256,512]{1,0:T(8,128)(2,1)S(1)} %get-tuple-element.30.cross_a_ref, ...), custom_call_target="tpu_custom_call" | custom-call | flops 100000000 | bytes 1000000 | tf_op jit(solution)/shard_map/pallas_call | solution.py:447
  3.8 0.7 %collective-permute-start.4 = (bf16[512,1024]{1,0:T(8,128)(2,1)S(1)}, bf16[512,1024]{1,0:T(8,128)(2,1)S(1)}, u32[]{:S(2)}, u32[]{:S(2)}) collective-permute-start(bf16[512,1024]{1,0:T(8,128)(2,1)S(1)} %get-tuple-element.34.give_ref), channel_id=1, source_target_pairs={{0,1},{1,0},{2,3},{3,2},{4,5},{5,4},{6,7},{7,6},{8,9},{9,8},{10,11... | collective-permute-start | bytes 3145736 | tf_op jit(solution)/shard_map/ppermute | solution.py:421
  4.5 0.3 collective-permute-start.3
  4.8 2.0 %collective-permute-done.4.given_ref = bf16[512,1024]{1,0:T(8,128)(2,1)S(1)} collective-permute-done((bf16[512,1024]{1,0:T(8,128)(2,1)S(1)}, bf16[512,1024]{1,0:T(8,128)(2,1)S(1)}, u32[]{:S(2)}, u32[]{:S(2)}) %collective-permute-start.4) | collective-permute-done | bytes 1048608 | tf_op jit(solution)/shard_map/ppermute | solution.py:421
  6.8 0.0 copy-start.1
  6.8 4.0 %shard_map.49 = (f32[2,512,1024]{2,1,0:T(8,128)S(1)}, f32[2,512,512]{2,1,0:T(8,128)S(1)}) custom-call(s32[2,512,128]{2,1,0:T(8,128)S(1)} %get-tuple-element.32.starts_ref, bf16[2,512,512]{2,1,0:T(8,128)(2,1)S(1)} %get-tuple-element.33.q_ref, bf16[512,1024]{1,0:T(8,128)(2,1)S(1)} %get-tuple-element.34.give_ref, ...), custom_call_target="tpu_custom_call" | custom-call | flops 100000000 | bytes 1000000 | tf_op jit(solution)/shard_map/pallas_call | solution.py:447
  10.8 7.1 %collective-permute-done.3.far_ref = bf16[512,512]{1,0:T(8,128)(2,1)S(1)} collective-permute-done((bf16[512,512]{1,0:T(8,128)(2,1)S(1)}, bf16[512,512]{1,0:T(8,128)(2,1)S(1)}, u32[]{:S(2)}, u32[]{:S(2)}) %collective-permute-start.3) | collective-permute-done | bytes 524320 | tf_op jit(solution)/shard_map/ppermute | solution.py:421
  17.9 0.9 %collective-permute-start.5 = (bf16[512,512]{1,0:T(8,128)(2,1)S(1)}, bf16[512,512]{1,0:T(8,128)(2,1)S(1)}, u32[]{:S(2)}, u32[]{:S(2)}) collective-permute-start(bf16[512,512]{1,0:T(8,128)(2,1)S(1)} %collective-permute-done.3.far_ref), channel_id=1, source_target_pairs={{0,1},{1,0},{2,3},{3,2},{4,5},{5,4},{6,7},{7,6},{8,9},{9,8},{10,11... | collective-permute-start | bytes 1572872 | tf_op jit(solution)/shard_map/ppermute | solution.py:421
  18.9 3.1 %collective-permute-start = (bf16[256,512]{1,0:T(8,128)(2,1)S(1)}, bf16[256,512]{1,0:T(8,128)(2,1)S(1)}, u32[]{:S(2)}, u32[]{:S(2)}) collective-permute-start(bf16[256,512]{1,0:T(8,128)(2,1)S(1)} %get-tuple-element.30.cross_a_ref), channel_id=1, source_target_pairs={{2,6},{3,7},{4,0},{5,1},{10,14},{11,15},{12,8},{13,9},{18,22},{19,... | collective-permute-start | bytes 786440 | tf_op jit(solution)/shard_map/ppermute | solution.py:421
  22.0 2.1 %collective-permute-start.2 = (bf16[256,512]{1,0:T(8,128)(2,1)S(1)}, bf16[256,512]{1,0:T(8,128)(2,1)S(1)}, u32[]{:S(2)}, u32[]{:S(2)}) collective-permute-start(bf16[256,512]{1,0:T(8,128)(2,1)S(1)} %get-tuple-element.31.cross_b_ref), channel_id=1, source_target_pairs={{2,4},{3,5},{4,2},{5,3},{10,12},{11,13},{12,10},{13,11},{18,20},{1... | collective-permute-start | bytes 786440 | tf_op jit(solution)/shard_map/ppermute | solution.py:421
  24.1 3.5 %collective-permute-done = bf16[256,512]{1,0:T(8,128)(2,1)S(1)} collective-permute-done((bf16[256,512]{1,0:T(8,128)(2,1)S(1)}, bf16[256,512]{1,0:T(8,128)(2,1)S(1)}, u32[]{:S(2)}, u32[]{:S(2)}) %collective-permute-start) | collective-permute-done | bytes 262176 | tf_op jit(solution)/shard_map/ppermute | solution.py:421
  27.7 1.3 %collective-permute-start.1 = (bf16[256,512]{1,0:T(8,128)(2,1)S(1)}, bf16[256,512]{1,0:T(8,128)(2,1)S(1)}, u32[]{:S(2)}, u32[]{:S(2)}) collective-permute-start(bf16[256,512]{1,0:T(8,128)(2,1)S(1)} %collective-permute-done), channel_id=1, source_target_pairs={{6,4},{7,5},{0,2},{1,3},{14,12},{15,13},{8,10},{9,11},{22,20},{23,... | collective-permute-start | bytes 786440 | tf_op jit(solution)/shard_map/ppermute | solution.py:421
  29.0 0.0 copy-done.1
  29.0 3.2 %shard_map.50 = (f32[512,1024]{1,0:T(8,128)S(1)}, f32[512,512]{1,0:T(8,128)S(1)}, bf16[1,2,512,512]{3,2,1,0:T(8,128)(2,1)}) custom-call(s32[2,512,128]{2,1,0:T(8,128)S(1)} %get-tuple-element.32.starts_ref, bf16[512,512]{1,0:T(8,128)(2,1)S(1)} %collective-permute-done.3.far_ref, bf16[512,1536]{1,0:T(8,128)(2,1)S(1)} %copy-done, ...), custom_call_target="tpu_custom_call" | custom-call | flops 100000000 | bytes 1000000 | tf_op jit(solution)/shard_map/pallas_call | solution.py:447
  32.2 0.0 collective-permute-done.5.near_ref
  32.2 0.2 collective-permute-done.2.d_ref
  32.4 4.1 %collective-permute-done.1.r_ref = bf16[256,512]{1,0:T(8,128)(2,1)S(1)} collective-permute-done((bf16[256,512]{1,0:T(8,128)(2,1)S(1)}, bf16[256,512]{1,0:T(8,128)(2,1)S(1)}, u32[]{:S(2)}, u32[]{:S(2)}) %collective-permute-start.1) | collective-permute-done | bytes 262176 | tf_op jit(solution)/shard_map/ppermute | solution.py:421
  36.5 0.7 %shard_map.52.far_ref.kept_ref = bf16[512,1024]{1,0:T(8,128)(2,1)S(1)} custom-call(bf16[256,512]{1,0:T(8,128)(2,1)S(1)} %collective-permute-done.1.r_ref, bf16[256,512]{1,0:T(8,128)(2,1)S(1)} %collective-permute-done.2.d_ref, bf16[256,512]{1,0:T(8,128)(2,1)S(1)} %get-tuple-element.30.cross_a_ref, bf16[256,512]{1,0:T(8,128)(2,1)S(1)} %get-tuple-element.31.cross_b_ref, ...), custom_call_target="tpu_custom_call" | custom-call | flops 100000000 | bytes 1000000 | tf_op jit(solution)/shard_map/pallas_call | solution.py:447
  37.3 1.8 %collective-permute-start.6 = (bf16[512,1024]{1,0:T(8,128)(2,1)S(1)}, bf16[512,1024]{1,0:T(8,128)(2,1)S(1)}, u32[]{:S(2)}, u32[]{:S(2)}) collective-permute-start(bf16[512,1024]{1,0:T(8,128)(2,1)S(1)} %shard_map.52.far_ref.kept_ref), channel_id=1, source_target_pairs={{0,1},{1,0},{2,3},{3,2},{4,5},{5,4},{6,7},{7,6},{8,9},{9,8},{10,11... | collective-permute-start | bytes 3145736 | tf_op jit(solution)/shard_map/ppermute | solution.py:421
  39.1 1.6 %shard_map.54 = (f32[512,1024]{1,0:T(8,128)S(1)}, f32[512,512]{1,0:T(8,128)S(1)}, bf16[1,2,512,512]{3,2,1,0:T(8,128)(2,1)}) custom-call(s32[2,512,128]{2,1,0:T(8,128)S(1)} %get-tuple-element.32.starts_ref, bf16[512,1024]{1,0:T(8,128)(2,1)S(1)} %shard_map.52.far_ref.kept_ref, ...), custom_call_target="tpu_custom_call", output_to_operand_aliasing={{2}: (7, {})} | custom-call | flops 100000000 | bytes 1000000 | tf_op jit(solution)/shard_map/pallas_call | solution.py:447
  40.7 0.7 %collective-permute-done.6.swapped_ref = bf16[512,1024]{1,0:T(8,128)(2,1)S(1)} collective-permute-done((bf16[512,1024]{1,0:T(8,128)(2,1)S(1)}, bf16[512,1024]{1,0:T(8,128)(2,1)S(1)}, u32[]{:S(2)}, u32[]{:S(2)}) %collective-permute-start.6) | collective-permute-done | bytes 1048608 | tf_op jit(solution)/shard_map/ppermute | solution.py:421
  41.4 2.8 %shard_map.55 = bf16[1,2,512,512]{3,2,1,0:T(8,128)(2,1)} custom-call(s32[2,512,128]{2,1,0:T(8,128)S(1)} %get-tuple-element.32.starts_ref, bf16[512,1024]{1,0:T(8,128)(2,1)S(1)} %collective-permute-done.6.swapped_ref, bf16[512,1024]{1,0:T(8,128)(2,1)S(1)} %shard_map.52.far_ref.kept_ref, ...), custom_call_target="tpu_custom_call", output_to_operand_aliasing={{}: (7, {})} | custom-call | flops 100000000 | bytes 1000000 | tf_op jit(solution)/shard_map/pallas_call | solution.py:447
  (2 shorter events, 0.0 us)
Async XLA Ops:
  0.0 1.7 %copy-start = (bf16[512,1536]{1,0:T(8,128)(2,1)S(1)}, bf16[512,1536]{1,0:T(8,128)(2,1)}, u32[]{:S(2)}) copy-start(bf16[512,1536]{1,0:T(8,128)(2,1)} %w_ref.7) | copy-start | bytes 4718596
  0.0 1.7 %copy-start.2 = (s32[16]{0:T(128)S(1)}, s32[16]{0:T(128)}, u32[]{:S(2)}) copy-start(s32[16]{0:T(128)} %param.5) | copy-start | bytes 196
  3.8 3.0 %collective-permute-start.4 = (bf16[512,1024]{1,0:T(8,128)(2,1)S(1)}, bf16[512,1024]{1,0:T(8,128)(2,1)S(1)}, u32[]{:S(2)}, u32[]{:S(2)}) collective-permute-start(bf16[512,1024]{1,0:T(8,128)(2,1)S(1)} %get-tuple-element.34.give_ref), channel_id=1, source_target_pairs={{0,1},{1,0},{2,3},{3,2},{4,5},{5,4},{6,7},{7,6},{8,9},{9,8},{10,11... | collective-permute-start | bytes 3145736 | tf_op jit(solution)/shard_map/ppermute | solution.py:421
  4.5 13.4 %collective-permute-start.3 = (bf16[512,512]{1,0:T(8,128)(2,1)S(1)}, bf16[512,512]{1,0:T(8,128)(2,1)S(1)}, u32[]{:S(2)}, u32[]{:S(2)}) collective-permute-start(bf16[512,512]{1,0:T(8,128)(2,1)S(1)} %get-tuple-element.28.straight_ref), channel_id=1, source_target_pairs={{0,2},{1,3},{4,6},{5,7},{2,0},{3,1},{6,4},{7,5},{8,10},{9,11},{12,... | collective-permute-start | bytes 1572872 | tf_op jit(solution)/shard_map/ppermute | solution.py:421
  6.8 22.1 %copy-start.1 = (bf16[512,512]{1,0:T(8,128)(2,1)S(1)}, bf16[512,512]{1,0:T(8,128)(2,1)}, u32[]{:S(2)}) copy-start(bf16[512,512]{1,0:T(8,128)(2,1)} %w_out_ref.7) | copy-start | bytes 1572868
  17.9 14.2 %collective-permute-start.5 = (bf16[512,512]{1,0:T(8,128)(2,1)S(1)}, bf16[512,512]{1,0:T(8,128)(2,1)S(1)}, u32[]{:S(2)}, u32[]{:S(2)}) collective-permute-start(bf16[512,512]{1,0:T(8,128)(2,1)S(1)} %collective-permute-done.3.far_ref), channel_id=1, source_target_pairs={{0,1},{1,0},{2,3},{3,2},{4,5},{5,4},{6,7},{7,6},{8,9},{9,8},{10,11... | collective-permute-start | bytes 1572872 | tf_op jit(solution)/shard_map/ppermute | solution.py:421
  18.9 8.8 %collective-permute-start = (bf16[256,512]{1,0:T(8,128)(2,1)S(1)}, bf16[256,512]{1,0:T(8,128)(2,1)S(1)}, u32[]{:S(2)}, u32[]{:S(2)}) collective-permute-start(bf16[256,512]{1,0:T(8,128)(2,1)S(1)} %get-tuple-element.30.cross_a_ref), channel_id=1, source_target_pairs={{2,6},{3,7},{4,0},{5,1},{10,14},{11,15},{12,8},{13,9},{18,22},{19,... | collective-permute-start | bytes 786440 | tf_op jit(solution)/shard_map/ppermute | solution.py:421
  22.0 10.4 %collective-permute-start.2 = (bf16[256,512]{1,0:T(8,128)(2,1)S(1)}, bf16[256,512]{1,0:T(8,128)(2,1)S(1)}, u32[]{:S(2)}, u32[]{:S(2)}) collective-permute-start(bf16[256,512]{1,0:T(8,128)(2,1)S(1)} %get-tuple-element.31.cross_b_ref), channel_id=1, source_target_pairs={{2,4},{3,5},{4,2},{5,3},{10,12},{11,13},{12,10},{13,11},{18,20},{1... | collective-permute-start | bytes 786440 | tf_op jit(solution)/shard_map/ppermute | solution.py:421
  27.7 8.9 %collective-permute-start.1 = (bf16[256,512]{1,0:T(8,128)(2,1)S(1)}, bf16[256,512]{1,0:T(8,128)(2,1)S(1)}, u32[]{:S(2)}, u32[]{:S(2)}) collective-permute-start(bf16[256,512]{1,0:T(8,128)(2,1)S(1)} %collective-permute-done), channel_id=1, source_target_pairs={{6,4},{7,5},{0,2},{1,3},{14,12},{15,13},{8,10},{9,11},{22,20},{23,... | collective-permute-start | bytes 786440 | tf_op jit(solution)/shard_map/ppermute | solution.py:421
  37.3 4.1 %collective-permute-start.6 = (bf16[512,1024]{1,0:T(8,128)(2,1)S(1)}, bf16[512,1024]{1,0:T(8,128)(2,1)S(1)}, u32[]{:S(2)}, u32[]{:S(2)}) collective-permute-start(bf16[512,1024]{1,0:T(8,128)(2,1)S(1)} %shard_map.52.far_ref.kept_ref), channel_id=1, source_target_pairs={{0,1},{1,0},{2,3},{3,2},{4,5},{5,4},{6,7},{7,6},{8,9},{9,8},{10,11... | collective-permute-start | bytes 3145736 | tf_op jit(solution)/shard_map/ppermute | solution.py:421

commit v6 on v5

--- a/solution.py
+++ b/solution.py
@@ -90,13 +90,13 @@
             peak = jnp.maximum(before, peak)
         mixes = []
         for tile, (kv_ref, _, low, size, top, bottom, _) in zip(scores, tiles):
-            weights = jnp.exp2(tile - across(peak[top:bottom], size)).astype(BF16)
+            weights = jnp.exp2((tile - across(peak[top:bottom], size)) * SCALE2).astype(BF16)
             ones = jnp.ones((size, LANES), BF16)
             mix = matmul(weights, beside(kv_ref[pl.ds(low, size), vs], ones))
             mixes.append((mix, top, bottom))
         mixed = spread(jnp.add, mixes, rows)
         if old is not None:
-            mixed = mixed + across(jnp.exp2(before - peak), WIDE) * old[0][:, ws]
+            mixed = mixed + across(jnp.exp2((before - peak) * SCALE2), WIDE) * old[0][:, ws]
         out.append((mixed, peak))
     return out
 
@@ -197,7 +197,7 @@
     for half, pair_ref in ((core, give_ref), (1 - core, kv_ref)):
         normed = blocks_ref[half]
         pair_ref[...] = matmul(normed, w_ref[:, width:]).astype(BF16)
-        q_ref[half] = (matmul(normed, w_ref[:, :width]) * SCALE2).astype(BF16)
+        q_ref[half] = matmul(normed, w_ref[:, :width]).astype(BF16)
     bounds = bounds_of(lengths_ref)
     for half in range(2):
         fill_starts(starts_ref.at[half], bounds, block_first(half, place, count, group))

time: 44.6 us -> 44.7 us (level)
  no operation moved by 1% of the time
where the time goes in v6:
time: 44.7 us; the launch traced here: 44.5 us
  waiting for transfers between devices  17.5 us (39%)
  Pallas kernels  16.4 us (37%)
  starting transfers between devices  10.2 us (23%)
    ppermute x7, waiting for transfers between devices, send(): return lax.ppermute(block, 'ctx', links)  17.5 us
    pallas_call x9, Pallas kernels, call(): pl.pallas_call(functools.partial(kernel, count), out_shape=outs, in_specs...  15 us
    ppermute x7, starting transfers between devices, send(): return lax.ppermute(block, 'ctx', links)  10.2 us
    pallas_call x1, Pallas kernels, local(): pl.pallas_call(prepare_kernel, out_shape=(block, block), in_specs=[HBM],...  1.37 us
  transfers between devices with their start and end apart: 7, of which 6 were waited for; matrix products, arithmetic and copies ran while one was open for 0% of the time, Pallas kernels for 20%

profile of v6, /device:TPU:19, one launch (start us, length us, event | category | flops | bytes accessed | tf_op | source)
XLA Modules:
  0.0 44.5 jit_solution(12477675320940261846)
XLA Ops:
  0.0 0.0 copy-start
  0.0 0.0 copy-start.2
  0.0 1.4 %shard_map.46 = (bf16[512,512]{1,0:T(8,128)(2,1)S(1)}, bf16[512,512]{1,0:T(8,128)(2,1)S(1)}) custom-call(bf16[1,2,512,512]{3,2,1,0:T(8,128)(2,1)} %frames_ref.1), custom_call_target="tpu_custom_call" | custom-call | flops 10000000000 | bytes 1000000 | tf_op jit(solution)/shard_map/pallas_call | solution.py:458
  1.4 0.2 shard_map.47
  1.6 0.1 copy-done
  1.7 0.0 copy-done.2
  1.7 2.1 %shard_map.48 = (bf16[2,512,512]{2,1,0:T(8,128)(2,1)S(1)}, bf16[512,1024]{1,0:T(8,128)(2,1)S(1)}, bf16[512,1024]{1,0:T(8,128)(2,1)S(1)}, s32[2,512,128]{2,1,0:T(8,128)S(1)}) custom-call(s32[1,16]{1,0:T(1,128)S(1)} %bitcast.1, bf16[512,512]{1,0:T(8,128)(2,1)S(1)} %get-tuple-element.28.straight_ref, bf16[256,512]{1,0:T(8,128)(2,1)S(1)} %get-tuple-element.30.cross_a_ref, ...), custom_call_target="tpu_custom_call" | custom-call | flops 100000000 | bytes 1000000 | tf_op jit(solution)/shard_map/pallas_call | solution.py:447
  3.8 0.7 %collective-permute-start.4 = (bf16[512,1024]{1,0:T(8,128)(2,1)S(1)}, bf16[512,1024]{1,0:T(8,128)(2,1)S(1)}, u32[]{:S(2)}, u32[]{:S(2)}) collective-permute-start(bf16[512,1024]{1,0:T(8,128)(2,1)S(1)} %get-tuple-element.34.give_ref), channel_id=1, source_target_pairs={{0,1},{1,0},{2,3},{3,2},{4,5},{5,4},{6,7},{7,6},{8,9},{9,8},{10,11... | collective-permute-start | bytes 3145736 | tf_op jit(solution)/shard_map/ppermute | solution.py:421
  4.5 0.3 collective-permute-start.3
  4.8 2.0 %collective-permute-done.4.given_ref = bf16[512,1024]{1,0:T(8,128)(2,1)S(1)} collective-permute-done((bf16[512,1024]{1,0:T(8,128)(2,1)S(1)}, bf16[512,1024]{1,0:T(8,128)(2,1)S(1)}, u32[]{:S(2)}, u32[]{:S(2)}) %collective-permute-start.4) | collective-permute-done | bytes 1048608 | tf_op jit(solution)/shard_map/ppermute | solution.py:421
  6.8 0.0 copy-start.1
  6.8 4.1 %shard_map.49 = (f32[2,512,1024]{2,1,0:T(8,128)S(1)}, f32[2,512,512]{2,1,0:T(8,128)S(1)}) custom-call(s32[2,512,128]{2,1,0:T(8,128)S(1)} %get-tuple-element.32.starts_ref, bf16[2,512,512]{2,1,0:T(8,128)(2,1)S(1)} %get-tuple-element.33.q_ref, bf16[512,1024]{1,0:T(8,128)(2,1)S(1)} %get-tuple-element.34.give_ref, ...), custom_call_target="tpu_custom_call" | custom-call | flops 100000000 | bytes 1000000 | tf_op jit(solution)/shard_map/pallas_call | solution.py:447
  10.9 7.0 %collective-permute-done.3.far_ref = bf16[512,512]{1,0:T(8,128)(2,1)S(1)} collective-permute-done((bf16[512,512]{1,0:T(8,128)(2,1)S(1)}, bf16[512,512]{1,0:T(8,128)(2,1)S(1)}, u32[]{:S(2)}, u32[]{:S(2)}) %collective-permute-start.3) | collective-permute-done | bytes 524320 | tf_op jit(solution)/shard_map/ppermute | solution.py:421
  17.9 0.9 %collective-permute-start.5 = (bf16[512,512]{1,0:T(8,128)(2,1)S(1)}, bf16[512,512]{1,0:T(8,128)(2,1)S(1)}, u32[]{:S(2)}, u32[]{:S(2)}) collective-permute-start(bf16[512,512]{1,0:T(8,128)(2,1)S(1)} %collective-permute-done.3.far_ref), channel_id=1, source_target_pairs={{0,1},{1,0},{2,3},{3,2},{4,5},{5,4},{6,7},{7,6},{8,9},{9,8},{10,11... | collective-permute-start | bytes 1572872 | tf_op jit(solution)/shard_map/ppermute | solution.py:421
  18.9 3.1 %collective-permute-start = (bf16[256,512]{1,0:T(8,128)(2,1)S(1)}, bf16[256,512]{1,0:T(8,128)(2,1)S(1)}, u32[]{:S(2)}, u32[]{:S(2)}) collective-permute-start(bf16[256,512]{1,0:T(8,128)(2,1)S(1)} %get-tuple-element.30.cross_a_ref), channel_id=1, source_target_pairs={{2,6},{3,7},{4,0},{5,1},{10,14},{11,15},{12,8},{13,9},{18,22},{19,... | collective-permute-start | bytes 786440 | tf_op jit(solution)/shard_map/ppermute | solution.py:421
  22.0 2.1 %collective-permute-start.2 = (bf16[256,512]{1,0:T(8,128)(2,1)S(1)}, bf16[256,512]{1,0:T(8,128)(2,1)S(1)}, u32[]{:S(2)}, u32[]{:S(2)}) collective-permute-start(bf16[256,512]{1,0:T(8,128)(2,1)S(1)} %get-tuple-element.31.cross_b_ref), channel_id=1, source_target_pairs={{2,4},{3,5},{4,2},{5,3},{10,12},{11,13},{12,10},{13,11},{18,20},{1... | collective-permute-start | bytes 786440 | tf_op jit(solution)/shard_map/ppermute | solution.py:421
  24.1 3.5 %collective-permute-done = bf16[256,512]{1,0:T(8,128)(2,1)S(1)} collective-permute-done((bf16[256,512]{1,0:T(8,128)(2,1)S(1)}, bf16[256,512]{1,0:T(8,128)(2,1)S(1)}, u32[]{:S(2)}, u32[]{:S(2)}) %collective-permute-start) | collective-permute-done | bytes 262176 | tf_op jit(solution)/shard_map/ppermute | solution.py:421
  27.7 1.3 %collective-permute-start.1 = (bf16[256,512]{1,0:T(8,128)(2,1)S(1)}, bf16[256,512]{1,0:T(8,128)(2,1)S(1)}, u32[]{:S(2)}, u32[]{:S(2)}) collective-permute-start(bf16[256,512]{1,0:T(8,128)(2,1)S(1)} %collective-permute-done), channel_id=1, source_target_pairs={{6,4},{7,5},{0,2},{1,3},{14,12},{15,13},{8,10},{9,11},{22,20},{23,... | collective-permute-start | bytes 786440 | tf_op jit(solution)/shard_map/ppermute | solution.py:421
  29.0 0.0 copy-done.1
  29.0 3.3 %shard_map.50 = (f32[512,1024]{1,0:T(8,128)S(1)}, f32[512,512]{1,0:T(8,128)S(1)}, bf16[1,2,512,512]{3,2,1,0:T(8,128)(2,1)}) custom-call(s32[2,512,128]{2,1,0:T(8,128)S(1)} %get-tuple-element.32.starts_ref, bf16[512,512]{1,0:T(8,128)(2,1)S(1)} %collective-permute-done.3.far_ref, bf16[512,1536]{1,0:T(8,128)(2,1)S(1)} %copy-done, ...), custom_call_target="tpu_custom_call" | custom-call | flops 100000000 | bytes 1000000 | tf_op jit(solution)/shard_map/pallas_call | solution.py:447
  32.2 0.0 collective-permute-done.5.near_ref
  32.3 0.1 collective-permute-done.2.d_ref
  32.4 4.1 %collective-permute-done.1.r_ref = bf16[256,512]{1,0:T(8,128)(2,1)S(1)} collective-permute-done((bf16[256,512]{1,0:T(8,128)(2,1)S(1)}, bf16[256,512]{1,0:T(8,128)(2,1)S(1)}, u32[]{:S(2)}, u32[]{:S(2)}) %collective-permute-start.1) | collective-permute-done | bytes 262176 | tf_op jit(solution)/shard_map/ppermute | solution.py:421
  36.5 0.7 %shard_map.52.far_ref.kept_ref = bf16[512,1024]{1,0:T(8,128)(2,1)S(1)} custom-call(bf16[256,512]{1,0:T(8,128)(2,1)S(1)} %collective-permute-done.1.r_ref, bf16[256,512]{1,0:T(8,128)(2,1)S(1)} %collective-permute-done.2.d_ref, bf16[256,512]{1,0:T(8,128)(2,1)S(1)} %get-tuple-element.30.cross_a_ref, bf16[256,512]{1,0:T(8,128)(2,1)S(1)} %get-tuple-element.31.cross_b_ref, ...), custom_call_target="tpu_custom_call" | custom-call | flops 100000000 | bytes 1000000 | tf_op jit(solution)/shard_map/pallas_call | solution.py:447
  37.3 1.8 %collective-permute-start.6 = (bf16[512,1024]{1,0:T(8,128)(2,1)S(1)}, bf16[512,1024]{1,0:T(8,128)(2,1)S(1)}, u32[]{:S(2)}, u32[]{:S(2)}) collective-permute-start(bf16[512,1024]{1,0:T(8,128)(2,1)S(1)} %shard_map.52.far_ref.kept_ref), channel_id=1, source_target_pairs={{0,1},{1,0},{2,3},{3,2},{4,5},{5,4},{6,7},{7,6},{8,9},{9,8},{10,11... | collective-permute-start | bytes 3145736 | tf_op jit(solution)/shard_map/ppermute | solution.py:421
  39.1 1.6 %shard_map.54 = (f32[512,1024]{1,0:T(8,128)S(1)}, f32[512,512]{1,0:T(8,128)S(1)}, bf16[1,2,512,512]{3,2,1,0:T(8,128)(2,1)}) custom-call(s32[2,512,128]{2,1,0:T(8,128)S(1)} %get-tuple-element.32.starts_ref, bf16[512,1024]{1,0:T(8,128)(2,1)S(1)} %shard_map.52.far_ref.kept_ref, ...), custom_call_target="tpu_custom_call", output_to_operand_aliasing={{2}: (7, {})} | custom-call | flops 100000000 | bytes 1000000 | tf_op jit(solution)/shard_map/pallas_call | solution.py:447
  40.8 0.6 %collective-permute-done.6.swapped_ref = bf16[512,1024]{1,0:T(8,128)(2,1)S(1)} collective-permute-done((bf16[512,1024]{1,0:T(8,128)(2,1)S(1)}, bf16[512,1024]{1,0:T(8,128)(2,1)S(1)}, u32[]{:S(2)}, u32[]{:S(2)}) %collective-permute-start.6) | collective-permute-done | bytes 1048608 | tf_op jit(solution)/shard_map/ppermute | solution.py:421
  41.4 3.0 %shard_map.55 = bf16[1,2,512,512]{3,2,1,0:T(8,128)(2,1)} custom-call(s32[2,512,128]{2,1,0:T(8,128)S(1)} %get-tuple-element.32.starts_ref, bf16[512,1024]{1,0:T(8,128)(2,1)S(1)} %collective-permute-done.6.swapped_ref, bf16[512,1024]{1,0:T(8,128)(2,1)S(1)} %shard_map.52.far_ref.kept_ref, ...), custom_call_target="tpu_custom_call", output_to_operand_aliasing={{}: (7, {})} | custom-call | flops 100000000 | bytes 1000000 | tf_op jit(solution)/shard_map/pallas_call | solution.py:447
  (2 shorter events, 0.0 us)
Async XLA Ops:
  0.0 1.7 %copy-start = (bf16[512,1536]{1,0:T(8,128)(2,1)S(1)}, bf16[512,1536]{1,0:T(8,128)(2,1)}, u32[]{:S(2)}) copy-start(bf16[512,1536]{1,0:T(8,128)(2,1)} %w_ref.7) | copy-start | bytes 4718596
  0.0 1.7 %copy-start.2 = (s32[16]{0:T(128)S(1)}, s32[16]{0:T(128)}, u32[]{:S(2)}) copy-start(s32[16]{0:T(128)} %param.5) | copy-start | bytes 196
  3.8 3.0 %collective-permute-start.4 = (bf16[512,1024]{1,0:T(8,128)(2,1)S(1)}, bf16[512,1024]{1,0:T(8,128)(2,1)S(1)}, u32[]{:S(2)}, u32[]{:S(2)}) collective-permute-start(bf16[512,1024]{1,0:T(8,128)(2,1)S(1)} %get-tuple-element.34.give_ref), channel_id=1, source_target_pairs={{0,1},{1,0},{2,3},{3,2},{4,5},{5,4},{6,7},{7,6},{8,9},{9,8},{10,11... | collective-permute-start | bytes 3145736 | tf_op jit(solution)/shard_map/ppermute | solution.py:421
  4.5 13.4 %collective-permute-start.3 = (bf16[512,512]{1,0:T(8,128)(2,1)S(1)}, bf16[512,512]{1,0:T(8,128)(2,1)S(1)}, u32[]{:S(2)}, u32[]{:S(2)}) collective-permute-start(bf16[512,512]{1,0:T(8,128)(2,1)S(1)} %get-tuple-element.28.straight_ref), channel_id=1, source_target_pairs={{0,2},{1,3},{4,6},{5,7},{2,0},{3,1},{6,4},{7,5},{8,10},{9,11},{12,... | collective-permute-start | bytes 1572872 | tf_op jit(solution)/shard_map/ppermute | solution.py:421
  6.8 22.1 %copy-start.1 = (bf16[512,512]{1,0:T(8,128)(2,1)S(1)}, bf16[512,512]{1,0:T(8,128)(2,1)}, u32[]{:S(2)}) copy-start(bf16[512,512]{1,0:T(8,128)(2,1)} %w_out_ref.7) | copy-start | bytes 1572868
  17.9 14.3 %collective-permute-start.5 = (bf16[512,512]{1,0:T(8,128)(2,1)S(1)}, bf16[512,512]{1,0:T(8,128)(2,1)S(1)}, u32[]{:S(2)}, u32[]{:S(2)}) collective-permute-start(bf16[512,512]{1,0:T(8,128)(2,1)S(1)} %collective-permute-done.3.far_ref), channel_id=1, source_target_pairs={{0,1},{1,0},{2,3},{3,2},{4,5},{5,4},{6,7},{7,6},{8,9},{9,8},{10,11... | collective-permute-start | bytes 1572872 | tf_op jit(solution)/shard_map/ppermute | solution.py:421
  18.9 8.8 %collective-permute-start = (bf16[256,512]{1,0:T(8,128)(2,1)S(1)}, bf16[256,512]{1,0:T(8,128)(2,1)S(1)}, u32[]{:S(2)}, u32[]{:S(2)}) collective-permute-start(bf16[256,512]{1,0:T(8,128)(2,1)S(1)} %get-tuple-element.30.cross_a_ref), channel_id=1, source_target_pairs={{2,6},{3,7},{4,0},{5,1},{10,14},{11,15},{12,8},{13,9},{18,22},{19,... | collective-permute-start | bytes 786440 | tf_op jit(solution)/shard_map/ppermute | solution.py:421
  22.0 10.4 %collective-permute-start.2 = (bf16[256,512]{1,0:T(8,128)(2,1)S(1)}, bf16[256,512]{1,0:T(8,128)(2,1)S(1)}, u32[]{:S(2)}, u32[]{:S(2)}) collective-permute-start(bf16[256,512]{1,0:T(8,128)(2,1)S(1)} %get-tuple-element.31.cross_b_ref), channel_id=1, source_target_pairs={{2,4},{3,5},{4,2},{5,3},{10,12},{11,13},{12,10},{13,11},{18,20},{1... | collective-permute-start | bytes 786440 | tf_op jit(solution)/shard_map/ppermute | solution.py:421
  27.7 8.9 %collective-permute-start.1 = (bf16[256,512]{1,0:T(8,128)(2,1)S(1)}, bf16[256,512]{1,0:T(8,128)(2,1)S(1)}, u32[]{:S(2)}, u32[]{:S(2)}) collective-permute-start(bf16[256,512]{1,0:T(8,128)(2,1)S(1)} %collective-permute-done), channel_id=1, source_target_pairs={{6,4},{7,5},{0,2},{1,3},{14,12},{15,13},{8,10},{9,11},{22,20},{23,... | collective-permute-start | bytes 786440 | tf_op jit(solution)/shard_map/ppermute | solution.py:421
  37.3 4.1 %collective-permute-start.6 = (bf16[512,1024]{1,0:T(8,128)(2,1)S(1)}, bf16[512,1024]{1,0:T(8,128)(2,1)S(1)}, u32[]{:S(2)}, u32[]{:S(2)}) collective-permute-start(bf16[512,1024]{1,0:T(8,128)(2,1)S(1)} %shard_map.52.far_ref.kept_ref), channel_id=1, source_target_pairs={{0,1},{1,0},{2,3},{3,2},{4,5},{5,4},{6,7},{7,6},{8,9},{9,8},{10,11... | collective-permute-start | bytes 3145736 | tf_op jit(solution)/shard_map/ppermute | solution.py:421
